TPU v7x, 32 devices: a whole 2x2x4 slice. The times are simulated.
32 devices in a mesh: dp: 8 (over y, x, core), shard: 4 (over z).
Axes of the slice: x: 2, y: 2, z: 4, core: 2. Of those that a mesh axis runs over, the one named last changes fastest.
Arguments:
- tokens: bfloat16 [8192, 2048], P(('dp', 'shard')), may hold values from -6 to 6
- doc_lengths: int32 [32, 4], P(('dp', 'shard')), may hold values from 1 to 128, 256 in all within a row
- weights: float32 [2048, 192, 128], P(('dp', 'shard')), may hold values from -2 to 2
- momentum: float32 [2048, 192, 128], P(('dp', 'shard')), may hold values from -8192 to 8192
- vectors: float32 [2048, 12], P(('dp', 'shard')), may hold values from -2 to 2
- vector_moment: float32 [2048, 12], P(('dp', 'shard')), may hold values from -8192 to 8192
- vector_second: float32 [2048, 12], P(('dp', 'shard')), may hold values from 0 to 8192, as said below
- cotangent: bfloat16 [8192, 2048], P(('dp', 'shard')), may hold values from -6 to 6
Outputs:
- layer_output: bfloat16 [8192, 2048], P(('dp', 'shard'))
- input_gradient: float32 [8192, 2048], P(('dp', 'shard'))
- weight_gradient: float32 [2048, 192, 128], P(('dp', 'shard'))
- new_weights: float32 [2048, 192, 128], P(('dp', 'shard'))
- new_momentum: float32 [2048, 192, 128], P(('dp', 'shard'))
- next_moment: float32 [2048, 12], P(('dp', 'shard'))
- next_second: float32 [2048, 12], P(('dp', 'shard'))
- next_vectors: float32 [2048, 12], P(('dp', 'shard'))
Inputs may be any that keep to these rules, and one draw needn't show every extreme that they name: `doc_lengths`: in each row the first 3 entries are sequence lengths and the last is the padding at the row's end; a row sums to 256 and its largest entry is exactly 128. `vector_second`: positive.
All inputs are finite; a program needn't handle non-finite values.
Results may differ from a plain program's by a relative error of at most 0.019.
Values may be sent and summed in bfloat16 or wider, within the bound.
A program may use at most 832 MiB of HBM per device.

v0:
```python
from functools import partial
import math

import jax
import jax.numpy as jnp
from jax import lax
from jax.sharding import PartitionSpec as P

D = 2048
HEADS = 16
HEAD = 128
FF = 8192
NS_ITERS = 5
STEP = 10


HIGHEST = lax.Precision.HIGHEST
COEF_A = 3.4445
COEF_B = -4.775
COEF_C = 2.0315


def for_sending(array):
    return jax.tree.map(lambda a: a.astype(jnp.bfloat16) if a.dtype == jnp.float32 else a, array)


def layer_norm(values, gain_row, shift_row):
    average = jnp.mean(values, axis=-1, keepdims=True)
    centered = values - average
    variance = jnp.mean(centered * centered, axis=-1, keepdims=True)
    return centered * lax.rsqrt(variance + 1e-05) * gain_row + shift_row


def allowed_mask(length_rows, row_length):
    boundary = jnp.cumsum(length_rows, axis=-1)
    places = jnp.arange(row_length, dtype=jnp.int32)
    segment = jnp.sum((places[None, :, None] >= boundary[:, None, :]).astype(jnp.int32), axis=-1)
    same_span = segment[:, :, None] == segment[:, None, :]
    causal = places[:, None] >= places[None, :]
    padded = segment[:, :, None] == length_rows.shape[-1] - 1
    diagonal = places[:, None] == places[None, :]
    return same_span & causal[None] & (jnp.logical_not(padded) | diagonal[None])


def forward_pass(blocks, vector_full, token_values, allowed):
    inner_count = FF // HEAD
    vector_values = vector_full.astype(jnp.float32)
    bias_query = vector_values[:, 4].reshape(HEADS, HEAD)
    bias_value = vector_values[:, 5].reshape(HEADS, HEAD)
    bias_up = vector_values[:, 8:].T.reshape(inner_count, HEAD)
    normed_one = layer_norm(token_values, vector_values[:, 0], vector_values[:, 1]).astype(
        jnp.bfloat16
    )
    joined = jnp.einsum(
        "td,dhc->thc", normed_one, blocks[:, : 3 * HEADS], preferred_element_type=jnp.float32
    )
    queries = (joined[:, :HEADS] + bias_query).astype(jnp.bfloat16)
    key_rows = joined[:, HEADS : 2 * HEADS].astype(jnp.bfloat16)
    value_rows = (joined[:, 2 * HEADS :] + bias_value).astype(jnp.bfloat16)
    scores = jnp.einsum(
        "qhc,khc->hqk", queries, key_rows, preferred_element_type=jnp.float32
    ) * HEAD ** (-0.5)
    scores = jnp.where(allowed[None], scores, -1e30)
    row_peak = jnp.max(scores, axis=-1, keepdims=True)
    exponent = jnp.exp(scores - row_peak)
    probability = exponent / jnp.sum(exponent, axis=-1, keepdims=True)
    probability_low = probability.astype(jnp.bfloat16)
    attended = jnp.einsum(
        "hqk,khc->qhc", probability_low, value_rows, preferred_element_type=jnp.float32
    ).astype(jnp.bfloat16)
    branch = (
        jnp.einsum(
            "thc,dhc->td",
            attended,
            blocks[:, 3 * HEADS : 4 * HEADS],
            preferred_element_type=jnp.float32,
        )
        + vector_values[:, 6]
    )
    middle = token_values + branch
    normed_two = layer_norm(middle, vector_values[:, 2], vector_values[:, 3]).astype(jnp.bfloat16)
    before = (
        jnp.einsum(
            "td,djc->tjc",
            normed_two,
            blocks[:, 4 * HEADS : 4 * HEADS + inner_count],
            preferred_element_type=jnp.float32,
        )
        + bias_up
    )
    activated = jax.nn.gelu(before, approximate=True).astype(jnp.bfloat16)
    branch_two = (
        jnp.einsum(
            "tjc,djc->td",
            activated,
            blocks[:, 4 * HEADS + inner_count :],
            preferred_element_type=jnp.float32,
        )
        + vector_values[:, 7]
    )
    output = middle + branch_two
    return (
        vector_values,
        normed_one,
        queries,
        key_rows,
        value_rows,
        probability,
        probability_low,
        attended,
        middle,
        normed_two,
        before,
        activated,
        output,
    )


def local(tokens, doc_lengths, weights, momentum, vectors, vector_moment, vector_second, cotangent):
    token_count = tokens.shape[0]
    inner_count = FF // HEAD
    allowed = allowed_mask(doc_lengths, token_count)[0]
    token_values = tokens.astype(jnp.float32)
    weight_low = weights.astype(jnp.bfloat16)
    vector_low = vectors.astype(jnp.bfloat16)
    blocks, vector_full = (
        lax.all_gather(weight_low, ("dp", "shard"), axis=0, tiled=True),
        lax.all_gather(vector_low, ("dp", "shard"), axis=0, tiled=True),
    )
    output = forward_pass(blocks, vector_full, token_values, allowed)[-1]
    blocks, vector_full = (
        lax.all_gather(weight_low, ("dp", "shard"), axis=0, tiled=True),
        lax.all_gather(vector_low, ("dp", "shard"), axis=0, tiled=True),
    )
    (
        vector_values,
        normed_one,
        queries,
        key_rows,
        value_rows,
        probability,
        probability_low,
        attended,
        middle,
        normed_two,
        before,
        activated,
        repeated,
    ) = forward_pass(blocks, vector_full, token_values, allowed)
    query_blocks = blocks[:, : 3 * HEADS]
    mixing_blocks = blocks[:, 3 * HEADS : 4 * HEADS]
    upper_blocks = blocks[:, 4 * HEADS : 4 * HEADS + inner_count]
    lower_blocks = blocks[:, 4 * HEADS + inner_count :]
    back_full = cotangent.astype(jnp.float32)
    grad_activated = jnp.einsum(
        "td,djc->tjc", cotangent, lower_blocks, preferred_element_type=jnp.float32
    )
    gelu_value, gelu_back = jax.vjp(partial(jax.nn.gelu, approximate=True), before)
    grad_before = gelu_back(grad_activated)[0].astype(jnp.bfloat16)
    grad_normed_two = jnp.einsum(
        "tjc,djc->td", grad_before, upper_blocks, preferred_element_type=jnp.float32
    )
    two_value, norm_back_two = jax.vjp(layer_norm, middle, vector_values[:, 2], vector_values[:, 3])
    grad_middle_part, grad_gain_two, grad_shift_two = norm_back_two(grad_normed_two)
    grad_middle = back_full + grad_middle_part
    grad_branch = grad_middle.astype(jnp.bfloat16)
    grad_attended = jnp.einsum(
        "td,dhc->thc", grad_branch, mixing_blocks, preferred_element_type=jnp.float32
    ).astype(jnp.bfloat16)
    grad_prob = jnp.einsum(
        "qhc,khc->hqk", grad_attended, value_rows, preferred_element_type=jnp.float32
    )
    row_total = jnp.sum(probability * grad_prob, axis=-1, keepdims=True)
    grad_scores = (probability * (grad_prob - row_total)).astype(jnp.bfloat16)
    score_scale = HEAD ** (-0.5)
    grad_queries = (
        jnp.einsum("hqk,khc->qhc", grad_scores, key_rows, preferred_element_type=jnp.float32)
        * score_scale
    ).astype(jnp.bfloat16)
    grad_keys = (
        jnp.einsum("hqk,qhc->khc", grad_scores, queries, preferred_element_type=jnp.float32)
        * score_scale
    ).astype(jnp.bfloat16)
    grad_values = jnp.einsum(
        "hqk,qhc->khc", probability_low, grad_attended, preferred_element_type=jnp.float32
    ).astype(jnp.bfloat16)
    grad_joined = jnp.concatenate([grad_queries, grad_keys, grad_values], axis=1)
    grad_normed_one = jnp.einsum(
        "thc,dhc->td", grad_joined, query_blocks, preferred_element_type=jnp.float32
    )
    one_value, norm_back_one = jax.vjp(
        layer_norm, token_values, vector_values[:, 0], vector_values[:, 1]
    )
    grad_tokens_part, grad_gain_one, grad_shift_one = norm_back_one(grad_normed_one)
    grad_tokens = grad_middle + grad_tokens_part
    plain_columns = jnp.stack(
        [
            grad_gain_one,
            grad_shift_one,
            grad_gain_two,
            grad_shift_two,
            jnp.sum(grad_queries, axis=0, dtype=jnp.float32).reshape(D),
            jnp.sum(grad_values, axis=0, dtype=jnp.float32).reshape(D),
            jnp.sum(grad_branch, axis=0, dtype=jnp.float32),
            jnp.sum(cotangent, axis=0, dtype=jnp.float32),
        ],
        axis=1,
    )
    hidden_columns = jnp.sum(grad_before, axis=0, dtype=jnp.float32).reshape(FF // D, D).T
    vector_terms = jnp.concatenate([plain_columns, hidden_columns], axis=1)
    query_part = jnp.einsum(
        "td,thc->dhc", normed_one, grad_joined, preferred_element_type=jnp.float32
    )
    mixing_part = jnp.einsum(
        "td,thc->dhc", grad_branch, attended, preferred_element_type=jnp.float32
    )
    upper_part = jnp.einsum(
        "td,tjc->djc", normed_two, grad_before, preferred_element_type=jnp.float32
    )
    lower_part = jnp.einsum("td,tjc->djc", cotangent, activated, preferred_element_type=jnp.float32)
    weight_grad = lax.psum_scatter(
        jnp.concatenate([query_part, mixing_part, upper_part, lower_part], axis=1),
        ("dp", "shard"),
        scatter_dimension=0,
        tiled=True,
    )
    vector_grad = lax.psum_scatter(vector_terms, ("dp", "shard"), scatter_dimension=0, tiled=True)
    moment_new = 0.95 * momentum + weight_grad
    groups = lax.axis_size("dp")
    per_group = moment_new.shape[1] // groups
    grouped = moment_new.reshape(moment_new.shape[0], groups, per_group, moment_new.shape[2])

    def gram_total(values):
        return lax.psum(
            jnp.einsum("rkc,rke->kce", values, values, precision=HIGHEST).astype(jnp.bfloat16),
            "shard",
        ).astype(jnp.float32)

    current = lax.all_to_all(
        grouped.astype(jnp.bfloat16), "dp", split_axis=1, concat_axis=0, tiled=True
    ).astype(grouped.dtype)[:, 0]
    gram_matrix = gram_total(current)
    scaling = 1.0 / (jnp.sqrt(jnp.trace(gram_matrix, axis1=1, axis2=2)) + 1e-07)
    current = current * scaling[None, :, None]
    gram_matrix = gram_matrix * (scaling * scaling)[:, None, None]
    for number in range(NS_ITERS):
        if number > 0:
            gram_matrix = gram_total(current)
        square = jnp.einsum("kce,kef->kcf", gram_matrix, gram_matrix, precision=HIGHEST)
        polynomial = COEF_B * gram_matrix + COEF_C * square
        current = COEF_A * current + jnp.einsum(
            "rkc,kce->rke", current, polynomial, precision=HIGHEST
        )
    orthogonal_rows = lax.all_to_all(
        for_sending(current[:, None]), "dp", split_axis=0, concat_axis=1, tiled=True
    )
    orthogonal_rows = orthogonal_rows.reshape(moment_new.shape)
    new_weights = weights * (1.0 - 0.15 * 0.1) - 0.15 * 0.2 * math.sqrt(D) * orthogonal_rows
    first_moment = 0.9 * vector_moment + 0.1 * vector_grad
    second = 0.95 * vector_second + 0.05 * vector_grad * vector_grad
    corrected = first_moment / (1.0 - 0.9**STEP)
    normal_second = second / (1.0 - 0.95**STEP)
    next_vectors = vectors - 0.5 * corrected / (jnp.sqrt(normal_second) + 1e-08)
    return (
        output.astype(jnp.bfloat16),
        grad_tokens,
        weight_grad,
        new_weights,
        moment_new,
        first_moment,
        second,
        next_vectors,
    )


def solution(mesh):
    return jax.shard_map(
        local,
        mesh=mesh,
        in_specs=(
            P(("dp", "shard"), None),
            P(("dp", "shard"), None),
            P(("dp", "shard"), None, None),
            P(("dp", "shard"), None, None),
            P(("dp", "shard"), None),
            P(("dp", "shard"), None),
            P(("dp", "shard"), None),
            P(("dp", "shard"), None),
        ),
        out_specs=(
            P(("dp", "shard"), None),
            P(("dp", "shard"), None),
            P(("dp", "shard"), None, None),
            P(("dp", "shard"), None, None),
            P(("dp", "shard"), None, None),
            P(("dp", "shard"), None),
            P(("dp", "shard"), None),
            P(("dp", "shard"), None),
        ),
        check_vma=False,
    )
```

profile of v0, /device:TPU:27, one launch (start us, length us, event | category | flops | bytes accessed | tf_op | source)
XLA Modules:
  0.0 3006.4 jit_solution(13417627830127713646)
XLA Ops:
  7.2 8.1 copy.255
  16.0 67.3 %all-gather = bf16[32,64,12]{1,2,0:T(8,128)(2,1)S(1)} all-gather(bf16[1,64,12]{1,2,0:T(8,128)(2,1)S(1)} %convert_bitcast_fusion.1), channel_id=1, replica_groups=mesh['dp'=8,'shard'=4] {'dp','shard'}, dimensions={0}, use_global_device_ids=true | all-gather | bytes 50688 | tf_op jit(solution)/shard_map/all_gather | solution.py:128
  85.8 465.1 %all-gather.3.cloned.1.call-done = bf16[2048,192,128]{2,0,1:T(8,128)(2,1)} async-done(((bf16[64,192,128]{2,0,1:T(8,128)(2,1)}), bf16[2048,192,128]{2,0,1:T(8,128)(2,1)}) %all-gather.3.cloned.1.call-update) | async-done | bytes 100663312 | tf_op jit(solution)/shard_map/all_gather | solution.py:127
  550.9 13.4 fusion.167
  564.3 3.4 fusion.107
  569.0 3.7 fusion.99
  572.8 6.3 fusion.169
  579.4 17.6 fusion.7
  597.0 19.8 convert_reduce_fusion
  616.8 16.6 multiply_reduce_fusion.1
  636.4 6.1 fusion.96
  651.0 7.1 fusion.109
  658.1 27.6 convolution_bitcast_fusion
  685.8 25.8 fusion.155
  711.6 19.6 fusion.104
  731.2 132.5 %pad_maximum_fusion = f32[2048,192,128]{2,0,1:T(8,128)} fusion(f32[2048,64,128]{2,0,1:T(8,128)} %convolution_bitcast_fusion, f32[2048,64,128]{2,0,1:T(8,128)} %fusion.155, f32[2048,16,128]{2,0,1:T(8,128)} %fusion.109, f32[2048,48,128]{2,0,1:T(8,128)} %fusion.104), kind=kLoop, calls=%fused_computation.1 | loop fusion | flops 150994944 | bytes 402653184 | tf_op jit(solution)/shard_map/concatenate | solution.py:222
  863.8 1596.4 %reduce-scatter.5.cloned.1.call-done = f32[64,192,128]{2,0,1:T(8,128)} async-done(((f32[2048,192,128]{2,0,1:T(8,128)}), f32[64,192,128]{2,0,1:T(8,128)}) %reduce-scatter.5.cloned.1.call-update) | async-done | bytes 6291472 | tf_op jit(solution)/shard_map/reduce_scatter | solution.py:221
  2460.2 11.4 fusion.163
  2471.6 40.2 %all_to_all.27 = bf16[64,8,24,128]{3,0,2,1:T(8,128)(2,1)S(1)} all-to-all(bf16[64,8,24,128]{3,0,2,1:T(8,128)(2,1)S(1)} %bitcast.142), channel_id=1, replica_groups=mesh['dp'=8,'shard'=4] {'dp'}, dimensions={1} | all-to-all | bytes 6291456 | tf_op jit(solution)/shard_map/all_to_all | solution.py:239
  2515.0 41.5 %all-reduce.6.cloned.1.call-done = bf16[24,128,128]{2,1,0:T(8,128)(2,1)} async-done(((bf16[24,128,128]{2,1,0:T(8,128)(2,1)}), bf16[24,128,128]{2,1,0:T(8,128)(2,1)}) %all-reduce.6.cloned.1.call-update) | async-done | bytes 786448 | tf_op jit(solution)/shard_map/psum | solution.py:234
  2558.0 3.5 fusion.74
  2561.5 7.5 bitcast_add_fusion.4
  2569.1 2.7 copy-done.2
  2571.8 11.6 convolution_convert_fusion.5
  2583.5 43.1 %all-reduce.8.cloned.1.call-done = bf16[24,128,128]{2,1,0:T(8,128)(2,1)} async-done(((bf16[24,128,128]{2,1,0:T(8,128)(2,1)}), bf16[24,128,128]{2,1,0:T(8,128)(2,1)}) %all-reduce.8.cloned.1.call-update) | async-done | bytes 786448 | tf_op jit(solution)/shard_map/psum | solution.py:234
  2628.6 9.6 bitcast_add_fusion.3
  2638.2 2.7 copy-done.3
  2640.9 11.2 convolution_convert_fusion.4
  2652.2 43.1 %all-reduce.10.cloned.1.call-done = bf16[24,128,128]{2,1,0:T(8,128)(2,1)} async-done(((bf16[24,128,128]{2,1,0:T(8,128)(2,1)}), bf16[24,128,128]{2,1,0:T(8,128)(2,1)}) %all-reduce.10.cloned.1.call-update) | async-done | bytes 786448 | tf_op jit(solution)/shard_map/psum | solution.py:234
  2697.3 9.8 bitcast_add_fusion.2
  2707.1 2.7 copy-done.1
  2709.8 11.2 convolution_convert_fusion.3
  2721.2 13.3 fusion.159
  2734.5 29.7 all-reduce.12.cloned.1.call-done
  2766.2 9.4 bitcast_add_fusion.1
  2775.7 2.7 copy-done
  2778.4 11.2 convolution_convert_fusion.2
  2790.1 2.7 fusion.66
  2792.9 4.3 convert_reduce_fusion.2
  2798.7 34.0 %all-reduce.14.cloned.1.call-done = bf16[24,128,128]{2,1,0:T(8,128)(2,1)} async-done(((bf16[24,128,128]{2,1,0:T(8,128)(2,1)}), bf16[24,128,128]{2,1,0:T(8,128)(2,1)}) %all-reduce.14.cloned.1.call-update) | async-done | bytes 786448 | tf_op jit(solution)/shard_map/psum | solution.py:234
  2834.8 10.5 fusion.28
  2845.3 3.7 copy.209
  2849.0 5.7 all-to-all-start.1
  2854.8 18.3 fusion.57
  2873.1 97.5 %reduce-scatter.7.cloned.1.call-done = f32[64,12]{1,0:T(8,128)} async-done(((f32[2048,12]{1,0:T(8,128)}), f32[64,12]{1,0:T(8,128)}) %reduce-scatter.7.cloned.1.call-update) | async-done | bytes 3088
  2972.0 9.1 copy.212
  2981.2 9.1 copy.211
  2995.4 4.0 multiply_subtract_fusion
  (179 shorter events, 37.7 us)
Async XLA Ops:
  7.2 543.7 %all-gather.3.cloned.1.call-start = ((), (), s32[]{:S(2)}) async-start(), calls=%async_computation.4 | async-start | bytes 103809024 | tf_op jit(solution)/shard_map/all_gather | solution.py:127
  15.3 68.2 %copy-start.54 = (s32[1,4]{1,0:T(1,128)S(1)}, s32[1,4]{1,0:T(1,128)}, u32[]{:S(2)}) copy-start(s32[1,4]{1,0:T(1,128)} %param.9) | copy-start | bytes 52
  15.3 68.5 %copy-start.4 = (bf16[256,2048]{1,0:T(8,128)(2,1)S(1)}, bf16[256,2048]{1,0:T(8,128)(2,1)}, u32[]{:S(2)}) copy-start(bf16[256,2048]{1,0:T(8,128)(2,1)} %param.8) | copy-start | bytes 3145732
  15.3 2444.8 %reduce-scatter.5.cloned.1.call-start = ((), (), s32[]{:S(2)}) async-start(), calls=%async_computation.5 | async-start | bytes 207618048 | tf_op jit(solution)/shard_map/reduce_scatter | solution.py:221
  83.5 574.6 %copy-start.26 = (f32[64,128]{1,0:T(8,128)}, f32[64,128]{1,0:T(8,128)S(1)}, u32[]{:S(2)}) copy-start(f32[64,128]{1,0:T(8,128)S(1)} %add.230) | copy-start | bytes 98308
  84.0 480.2 %copy-start.37 = (f32[256]{0:T(256)}, f32[256]{0:T(256)S(1)}, u32[]{:S(2)}) copy-start(f32[256]{0:T(256)S(1)} %broadcast_multiply_fusion.2) | copy-start | bytes 3076
  85.1 479.2 %copy-start.40 = (f32[256]{0:T(256)}, f32[256]{0:T(256)S(1)}, u32[]{:S(2)}) copy-start(f32[256]{0:T(256)S(1)} %fusion.139) | copy-start | bytes 3076
  85.8 478.5 %copy-start.28 = (f32[2048,1]{0,1:T(1,128)}, f32[2048,1]{0,1:T(1,128)S(1)}, u32[]{:S(2)}) copy-start(f32[2048,1]{0,1:T(1,128)S(1)} %get-tuple-element.75) | copy-start | bytes 24580
  85.8 478.5 %copy-start.32 = (f32[2048,1]{0,1:T(1,128)}, f32[2048,1]{0,1:T(1,128)S(1)}, u32[]{:S(2)}) copy-start(f32[2048,1]{0,1:T(1,128)S(1)} %get-tuple-element.74) | copy-start | bytes 24580
  569.0 3.7 copy-start.19
  572.8 6.3 copy-start.21
  579.0 106.7 %copy-start.7 = (f32[256,2048]{1,0:T(8,128)}, f32[256,2048]{1,0:T(8,128)S(1)}, u32[]{:S(2)}) copy-start(f32[256,2048]{1,0:T(8,128)S(1)} %get-tuple-element.81) | copy-start | bytes 6291460
  579.4 17.6 copy-start.11
  616.8 16.6 copy-start.17
  635.4 9.6 slice-start.2
  636.4 6.1 copy-start.20
  636.4 8.6 slice-start.3
  685.8 25.8 copy-start.5
  685.8 25.8 copy-start.29
  685.8 25.8 copy-start.33
  685.8 25.8 copy-start.38
  685.8 25.8 copy-start.41
  863.7 1692.8 %all-reduce.6.cloned.1.call-start = ((), (), s32[]{:S(2)}) async-start(), calls=%async_computation.6 | async-start | bytes 1572864 | tf_op jit(solution)/shard_map/psum | solution.py:234
  2514.7 111.8 %all-reduce.8.cloned.1.call-start = ((), (), s32[]{:S(2)}) async-start(), calls=%async_computation.7 | async-start | bytes 1572864 | tf_op jit(solution)/shard_map/psum | solution.py:234
  2556.5 5.0 copy-start.16
  2583.4 111.9 %all-reduce.10.cloned.1.call-start = ((), (), s32[]{:S(2)}) async-start(), calls=%async_computation.8 | async-start | bytes 1572864 | tf_op jit(solution)/shard_map/psum | solution.py:234
  2652.1 112.1 %all-reduce.12.cloned.1.call-start = ((), (), s32[]{:S(2)}) async-start(), calls=%async_computation.9 | async-start | bytes 1572864 | tf_op jit(solution)/shard_map/psum | solution.py:234
  2709.8 11.3 copy-start.6
  2709.8 11.3 copy-start.18
  2709.8 11.4 copy-start.23
  2709.8 11.4 copy-start.30
  2709.8 11.4 copy-start.39
  2721.1 13.4 copy-start.46
  2721.1 111.7 %all-reduce.14.cloned.1.call-start = ((), (), s32[]{:S(2)}) async-start(), calls=%async_computation.10 | async-start | bytes 1572864 | tf_op jit(solution)/shard_map/psum | solution.py:234
  2778.4 11.7 copy-start.42
  2789.6 180.9 %reduce-scatter.7.cloned.1.call-start = ((), (), s32[]{:S(2)}) async-start(), calls=%async_computation.11 | async-start | bytes 1081344
  2792.8 4.4 copy-start.31
  2792.8 4.4 copy-start.50
  2792.8 4.4 copy-start.51
  2792.9 4.4 copy-start.52
  2792.9 4.4 copy-start.53
  2849.0 5.7 copy-start.8
  2849.0 5.7 copy-start.27
  2849.0 5.7 copy-start.49
  2849.0 141.3 %all-to-all-start.1 = ((bf16[512,1,24,128]{3,2,1,0:T(8,128)(2,1)}), bf16[512,1,24,128]{3,2,1,0:T(8,128)(2,1)}, u32[]{:S(2)}, u32[]{:S(2)}) async-start(bf16[512,1,24,128]{3,2,1,0:T(8,128)(2,1)} %copy.209), calls=%async_computation.2 | async-start | bytes 6291456 | tf_op jit(solution)/shard_map/all_to_all | solution.py:254
  2854.7 116.7 %copy-start.35 = (f32[64,12]{0,1:T(8,128)S(1)}, f32[64,12]{0,1:T(8,128)}, u32[]{:S(2)}) copy-start(f32[64,12]{0,1:T(8,128)} %param.12) | copy-start | bytes 9220
  2854.7 116.7 %copy-start.47 = (f32[64,12]{0,1:T(8,128)S(1)}, f32[64,12]{0,1:T(8,128)}, u32[]{:S(2)}) copy-start(f32[64,12]{0,1:T(8,128)} %param.14) | copy-start | bytes 9220
  2854.8 116.6 %copy-start.48 = (f32[64,12]{0,1:T(8,128)S(1)}, f32[64,12]{0,1:T(8,128)}, u32[]{:S(2)}) copy-start(f32[64,12]{0,1:T(8,128)} %param.13) | copy-start | bytes 9220
  (20 other events, 45.7 us)
Sparse Core Ops, SparseCore 0:
  15.5 535.3 all-gather.2
  863.9 1596.2 reduce-scatter.4
  2514.9 41.6 all-reduce.5
  2583.5 42.9 all-reduce.7
  2652.2 42.9 all-reduce.9
  2721.2 42.9 all-reduce.11
  2789.7 42.9 all-reduce.13
  2835.6 134.9 reduce-scatter.6
where the time goes:
time: 3020 us; the launch traced here: 3010 us
  waiting for transfers between devices  2350 us (78%)
  matrix products  311 us (10%)
  other arithmetic  165 us (5%)
  blocking collectives  108 us (4%)
  local copies, waits for them, and re-layouts  50.4 us (2%)
    reduce_scatter x1, waiting for transfers between devices, local(): lax.psum_scatter(jnp.concatenate([query_part, mixing_part, upper_part, lo...  1600 us
    all_gather x1, waiting for transfers between devices, local(): lax.all_gather(weight_low, ('dp', 'shard'), axis=0, tiled=True)  465 us
    psum x5, waiting for transfers between devices, gram_total(): lax.psum(jnp.einsum('rkc,rke->kce', values, values, precision=HIGHEST).as...  191 us
    concatenate x1, other arithmetic, local(): jnp.concatenate([query_part, mixing_part, upper_part, lower_part], axis=1)  133 us
    unnamed x9, waiting for transfers between devices  97.6 us
    all_gather x1, blocking collectives, local(): lax.all_gather(vector_low, ('dp', 'shard'), axis=0, tiled=True)  67.3 us
  transfers between devices with their start and end apart: 9, of which 8 were waited for; matrix products, arithmetic and copies ran while one was open for 3% of the time, Pallas kernels for 0%

commit v1 on v0

v1 whole, which is shorter than its diff:
```python
from functools import partial
import math

import jax
import jax.numpy as jnp
from jax import lax
from jax.sharding import Mesh, PartitionSpec as P

HEADS = 16
HEAD = 128
NS_ITERS = 5
STEP = 10

COEF_A = 3.4445
COEF_B = -4.775
COEF_C = 2.0315
BF = jnp.bfloat16
F32 = jnp.float32
ALL = ("hi", "tp", "shard")
FS = ("hi", "shard")


def dot(spec, a, b, **kw):
    return jnp.einsum(spec, a, b, preferred_element_type=F32, **kw)


def layer_norm(values, gain_row, shift_row):
    average = jnp.mean(values, axis=-1, keepdims=True)
    centered = values - average
    variance = jnp.mean(centered * centered, axis=-1, keepdims=True)
    return centered * lax.rsqrt(variance + 1e-05) * gain_row + shift_row


def allowed_mask(length_rows, row_length):
    ends = [length_rows[:, 0]]
    for span in range(1, length_rows.shape[-1]):
        ends.append(ends[-1] + length_rows[:, span])
    boundary = jnp.stack(ends, axis=-1)
    places = jnp.arange(row_length, dtype=jnp.int32)
    segment = jnp.sum((places[None, :, None] >= boundary[:, None, :]).astype(jnp.int32), axis=-1)
    same_span = segment[:, :, None] == segment[:, None, :]
    causal = places[:, None] >= places[None, :]
    padded = segment[:, :, None] == length_rows.shape[-1] - 1
    diagonal = places[:, None] == places[None, :]
    return same_span & causal[None] & (jnp.logical_not(padded) | diagonal[None])


def newton_schulz(current):
    def ein(spec, a, b):
        return jnp.einsum(spec, a, b, precision=lax.Precision.HIGH, preferred_element_type=F32)
    total = jnp.sum(current * current, axis=(0, 2))
    current = current * (1.0 / (jnp.sqrt(total) + 1e-07))[None, :, None]
    for number in range(NS_ITERS):
        gram = ein("rkc,rke->kce", current, current)
        square = ein("kce,kef->kcf", gram, gram)
        polynomial = COEF_B * gram + COEF_C * square
        current = COEF_A * current + ein("rkc,kce->rke", current, polynomial)
    return current


def local(tokens, doc_lengths, weights, momentum, vectors, vector_moment, vector_second, cotangent):
    hi, tp, sh = (lax.axis_size(a) for a in ALL)
    groups, world = hi * sh, hi * tp * sh
    rows, blocks, head = weights.shape
    row_tokens, d = tokens.shape
    heads = HEADS // tp
    inner_all = (blocks - 4 * HEADS) // 2
    inner = inner_all // tp
    attn_blocks = 4 * heads
    me = lax.axis_index("tp")
    t_all = tp * row_tokens

    low = weights.astype(BF)
    attn_send = low[:, : 4 * HEADS].reshape(rows, 4, tp, heads, head).transpose(2, 0, 1, 3, 4).reshape(tp, rows, attn_blocks * head)
    mlp_send = low[:, 4 * HEADS :].reshape(rows, 2, tp, inner, head).transpose(2, 0, 1, 3, 4).reshape(tp, rows, 2 * inner * head)

    def rows_in_order(gathered):
        n = gathered.shape[-1]
        return gathered.reshape(hi, sh, tp, rows, n).transpose(0, 2, 1, 3, 4).reshape(d, n)

    def spread(array):
        swapped = lax.all_to_all(array, "tp", split_axis=0, concat_axis=0, tiled=True)
        return rows_in_order(lax.all_gather(swapped, FS, axis=0, tiled=False))

    w_attn = spread(attn_send)
    w_mlp = spread(mlp_send)
    vec = lax.all_gather(vectors.astype(BF), "tp", axis=0, tiled=False)
    vec = lax.all_gather(vec, FS, axis=0, tiled=False)
    vec = vec.reshape(hi, sh, tp, rows, -1).transpose(0, 2, 1, 3, 4).reshape(d, -1).astype(F32)

    tok_all = lax.all_gather(tokens, "tp", axis=0, tiled=True)
    cot_all = lax.all_gather(cotangent, "tp", axis=0, tiled=True)
    lengths = lax.all_gather(doc_lengths, "tp", axis=0, tiled=True)
    allowed = allowed_mask(lengths, row_tokens)

    def per_of(count):
        return -(-count // groups)

    def to_owners(part, count):
        per = per_of(count)
        part = jnp.pad(part, ((0, 0), (0, 0), (0, per * groups - count), (0, 0)))
        part = part.reshape(rows, tp, hi, sh, per * head)
        return part.transpose(2, 1, 3, 0, 4)

    def split(array):
        attn = array[:, : 4 * HEADS].reshape(rows, 4, tp, heads, head).transpose(0, 2, 1, 3, 4).reshape(rows, tp, attn_blocks, head)
        mlp = array[:, 4 * HEADS :].reshape(rows, 2, tp, inner, head)
        return ((attn, attn_blocks), (mlp[:, 0], inner), (mlp[:, 1], inner))

    mom_send = jnp.concatenate([to_owners(p, c) for p, c in split(momentum.astype(BF))], axis=-1)
    width = mom_send.shape[-1]
    mom_mine = lax.all_to_all(mom_send.reshape(world, rows, width), ALL, split_axis=0, concat_axis=0, tiled=True)
    mom_mine = mom_mine.reshape(d, width)

    bias_q = lax.dynamic_slice(vec[:, 4], (me * heads * head,), (heads * head,))
    bias_v = lax.dynamic_slice(vec[:, 5], (me * heads * head,), (heads * head,))
    bias_up = lax.dynamic_slice(vec[:, 8:].T.reshape(-1), (me * inner * head,), (inner * head,))
    hc = heads * head
    w_qkv, w_out = w_attn[:, : 3 * hc], w_attn[:, 3 * hc :]
    w_up, w_down = w_mlp[:, : inner * head], w_mlp[:, inner * head :]

    normed_one = layer_norm(tok_all.astype(F32), vec[:, 0], vec[:, 1]).astype(BF)
    joined = dot("td,dn->tn", normed_one, w_qkv)

    def per_head(values):
        return values.reshape(tp, row_tokens, heads, head)

    queries = per_head((joined[:, :hc] + bias_q).astype(BF))
    key_rows = per_head(joined[:, hc : 2 * hc].astype(BF))
    value_rows = per_head((joined[:, 2 * hc :] + bias_v).astype(BF))
    scores = dot("rqhc,rkhc->rhqk", queries, key_rows) * head ** (-0.5)
    scores = jnp.where(allowed[:, None], scores, -1e30)
    row_peak = jnp.max(scores, axis=-1, keepdims=True)
    exponent = jnp.exp(scores - row_peak)
    probability = exponent / jnp.sum(exponent, axis=-1, keepdims=True)
    probability_low = probability.astype(BF)
    attended = dot("rhqk,rkhc->rqhc", probability_low, value_rows).astype(BF).reshape(t_all, hc)

    def own_sum(partial_rows):
        return lax.psum_scatter(partial_rows.astype(BF), "tp", scatter_dimension=0, tiled=True).astype(F32)

    branch = own_sum(dot("tc,dc->td", attended, w_out)) + vec[:, 6]
    token_values = tokens.astype(F32)
    middle = token_values + branch
    normed_two_own = layer_norm(middle, vec[:, 2], vec[:, 3]).astype(BF)
    normed_two = lax.all_gather(normed_two_own, "tp", axis=0, tiled=True)
    before = dot("td,dn->tn", normed_two, w_up) + bias_up
    grad_activated = dot("td,dn->tn", cot_all, w_down)
    gelu_value, gelu_back = jax.vjp(partial(jax.nn.gelu, approximate=True), before)
    activated = gelu_value.astype(BF)
    grad_before = gelu_back(grad_activated)[0].astype(BF)

    grad_normed_two = own_sum(dot("tn,dn->td", grad_before, w_up))
    _, norm_back_two = jax.vjp(layer_norm, middle, vec[:, 2], vec[:, 3])
    grad_middle_part, grad_gain_two, grad_shift_two = norm_back_two(grad_normed_two)
    grad_middle = cotangent.astype(F32) + grad_middle_part
    grad_branch_own = grad_middle.astype(BF)
    grad_branch = lax.all_gather(grad_branch_own, "tp", axis=0, tiled=True)
    output = middle + own_sum(dot("tn,dn->td", activated, w_down)) + vec[:, 7]
    grad_attended = dot("td,dc->tc", grad_branch, w_out).astype(BF)
    grad_att = per_head(grad_attended)
    grad_prob = dot("rqhc,rkhc->rhqk", grad_att, value_rows)
    row_total = jnp.sum(probability * grad_prob, axis=-1, keepdims=True)
    grad_scores = (probability * (grad_prob - row_total)).astype(BF)
    scale = head ** (-0.5)
    grad_q = (dot("rhqk,rkhc->rqhc", grad_scores, key_rows) * scale).astype(BF).reshape(t_all, hc)
    grad_k = (dot("rhqk,rqhc->rkhc", grad_scores, queries) * scale).astype(BF).reshape(t_all, hc)
    grad_v = dot("rhqk,rqhc->rkhc", probability_low, grad_att).astype(BF).reshape(t_all, hc)
    grad_joined = jnp.concatenate([grad_q, grad_k, grad_v], axis=1)
    grad_normed_one = own_sum(dot("tn,dn->td", grad_joined, w_qkv))
    _, norm_back_one = jax.vjp(layer_norm, token_values, vec[:, 0], vec[:, 1])
    grad_tokens_part, grad_gain_one, grad_shift_one = norm_back_one(grad_normed_one)
    grad_tokens = grad_middle + grad_tokens_part

    def to_block_owners(left_right, count):
        per = per_of(count)
        parts = [dot("td,tn->dn", a, b).astype(BF) for a, b in left_right]
        joined_part = parts[0] if len(parts) == 1 else jnp.concatenate(parts, axis=1)
        joined_part = jnp.pad(joined_part, ((0, 0), (0, (per * groups - count) * head)))
        stacked = joined_part.reshape(d, groups, per * head).transpose(1, 0, 2)
        return lax.psum_scatter(stacked, FS, scatter_dimension=0, tiled=False)

    g_down = to_block_owners([(cot_all, activated)], inner)
    g_up = to_block_owners([(normed_two, grad_before)], inner)
    g_attn = to_block_owners([(normed_one, grad_joined), (grad_branch, attended)], attn_blocks)
    g_mine = jnp.concatenate([g_attn, g_up, g_down], axis=1)

    def to_row_owners(mine):
        back = lax.all_to_all(mine.astype(BF).reshape(world, rows, width), ALL, split_axis=0, concat_axis=0, tiled=True)
        back = back.reshape(hi, tp, sh, rows, width)
        pieces, at = [], 0
        for number, count in enumerate((attn_blocks, inner, inner)):
            per = per_of(count)
            piece = back[..., at : at + per * head].reshape(hi, tp, sh, rows, per, head)
            at += per * head
            piece = piece.transpose(3, 1, 0, 2, 4, 5).reshape(rows, tp, groups * per, head)[:, :, :count]
            if number == 0:
                piece = piece.reshape(rows, tp, 4, heads, head).transpose(0, 2, 1, 3, 4)
            pieces.append(piece.reshape(rows, -1, head))
        return jnp.concatenate(pieces, axis=1)

    weight_grad = to_row_owners(g_mine).astype(F32)
    moment_new = 0.95 * momentum + weight_grad

    moment_mine = 0.95 * mom_mine.astype(F32) + g_mine.astype(F32)
    orthogonal = newton_schulz(moment_mine.reshape(d, width // head, head)).reshape(d, width)
    orthogonal_rows = to_row_owners(orthogonal).astype(F32)
    new_weights = weights * (1.0 - 0.15 * 0.1) - 0.15 * 0.2 * math.sqrt(d) * orthogonal_rows

    plain = jnp.stack(
        [
            grad_gain_one,
            grad_shift_one,
            grad_gain_two,
            grad_shift_two,
            jnp.zeros((d,), F32),
            jnp.zeros((d,), F32),
            jnp.sum(grad_branch_own, axis=0, dtype=F32),
            jnp.sum(cotangent, axis=0, dtype=F32),
        ],
        axis=0,
    )
    plain = lax.dynamic_update_slice(plain, jnp.sum(grad_q, axis=0, dtype=F32)[None], (4, me * hc))
    plain = lax.dynamic_update_slice(plain, jnp.sum(grad_v, axis=0, dtype=F32)[None], (5, me * hc))
    hidden = jnp.zeros((inner_all * head,), F32)
    hidden = lax.dynamic_update_slice(hidden, jnp.sum(grad_before, axis=0, dtype=F32), (me * inner * head,))
    terms = jnp.concatenate([plain, hidden.reshape(-1, d)], axis=0)
    terms = terms.reshape(-1, world, rows).transpose(1, 0, 2).reshape(world, -1)
    vector_grad = jnp.sum(lax.all_to_all(terms, ALL, split_axis=0, concat_axis=0, tiled=True), axis=0)
    vector_grad = vector_grad.reshape(-1, rows).T
    first_moment = 0.9 * vector_moment + 0.1 * vector_grad
    second = 0.95 * vector_second + 0.05 * vector_grad * vector_grad
    corrected = first_moment / (1.0 - 0.9**STEP)
    normal_second = second / (1.0 - 0.95**STEP)
    next_vectors = vectors - 0.5 * corrected / (jnp.sqrt(normal_second) + 1e-08)
    return (
        output.astype(BF),
        grad_tokens,
        weight_grad,
        new_weights,
        moment_new,
        first_moment,
        second,
        next_vectors,
    )


def solution(mesh):
    dp, sh = mesh.shape["dp"], mesh.shape["shard"]
    tp = math.gcd(dp, 8)
    fine = Mesh(mesh.devices.reshape(dp // tp, tp, sh), ALL)
    two, three = P(ALL, None), P(ALL, None, None)
    return jax.shard_map(
        local,
        mesh=fine,
        in_specs=(two, two, three, three, two, two, two, two),
        out_specs=(two, two, three, three, three, two, two, two),
        check_vma=False,
    )
```

time: 3020 us -> 1430 us (0.47)
  waiting for transfers between devices: 2350 us -> 796 us
  matrix products: 311 us -> 200 us
  local copies, waits for them, and re-layouts: 50.4 us -> 152 us
  other arithmetic: 165 us -> 77.3 us
  blocking collectives: 108 us -> 155 us
    reduce_scatter x1 -> x7, waiting for transfers between devices: 1600 us -> 350 us  [the longest x3 187 us: to_block_owners(): return lax.psum_scatter(stacked, FS, scatter_dimension=0, tiled=False)]
    psum x5 -> x0, waiting for transfers between devices: 191 us -> none  [gram_total(): lax.psum(jnp.einsum('rkc,rke->kce', values, values, precision=HIGHEST).as...]
    concatenate x1 -> x3, other arithmetic: 133 us -> 9.28 us  [the longest x1 4.94 us: local(): jnp.concatenate([to_owners(p, c) for p, c in split(momentum.astype(BF))],...]
    all_gather x1 -> x6, waiting for transfers between devices: 465 us -> 346 us  [the longest x2 191 us: spread(): return rows_in_order(lax.all_gather(swapped, FS, axis=0, tiled=False))]
    dot_general x33 -> x32, matrix products: 311 us -> 195 us  [the longest x17 145 us: dot(): return jnp.einsum(spec, a, b, preferred_element_type=F32, **kw)]
    all_to_all x1 -> x3, waiting for transfers between devices: 0.01 us -> 98.2 us  [the longest x1 66.9 us: to_row_owners(): lax.all_to_all(mine.astype(BF).reshape(world, rows, width), ALL, split_ax...]
    unnamed x9 -> x13, waiting for transfers between devices: 97.6 us -> 1.4 us
    all_to_all x1 -> x3, blocking collectives: 40.2 us -> 126 us  [the longest x1 74.5 us: to_row_owners(): lax.all_to_all(mine.astype(BF).reshape(world, rows, width), ALL, split_ax...]
  transfers between devices with their start and end apart: 9 -> 16, of which waited for: 8 -> 14; matrix products, arithmetic and copies ran while one was open for 3% -> 23% of each run, Pallas kernels for 0% -> 0%
where the time goes in v1:
time: 1430 us; the launch traced here: 1420 us
  waiting for transfers between devices  796 us (56%)
  matrix products  200 us (14%)
  blocking collectives  155 us (11%)
  local copies, waits for them, and re-layouts  152 us (11%)
  other arithmetic  77.3 us (5%)
  starting transfers between devices  20.9 us (1%)
  between operations  15.3 us (1%)
    all_gather x2, waiting for transfers between devices, spread(): return rows_in_order(lax.all_gather(swapped, FS, axis=0, tiled=False))  191 us
    reduce_scatter x3, waiting for transfers between devices, to_block_owners(): return lax.psum_scatter(stacked, FS, scatter_dimension=0, tiled=False)  187 us
    reduce_scatter x4, waiting for transfers between devices, own_sum(): lax.psum_scatter(partial_rows.astype(BF), 'tp', scatter_dimension=0, tile...  164 us
    dot_general x17, matrix products, dot(): return jnp.einsum(spec, a, b, preferred_element_type=F32, **kw)  145 us
    all_to_all x1, blocking collectives, to_row_owners(): lax.all_to_all(mine.astype(BF).reshape(world, rows, width), ALL, split_ax...  74.5 us
    all_to_all x1, waiting for transfers between devices, to_row_owners(): lax.all_to_all(mine.astype(BF).reshape(world, rows, width), ALL, split_ax...  66.9 us
    all_gather x1, waiting for transfers between devices, local(): tok_all = lax.all_gather(tokens, 'tp', axis=0, tiled=True)  52.6 us
    all_to_all x2, blocking collectives, spread(): lax.all_to_all(array, 'tp', split_axis=0, concat_axis=0, tiled=True)  51.6 us
  transfers between devices with their start and end apart: 16, of which 14 were waited for; matrix products, arithmetic and copies ran while one was open for 23% of the time, Pallas kernels for 0%

profile of v1, /device:TPU:27, one launch (start us, length us, event | category | flops | bytes accessed | tf_op | source)
XLA Modules:
  0.0 1416.3 jit_solution(12227850754739351152)
XLA Ops:
  13.8 18.1 %all_to_all.35 = bf16[8,64,1024]{2,1,0:T(8,128)(2,1)} all-to-all(bf16[8,64,1024]{2,1,0:T(8,128)(2,1)S(1)} %reshape.316), channel_id=1, replica_groups=mesh['dp'=8,'shard'=4] {'dp'}, dimensions={0} | all-to-all | bytes 2097152 | tf_op jit(solution)/shard_map/all_to_all | solution.py:82
  32.8 9.1 all-gather.5
  42.0 8.1 all-gather.4
  50.1 11.4 all-gather.1
  64.1 48.0 %all-gather.21.cloned.1.call-done = bf16[32,64,1024]{2,1,0:T(8,128)(2,1)} async-done(((bf16[8,64,1024]{2,1,0:T(8,128)(2,1)}), bf16[32,64,1024]{2,1,0:T(8,128)(2,1)}) %all-gather.21.cloned.1.call-update) | async-done | bytes 4194320 | tf_op jit(solution)/shard_map/all_gather | solution.py:83
  117.0 52.6 %all-gather.13.cloned.1.call-done = bf16[2048,2048]{1,0:T(8,128)(2,1)} async-done(((bf16[256,2048]{1,0:T(8,128)(2,1)}), bf16[2048,2048]{1,0:T(8,128)(2,1)}) %all-gather.13.cloned.1.call-update) | async-done | bytes 8388624 | tf_op jit(solution)/shard_map/all_gather | solution.py:91
  181.4 6.9 fusion.29
  202.6 7.2 convolution_convert_fusion.3
  216.1 33.5 %all_to_all.36 = bf16[8,64,2048]{2,1,0:T(8,128)(2,1)} all-to-all(bf16[8,64,2048]{2,1,0:T(8,128)(2,1)S(1)} %reshape.324), channel_id=1, replica_groups=mesh['dp'=8,'shard'=4] {'dp'}, dimensions={0} | all-to-all | bytes 4194304 | tf_op jit(solution)/shard_map/all_to_all | solution.py:82
  249.6 38.9 %reduce-scatter.8.cloned.1.call-done = bf16[256,2048]{1,0:T(8,128)(2,1)} async-done(((bf16[2048,2048]{1,0:T(8,128)(2,1)}), bf16[256,2048]{1,0:T(8,128)(2,1)}) %reduce-scatter.8.cloned.1.call-update) | async-done | bytes 1048592 | tf_op jit(solution)/shard_map/reduce_scatter | solution.py:140
  294.3 142.8 %all-gather.23.cloned.1.call-done = bf16[32,64,2048]{2,1,0:T(8,128)(2,1)} async-done(((bf16[8,64,2048]{2,1,0:T(8,128)(2,1)}), bf16[32,64,2048]{2,1,0:T(8,128)(2,1)}) %all-gather.23.cloned.1.call-update) | async-done | bytes 8388624 | tf_op jit(solution)/shard_map/all_gather | solution.py:83
  437.2 8.3 copy.295
  445.4 49.8 %all-gather.15.cloned.1.call-done = bf16[2048,2048]{1,0:T(8,128)(2,1)} async-done(((bf16[256,2048]{1,0:T(8,128)(2,1)}), bf16[2048,2048]{1,0:T(8,128)(2,1)}) %all-gather.15.cloned.1.call-update) | async-done | bytes 8388624 | tf_op jit(solution)/shard_map/all_gather | solution.py:146
  495.3 14.8 %fusion.21 = f32[2048,1024]{1,0:T(8,128)} fusion(bf16[2048,2048]{1,0:T(8,128)(2,1)} %all-gather.15.cloned.1.call-done, bf16[2048,2048]{1,0:T(8,128)(2,1)} %bitcast.237), kind=kOutput, calls=%fused_computation.46 | convolution fusion | flops 8589934592 | bytes 20971520 | tf_op jit(solution)/shard_map/td,dn->tn/dot_general | solution.py:24
  510.1 41.5 %all-gather.17.cloned.1.call-done = bf16[2048,2048]{1,0:T(8,128)(2,1)} async-done(((bf16[256,2048]{1,0:T(8,128)(2,1)}), bf16[2048,2048]{1,0:T(8,128)(2,1)}) %all-gather.17.cloned.1.call-update) | async-done | bytes 8388624 | tf_op jit(solution)/shard_map/all_gather | solution.py:92
  551.6 20.7 %convert_reduce_fusion.1 = (f32[1024]{0:T(1024)}, bf16[2048,1024]{1,0:T(8,128)(2,1)S(1)}) fusion(f32[2048,1024]{1,0:T(8,128)} %fusion.21, f32[1024]{0:T(1024)S(1)} %dynamic_slice.11, bf16[2048,2048]{1,0:T(8,128)(2,1)} %all-gather.17.cloned.1.call-done, bf16[2048,2048]{1,0:T(8,128)(2,1)} %bitcast.238), kind=kOutput, calls=%fused_computation.18 | convolution fusion | flops 8638168064 | bytes 25174016 | tf_op jit(solution)/shard_map/td,dn->tn/dot_general | solution.py:24
  574.3 11.1 convolution_convert_fusion.1
  585.4 17.7 %convolution_convert_fusion.2 = bf16[2048,2048]{1,0:T(8,128)(2,1)} fusion(bf16[2048,2048]{1,0:T(8,128)(2,1)} %bitcast.239, f32[2048,1024]{1,0:T(8,128)} %fusion.21, f32[1024]{0:T(1024)S(1)} %dynamic_slice.11), kind=kOutput, calls=%fused_computation.22 | convolution fusion | flops 8615100416 | bytes 20975616 | tf_op jit(solution)/shard_map/tn,dn->td/dot_general | solution.py:24
  603.2 53.1 %reduce-scatter.12.cloned.1.call-done = bf16[256,2048]{1,0:T(8,128)(2,1)} async-done(((bf16[2048,2048]{1,0:T(8,128)(2,1)}), bf16[256,2048]{1,0:T(8,128)(2,1)}) %reduce-scatter.12.cloned.1.call-update) | async-done | bytes 1048592 | tf_op jit(solution)/shard_map/reduce_scatter | solution.py:140
  659.5 71.5 %reduce-scatter.10.cloned.1.call-done = bf16[256,2048]{1,0:T(8,128)(2,1)} async-done(((bf16[2048,2048]{1,0:T(8,128)(2,1)}), bf16[256,2048]{1,0:T(8,128)(2,1)}) %reduce-scatter.10.cloned.1.call-update) | async-done | bytes 1048592 | tf_op jit(solution)/shard_map/reduce_scatter | solution.py:140
  738.0 16.7 %convolution_convert_fusion.4 = bf16[1024,2048]{1,0:T(8,128)(2,1)} fusion(bf16[2048,2048]{1,0:T(8,128)(2,1)} %all-gather.17.cloned.1.call-done, f32[2048,1024]{1,0:T(8,128)} %fusion.21, f32[1024]{0:T(1024)S(1)} %dynamic_slice.11), kind=kOutput, calls=%fused_computation.40 | convolution fusion | flops 8613003264 | bytes 20975616 | tf_op jit(solution)/shard_map/td,tn->dn/dot_general | solution.py:24
  754.8 6.2 copy.309
  761.1 13.9 convolution_convert_fusion.5
  775.0 6.2 copy.308
  781.3 11.7 all-gather.19.cloned.1.call-done
  793.0 6.0 convolution_convert_fusion.8
  817.1 6.9 convolution_convert_fusion.6
  826.3 6.2 copy.307
  832.6 11.6 convolution_convert_fusion
  844.3 26.9 %reduce-scatter.20.cloned.1.call-done = bf16[1,2048,256]{2,1,0:T(8,128)(2,1)} async-done(((bf16[4,2048,256]{2,1,0:T(8,128)(2,1)}), bf16[1,2048,256]{2,1,0:T(8,128)(2,1)}) %reduce-scatter.20.cloned.1.call-update) | async-done | bytes 1048592 | tf_op jit(solution)/shard_map/reduce_scatter | solution.py:181
  871.2 79.6 %reduce-scatter.18.cloned.1.call-done = bf16[1,2048,256]{2,1,0:T(8,128)(2,1)} async-done(((bf16[4,2048,256]{2,1,0:T(8,128)(2,1)}), bf16[1,2048,256]{2,1,0:T(8,128)(2,1)}) %reduce-scatter.18.cloned.1.call-update) | async-done | bytes 1048592 | tf_op jit(solution)/shard_map/reduce_scatter | solution.py:181
  950.8 80.1 %reduce-scatter.16.cloned.1.call-done = bf16[1,2048,256]{2,1,0:T(8,128)(2,1)} async-done(((bf16[4,2048,256]{2,1,0:T(8,128)(2,1)}), bf16[1,2048,256]{2,1,0:T(8,128)(2,1)}) %reduce-scatter.16.cloned.1.call-update) | async-done | bytes 1048592 | tf_op jit(solution)/shard_map/reduce_scatter | solution.py:181
  1032.9 74.5 %all_to_all.37 = bf16[32,64,768]{2,1,0:T(8,128)(2,1)S(1)} all-to-all(bf16[32,64,768]{2,1,0:T(8,128)(2,1)S(1)} %pad_maximum_fusion.1), channel_id=1, replica_groups=mesh['dp'=8,'shard'=4] {'dp','shard'}, dimensions={0} | all-to-all | bytes 6291456 | tf_op jit(solution)/shard_map/all_to_all | solution.py:189
  1119.6 10.6 multiply_add_fusion
  1149.2 6.5 all-to-all-start.3
  1165.7 8.4 copy.321
  1174.1 9.0 reshape.357
  1191.9 31.3 %all-to-all-done.3 = bf16[32,64,768]{2,1,0:T(8,128)(2,1)} async-done(((bf16[32,64,768]{2,1,0:T(8,128)(2,1)}), bf16[32,64,768]{2,1,0:T(8,128)(2,1)}, u32[]{:S(2)}, u32[]{:S(2)}) %all-to-all-start.3) | async-done | bytes 3145760 | tf_op jit(solution)/shard_map/all_to_all | solution.py:112
  1223.2 7.9 all-to-all-start.5
  1231.1 7.7 multiply_reduce_fusion
  1238.9 8.5 mul.379
  1247.4 8.4 copy.320
  1255.9 11.1 fusion.64
  1267.3 7.3 bitcast_add_fusion.4
  1306.0 6.3 copy.337
  1312.4 7.7 convert_element_type.223
  1320.1 5.9 all-to-all-start.4
  1326.8 66.9 %all-to-all-done.4 = bf16[32,64,768]{2,1,0:T(8,128)(2,1)} async-done(((bf16[32,64,768]{2,1,0:T(8,128)(2,1)}), bf16[32,64,768]{2,1,0:T(8,128)(2,1)}, u32[]{:S(2)}, u32[]{:S(2)}) %all-to-all-start.4) | async-done | bytes 3145760 | tf_op jit(solution)/shard_map/all_to_all | solution.py:189
  (262 shorter events, 185.8 us)
Async XLA Ops:
  7.2 104.9 %all-gather.21.cloned.1.call-start = ((), (), s32[]{:S(2)}) async-start(), calls=%async_computation.24 | async-start | bytes 5242880 | tf_op jit(solution)/shard_map/all_gather | solution.py:83
  12.3 20.5 %copy-start.43 = (s32[1,4]{1,0:T(1,128)S(1)}, s32[1,4]{1,0:T(1,128)}, u32[]{:S(2)}) copy-start(s32[1,4]{1,0:T(1,128)} %param.9) | copy-start | bytes 52
  12.3 29.7 %copy-start.35 = (f32[64,12]{0,1:T(8,128)S(1)}, f32[64,12]{0,1:T(8,128)}, u32[]{:S(2)}) copy-start(f32[64,12]{0,1:T(8,128)} %param.12) | copy-start | bytes 9220
  32.0 137.6 %all-gather.13.cloned.1.call-start = ((), (), s32[]{:S(2)}) async-start(), calls=%async_computation.13 | async-start | bytes 9437184 | tf_op jit(solution)/shard_map/all_gather | solution.py:91
  32.7 255.7 %reduce-scatter.8.cloned.1.call-start = ((), (), s32[]{:S(2)}) async-start(), calls=%async_computation.14 | async-start | bytes 9437184 | tf_op jit(solution)/shard_map/reduce_scatter | solution.py:140
  62.4 115.3 %copy-start.30 = (f32[2048,1]{0,1:T(1,128)}, f32[2048,1]{0,1:T(1,128)S(1)}, u32[]{:S(2)}) copy-start(f32[2048,1]{0,1:T(1,128)S(1)} %get-tuple-element.52) | copy-start | bytes 24580
  169.6 5.8 copy-start.1
  177.7 3.7 copy-start.11
  181.4 7.0 copy-start.9
  191.1 7.8 copy-start.22
  192.1 6.7 copy-start.14
  193.9 5.0 copy-start.27
  202.6 7.2 copy-start.12
  209.9 227.3 %all-gather.23.cloned.1.call-start = ((), (), s32[]{:S(2)}) async-start(), calls=%async_computation.25 | async-start | bytes 10485760 | tf_op jit(solution)/shard_map/all_gather | solution.py:83
  216.1 72.4 %copy-start = (bf16[256,2048]{1,0:T(8,128)(2,1)S(1)}, bf16[256,2048]{1,0:T(8,128)(2,1)}, u32[]{:S(2)}) copy-start(bf16[256,2048]{1,0:T(8,128)(2,1)} %param.8) | copy-start | bytes 3145732
  249.6 245.7 %all-gather.15.cloned.1.call-start = ((), (), s32[]{:S(2)}) async-start(), calls=%async_computation.15 | async-start | bytes 9437184 | tf_op jit(solution)/shard_map/all_gather | solution.py:146
  293.7 257.9 %all-gather.17.cloned.1.call-start = ((), (), s32[]{:S(2)}) async-start(), calls=%async_computation.17 | async-start | bytes 9437184 | tf_op jit(solution)/shard_map/all_gather | solution.py:92
  294.3 362.0 %reduce-scatter.12.cloned.1.call-start = ((), (), s32[]{:S(2)}) async-start(), calls=%async_computation.18 | async-start | bytes 9437184 | tf_op jit(solution)/shard_map/reduce_scatter | solution.py:140
  551.6 22.7 %copy-start.10 = (bf16[1,8,4,64,2048]{4,3,2,1,0:T(8,128)(2,1)S(1)}, bf16[1,8,4,64,2048]{4,3,2,1,0:T(8,128)(2,1)}, u32[]{:S(2)}) copy-start(bf16[1,8,4,64,2048]{4,3,2,1,0:T(8,128)(2,1)} %copy.295) | copy-start | bytes 25165828
  585.4 145.7 %reduce-scatter.10.cloned.1.call-start = ((), (), s32[]{:S(2)}) async-start(), calls=%async_computation.16 | async-start | bytes 9437184 | tf_op jit(solution)/shard_map/reduce_scatter | solution.py:140
  603.1 127.9 %copy-start.37 = (f32[2048,1]{0,1:T(1,128)S(1)}, f32[2048,1]{0,1:T(1,128)}, u32[]{:S(2)}) copy-start(f32[2048,1]{0,1:T(1,128)} %get-tuple-element.45) | copy-start | bytes 24580
  603.1 189.9 %all-gather.19.cloned.1.call-start = ((), (), s32[]{:S(2)}) async-start(), calls=%async_computation.19 | async-start | bytes 9437184 | tf_op jit(solution)/shard_map/all_gather | solution.py:158
  659.5 76.5 %copy-start.6 = (bf16[256,2048]{1,0:T(8,128)(2,1)S(1)}, bf16[256,2048]{1,0:T(8,128)(2,1)}, u32[]{:S(2)}) copy-start(bf16[256,2048]{1,0:T(8,128)(2,1)} %param.15) | copy-start | bytes 3145732
  738.0 133.2 %reduce-scatter.20.cloned.1.call-start = ((), (), s32[]{:S(2)}) async-start(), calls=%async_computation.23 | async-start | bytes 5242880 | tf_op jit(solution)/shard_map/reduce_scatter | solution.py:181
  761.0 189.8 %reduce-scatter.18.cloned.1.call-start = ((), (), s32[]{:S(2)}) async-start(), calls=%async_computation.22 | async-start | bytes 5242880 | tf_op jit(solution)/shard_map/reduce_scatter | solution.py:181
  781.3 249.6 %reduce-scatter.16.cloned.1.call-start = ((), (), s32[]{:S(2)}) async-start(), calls=%async_computation.21 | async-start | bytes 5242880 | tf_op jit(solution)/shard_map/reduce_scatter | solution.py:181
  800.5 4.9 copy-start.28
  811.9 4.0 slice-start.1
  813.5 3.6 slice-start.2
  832.6 350.5 %reduce-scatter.14.cloned.1.call-start = ((), (), s32[]{:S(2)}) async-start(), calls=%async_computation.20 | async-start | bytes 9437184 | tf_op jit(solution)/shard_map/reduce_scatter | solution.py:140
  1136.5 4.4 copy-start.25
  1149.2 6.6 copy-start.42
  1149.2 6.9 copy-start.24
  1149.2 74.0 %all-to-all-start.3 = ((bf16[32,64,768]{2,1,0:T(8,128)(2,1)}), bf16[32,64,768]{2,1,0:T(8,128)(2,1)}, u32[]{:S(2)}, u32[]{:S(2)}) async-start(bf16[32,64,768]{2,1,0:T(8,128)(2,1)} %bitcast.231), calls=%async_computation.10 | async-start | bytes 6291456 | tf_op jit(solution)/shard_map/all_to_all | solution.py:112
  1156.8 8.9 copy-start.16
  1158.6 7.0 copy-start.18
  1174.1 9.0 copy-start.31
  1183.0 4.7 copy-start.4
  1183.1 4.7 copy-start.7
  1183.1 4.7 copy-start.8
  1223.2 96.9 %all-to-all-start.5 = ((f32[32,1,768]{2,1,0:T(1,128)}), f32[32,1,768]{2,1,0:T(1,128)S(1)}, u32[]{:S(2)}, u32[]{:S(2)}) async-start(f32[32,1,768]{2,1,0:T(1,128)} %all_to_all.28), calls=%async_computation.12 | async-start | bytes 196608 | tf_op jit(solution)/shard_map/all_to_all | solution.py:229
  1247.4 8.4 copy-start.17
  1247.4 8.4 copy-start.19
  1247.4 8.4 copy-start.20
  1320.1 6.1 copy-start.36
  1320.1 6.1 copy-start.40
  1320.1 6.1 copy-start.41
  1320.1 73.6 %all-to-all-start.4 = ((bf16[32,64,768]{2,1,0:T(8,128)(2,1)}), bf16[32,64,768]{2,1,0:T(8,128)(2,1)}, u32[]{:S(2)}, u32[]{:S(2)}) async-start(bf16[32,64,768]{2,1,0:T(8,128)(2,1)} %convert_element_type.223), calls=%async_computation.11 | async-start | bytes 6291456 | tf_op jit(solution)/shard_map/all_to_all | solution.py:189
  (18 other events, 40.3 us)
Sparse Core Ops, SparseCore 0:
  32.1 79.9 all-gather.20
  114.0 55.5 all-gather.12
  210.0 78.4 reduce-scatter.7
  290.0 147.1 all-gather.22
  439.6 55.6 all-gather.14
  497.2 54.3 all-gather.16
  585.5 70.7 reduce-scatter.11
  659.7 71.2 reduce-scatter.9
  738.1 54.8 all-gather.18
  795.3 75.8 reduce-scatter.19
  873.5 77.2 reduce-scatter.17
  953.6 77.2 reduce-scatter.15
  1034.4 86.0 reduce-scatter.13

commit v2 on v1

--- a/solution.py
+++ b/solution.py
@@ -4,6 +4,8 @@
 import jax
 import jax.numpy as jnp
 from jax import lax
+from jax.experimental import pallas as pl
+from jax.experimental.pallas import tpu as pltpu
 from jax.sharding import Mesh, PartitionSpec as P
 
 HEADS = 16
@@ -18,6 +20,299 @@
 F32 = jnp.float32
 ALL = ("hi", "tp", "shard")
 FS = ("hi", "shard")
+
+
+MESH = pl.DeviceIdType.MESH
+WIDE = 256
+
+
+def rem(a, b):
+    return lax.rem(a, jnp.int32(b))
+
+
+def div(a, b):
+    return lax.div(a, jnp.int32(b))
+
+
+def spots():
+    me = lax.axis_index("tp")
+    c, x, y = rem(me, 2), rem(div(me, 2), 2), div(me, 4)
+    return me, c, x, y, me + 1 - 2 * c, me + 2 - 4 * x, me + 4 - 8 * y
+
+
+def meet(peers):
+    barrier = pltpu.get_barrier_semaphore()
+    for peer in peers:
+        pl.semaphore_signal(barrier, inc=1, device_id={"tp": peer}, device_id_type=MESH)
+    pl.semaphore_wait(barrier, len(peers))
+
+
+def remote(src, dst, send, recv, peer):
+    return pltpu.make_async_remote_copy(
+        src_ref=src, dst_ref=dst, send_sem=send, recv_sem=recv, device_id={"tp": peer}, device_id_type=MESH
+    )
+
+
+def sum_scratch(rows, width):
+    count = width // WIDE
+    return [
+        pltpu.VMEM((count, 2, 2, 2, rows, WIDE), BF),
+        pltpu.VMEM((count, 2, 2, rows, WIDE), BF),
+        pltpu.VMEM((count, 2, rows, WIDE), BF),
+        pltpu.VMEM((count, rows, WIDE), BF),
+        pltpu.SemaphoreType.DMA((3, count)),
+        pltpu.SemaphoreType.DMA((3, count)),
+    ]
+
+
+class Summing:
+    def __init__(self, left, right, total, scratch):
+        self.left, self.right, self.total = left, right, total
+        self.part, self.from_c, self.from_1, self.from_2, self.send, self.recv = scratch
+        self.count = self.part.shape[0]
+        self.rows = self.part.shape[4]
+        self.copies = {}
+
+    def fill(self, k):
+        right = self.right[k * WIDE : (k + 1) * WIDE, :]
+
+        def one(dest, carry):
+            rows = self.left[pl.ds(pl.multiple_of(dest * self.rows, self.rows), self.rows), :]
+            made = lax.dot_general(rows, right, (((1,), (1,)), ((), ())), preferred_element_type=F32)
+            self.part[k, div(dest, 4), rem(div(dest, 2), 2), rem(dest, 2)] = made.astype(BF)
+            return carry
+
+        lax.fori_loop(0, 8, one, 0)
+
+    def begin(self, stage, k, src, dst, peer):
+        copy = remote(src, dst, self.send.at[stage, k], self.recv.at[stage, k], peer)
+        copy.start()
+        self.copies[stage, k] = copy
+
+    def run(self):
+        me, c, x, y, pc, px, py = spots()
+        oc, ox, oy = 1 - c, 1 - x, 1 - y
+        part = self.part
+
+        def core_stage(k):
+            self.copies[0, k].wait_recv()
+            for i in range(4):
+                a, b = i // 2, i % 2
+                part[k, a, b, c] = (part[k, a, b, c].astype(F32) + self.from_c[k, a, b].astype(F32)).astype(BF)
+            if k % 2 == 0:
+                self.begin(1, k, part.at[k, :, ox, c], self.from_1.at[k], px)
+            else:
+                self.begin(1, k, part.at[k, oy, :, c], self.from_1.at[k], py)
+
+        for k in range(self.count):
+            self.fill(k)
+            self.begin(0, k, part.at[k, :, :, oc], self.from_c.at[k], pc)
+            if k:
+                core_stage(k - 1)
+        core_stage(self.count - 1)
+        for k in range(self.count):
+            self.copies[1, k].wait_recv()
+            for i in range(2):
+                if k % 2 == 0:
+                    part[k, i, x, c] = (part[k, i, x, c].astype(F32) + self.from_1[k, i].astype(F32)).astype(BF)
+                else:
+                    part[k, y, i, c] = (part[k, y, i, c].astype(F32) + self.from_1[k, i].astype(F32)).astype(BF)
+            if k % 2 == 0:
+                self.begin(2, k, part.at[k, oy, x, c], self.from_2.at[k], py)
+            else:
+                self.begin(2, k, part.at[k, y, ox, c], self.from_2.at[k], px)
+        for k in range(self.count):
+            self.copies[2, k].wait_recv()
+            self.total[:, k * WIDE : (k + 1) * WIDE] = part[k, y, x, c].astype(F32) + self.from_2[k].astype(F32)
+
+    def end(self):
+        for copy in self.copies.values():
+            copy.wait_send()
+
+
+class Gathering:
+    def __init__(self, own, out, send, recv, local):
+        self.own, self.out, self.send, self.recv, self.local = own, out, send, recv, local
+        self.copies = []
+
+    def begin(self, src, dst, peer):
+        n = len(self.copies)
+        copy = remote(src, dst, self.send.at[n], self.recv.at[n], peer)
+        copy.start()
+        self.copies.append(copy)
+        return copy
+
+    def start(self):
+        me, c, x, y, pc, px, py = spots()
+        self.spots = me, px, py, pc
+        own, out = self.own, self.out
+        half = own.shape[-1] // 2
+        self.low, self.high = pl.ds(0, half), pl.ds(half, half)
+        low, high = self.low, self.high
+        self.px_high = self.begin(own.at[:, high], out.at[me, :, high], px)
+        self.py_low = self.begin(own.at[:, low], out.at[me, :, low], py)
+        self.begin(own, out.at[me], pc)
+        self.px_low = self.begin(own.at[:, low], out.at[me, :, low], px)
+        self.py_high = self.begin(own.at[:, high], out.at[me, :, high], py)
+        self.kept = pltpu.make_async_copy(own, out.at[me], self.local)
+        self.kept.start()
+
+    def forward(self):
+        me, px, py, pc = self.spots
+        out, low, high = self.out, self.low, self.high
+        across = px + py - me
+        self.px_high.wait_recv()
+        a = self.begin(out.at[px, :, high], out.at[px, :, high], py)
+        self.begin(out.at[px, :, high], out.at[px, :, high], pc)
+        self.py_low.wait_recv()
+        b = self.begin(out.at[py, :, low], out.at[py, :, low], px)
+        self.begin(out.at[py, :, low], out.at[py, :, low], pc)
+        self.px_low.wait_recv()
+        self.begin(out.at[px, :, low], out.at[px, :, low], pc)
+        self.py_high.wait_recv()
+        self.begin(out.at[py, :, high], out.at[py, :, high], pc)
+        a.wait_recv()
+        self.begin(out.at[across, :, high], out.at[across, :, high], pc)
+        b.wait_recv()
+        self.begin(out.at[across, :, low], out.at[across, :, low], pc)
+        self.seen = (0, 1, 3, 4, 5, 7)
+
+    def end(self):
+        for n, copy in enumerate(self.copies):
+            if n not in self.seen:
+                copy.wait_recv()
+            copy.wait_send()
+        self.kept.wait()
+
+
+def gather_scratch():
+    return [pltpu.SemaphoreType.DMA((13,)), pltpu.SemaphoreType.DMA((13,)), pltpu.SemaphoreType.DMA]
+
+
+def row_loop(rows, body):
+    def one(i, carry):
+        body(pl.ds(pl.multiple_of(i * 16, 16), 16))
+        return carry
+
+    lax.fori_loop(0, rows // 16, one, 0)
+
+
+def normalized(values):
+    average = jnp.mean(values, axis=-1, keepdims=True)
+    centered = values - average
+    variance = jnp.mean(centered * centered, axis=-1, keepdims=True)
+    scale = lax.rsqrt(variance + 1e-05)
+    return centered * scale, scale
+
+
+def norm_back(values, grad, gain):
+    unit, scale = normalized(values)
+    weighted = grad * gain
+    mean_one = jnp.mean(weighted, axis=-1, keepdims=True)
+    mean_two = jnp.mean(weighted * unit, axis=-1, keepdims=True)
+    return scale * (weighted - mean_one - unit * mean_two), grad * unit
+
+
+def gather_kernel(one_ref, two_ref, one_out, two_out, *sems):
+    me, c, x, y, pc, px, py = spots()
+    meet((pc, px, py))
+    one = Gathering(one_ref, one_out, *sems[:3])
+    two = Gathering(two_ref, two_out, *sems[3:])
+    one.start()
+    one.forward()
+    two.start()
+    two.forward()
+    one.end()
+    two.end()
+
+
+def middle_kernel(att, w_out, tok, vec, middle, normed_all, total, own, *scratch):
+    me, c, x, y, pc, px, py = spots()
+    meet((pc, px, py))
+    sums = Summing(att, w_out, total, scratch[:6])
+    sums.run()
+
+    def body(at):
+        values = tok[at, :].astype(F32) + total[at, :] + vec[6:7, :]
+        middle[at, :] = values
+        unit, _ = normalized(values)
+        own[at, :] = (unit * vec[2:3, :] + vec[3:4, :]).astype(BF)
+
+    row_loop(own.shape[0], body)
+    spread = Gathering(own, normed_all, *scratch[6:])
+    spread.start()
+    spread.forward()
+    sums.end()
+    spread.end()
+
+
+def branch_kernel(grad_before, w_up, middle, cot, vec, grad_middle, sums_out, branch_all, total, own, *scratch):
+    me, c, x, y, pc, px, py = spots()
+    meet((pc, px, py))
+    sums = Summing(grad_before, w_up, total, scratch[:6])
+    sums.run()
+    sums_out[...] = jnp.zeros_like(sums_out)
+
+    def body(at):
+        grad = total[at, :]
+        part, for_gain = norm_back(middle[at, :], grad, vec[2:3, :])
+        back = cot[at, :].astype(F32)
+        whole = back + part
+        grad_middle[at, :] = whole
+        low = whole.astype(BF)
+        own[at, :] = low
+        low = low.astype(F32)
+        for n, values in enumerate((for_gain, grad, low, back)):
+            sums_out[n] += values[:8] + values[8:]
+
+    row_loop(own.shape[0], body)
+    spread = Gathering(own, branch_all, *scratch[6:])
+    spread.start()
+    spread.forward()
+    sums.end()
+    spread.end()
+
+
+def last_kernel(grad_joined, w_qkv, activated, w_down, tok, middle, grad_middle, vec, grad_tokens, sums_out, output, total, *scratch):
+    me, c, x, y, pc, px, py = spots()
+    meet((pc, px, py))
+    sums = Summing(grad_joined, w_qkv, total, scratch[:6])
+    sums.run()
+    sums_out[...] = jnp.zeros_like(sums_out)
+
+    def body(at):
+        grad = total[at, :]
+        part, for_gain = norm_back(tok[at, :].astype(F32), grad, vec[0:1, :])
+        grad_tokens[at, :] = grad_middle[at, :] + part
+        for n, values in enumerate((for_gain, grad)):
+            sums_out[n] += values[:8] + values[8:]
+
+    row_loop(total.shape[0], body)
+    more = Summing(activated, w_down, total, scratch[6:])
+    more.run()
+
+    def body_two(at):
+        output[at, :] = (middle[at, :] + total[at, :] + vec[7:8, :]).astype(BF)
+
+    row_loop(total.shape[0], body_two)
+    sums.end()
+    more.end()
+
+
+def call(body, ins, outs, scratch, number, microseconds, name):
+    spec = {True: pl.BlockSpec(memory_space=pl.ANY), False: pl.BlockSpec(memory_space=pltpu.VMEM)}
+    return pl.pallas_call(
+        body,
+        out_shape=[s for s, _ in outs],
+        in_specs=[spec[stays] for _, stays in ins],
+        out_specs=[spec[stays] for _, stays in outs],
+        scratch_shapes=scratch,
+        compiler_params=pltpu.CompilerParams(
+            collective_id=number, has_side_effects=True, vmem_limit_bytes=60 * 2**20
+        ),
+        cost_estimate=pl.CostEstimate(flops=0, transcendentals=0, bytes_accessed=int(microseconds * 3.0e6)),
+        name=name,
+    )(*[a for a, _ in ins])
 
 
 def dot(spec, a, b, **kw):
@@ -88,8 +383,11 @@
     vec = lax.all_gather(vec, FS, axis=0, tiled=False)
     vec = vec.reshape(hi, sh, tp, rows, -1).transpose(0, 2, 1, 3, 4).reshape(d, -1).astype(F32)
 
-    tok_all = lax.all_gather(tokens, "tp", axis=0, tiled=True)
-    cot_all = lax.all_gather(cotangent, "tp", axis=0, tiled=True)
+    gathered = jax.ShapeDtypeStruct((tp, row_tokens, d), BF)
+    tok_all, cot_all = call(
+        gather_kernel, [(tokens, True), (cotangent, True)], [(gathered, True)] * 2, gather_scratch() * 2, 1, 75, "gather_rows"
+    )
+    tok_all, cot_all = tok_all.reshape(t_all, d), cot_all.reshape(t_all, d)
     lengths = lax.all_gather(doc_lengths, "tp", axis=0, tiled=True)
     allowed = allowed_mask(lengths, row_tokens)
 
@@ -136,27 +434,35 @@
     probability_low = probability.astype(BF)
     attended = dot("rhqk,rkhc->rqhc", probability_low, value_rows).astype(BF).reshape(t_all, hc)
 
-    def own_sum(partial_rows):
-        return lax.psum_scatter(partial_rows.astype(BF), "tp", scatter_dimension=0, tiled=True).astype(F32)
-
-    branch = own_sum(dot("tc,dc->td", attended, w_out)) + vec[:, 6]
-    token_values = tokens.astype(F32)
-    middle = token_values + branch
-    normed_two_own = layer_norm(middle, vec[:, 2], vec[:, 3]).astype(BF)
-    normed_two = lax.all_gather(normed_two_own, "tp", axis=0, tiled=True)
+    vec_rows = jnp.pad(vec.T, ((0, 4), (0, 0)))
+    own_f32 = jax.ShapeDtypeStruct((row_tokens, d), F32)
+    own_scratch = [pltpu.VMEM((row_tokens, d), F32), pltpu.VMEM((row_tokens, d), BF)]
+    middle, normed_two = call(
+        middle_kernel,
+        [(attended, False), (w_out, False), (tokens, False), (vec_rows, False)],
+        [(own_f32, False), (gathered, True)],
+        own_scratch + sum_scratch(row_tokens, d) + gather_scratch(),
+        2,
+        95,
+        "attention_output",
+    )
+    normed_two = normed_two.reshape(t_all, d)
     before = dot("td,dn->tn", normed_two, w_up) + bias_up
     grad_activated = dot("td,dn->tn", cot_all, w_down)
     gelu_value, gelu_back = jax.vjp(partial(jax.nn.gelu, approximate=True), before)
     activated = gelu_value.astype(BF)
     grad_before = gelu_back(grad_activated)[0].astype(BF)
 
-    grad_normed_two = own_sum(dot("tn,dn->td", grad_before, w_up))
-    _, norm_back_two = jax.vjp(layer_norm, middle, vec[:, 2], vec[:, 3])
-    grad_middle_part, grad_gain_two, grad_shift_two = norm_back_two(grad_normed_two)
-    grad_middle = cotangent.astype(F32) + grad_middle_part
-    grad_branch_own = grad_middle.astype(BF)
-    grad_branch = lax.all_gather(grad_branch_own, "tp", axis=0, tiled=True)
-    output = middle + own_sum(dot("tn,dn->td", activated, w_down)) + vec[:, 7]
+    grad_middle, sums_two, grad_branch = call(
+        branch_kernel,
+        [(grad_before, False), (w_up, False), (middle, False), (cotangent, False), (vec_rows, False)],
+        [(own_f32, False), (jax.ShapeDtypeStruct((4, 8, d), F32), False), (gathered, True)],
+        own_scratch + sum_scratch(row_tokens, d) + gather_scratch(),
+        3,
+        95,
+        "second_norm_backward",
+    )
+    grad_branch = grad_branch.reshape(t_all, d)
     grad_attended = dot("td,dc->tc", grad_branch, w_out).astype(BF)
     grad_att = per_head(grad_attended)
     grad_prob = dot("rqhc,rkhc->rhqk", grad_att, value_rows)
@@ -167,10 +473,16 @@
     grad_k = (dot("rhqk,rqhc->rkhc", grad_scores, queries) * scale).astype(BF).reshape(t_all, hc)
     grad_v = dot("rhqk,rqhc->rkhc", probability_low, grad_att).astype(BF).reshape(t_all, hc)
     grad_joined = jnp.concatenate([grad_q, grad_k, grad_v], axis=1)
-    grad_normed_one = own_sum(dot("tn,dn->td", grad_joined, w_qkv))
-    _, norm_back_one = jax.vjp(layer_norm, token_values, vec[:, 0], vec[:, 1])
-    grad_tokens_part, grad_gain_one, grad_shift_one = norm_back_one(grad_normed_one)
-    grad_tokens = grad_middle + grad_tokens_part
+    grad_tokens, sums_one, output = call(
+        last_kernel,
+        [(grad_joined, False), (w_qkv, False), (activated, False), (w_down, False)]
+        + [(tokens, False), (middle, False), (grad_middle, False), (vec_rows, False)],
+        [(own_f32, False), (jax.ShapeDtypeStruct((2, 8, d), F32), False), (jax.ShapeDtypeStruct((row_tokens, d), BF), False)],
+        own_scratch[:1] + sum_scratch(row_tokens, d) * 2,
+        4,
+        85,
+        "first_norm_backward",
+    )
 
     def to_block_owners(left_right, count):
         per = per_of(count)
@@ -207,16 +519,17 @@
     orthogonal_rows = to_row_owners(orthogonal).astype(F32)
     new_weights = weights * (1.0 - 0.15 * 0.1) - 0.15 * 0.2 * math.sqrt(d) * orthogonal_rows
 
+    sums_one, sums_two = jnp.sum(sums_one, axis=1), jnp.sum(sums_two, axis=1)
     plain = jnp.stack(
         [
-            grad_gain_one,
-            grad_shift_one,
-            grad_gain_two,
-            grad_shift_two,
+            sums_one[0],
+            sums_one[1],
+            sums_two[0],
+            sums_two[1],
             jnp.zeros((d,), F32),
             jnp.zeros((d,), F32),
-            jnp.sum(grad_branch_own, axis=0, dtype=F32),
-            jnp.sum(cotangent, axis=0, dtype=F32),
+            sums_two[2],
+            sums_two[3],
         ],
         axis=0,
     )
@@ -234,7 +547,7 @@
     normal_second = second / (1.0 - 0.95**STEP)
     next_vectors = vectors - 0.5 * corrected / (jnp.sqrt(normal_second) + 1e-08)
     return (
-        output.astype(BF),
+        output,
         grad_tokens,
         weight_grad,
         new_weights,

time: 1430 us -> 1110 us (0.78)
  waiting for transfers between devices: 796 us -> 145 us
  Pallas kernels: 0 us -> 378 us
  matrix products: 200 us -> 162 us
    pallas_call x0 -> x4, Pallas kernels: none -> 378 us  [call(): pl.pallas_call(body, out_shape=[s for s, _ in outs], in_specs=[spec[stays...]
    all_gather x2, waiting for transfers between devices: 191 us -> 0.02 us  [spread(): return rows_in_order(lax.all_gather(swapped, FS, axis=0, tiled=False))]
    reduce_scatter x4 -> x0, waiting for transfers between devices: 164 us -> none  [own_sum(): lax.psum_scatter(partial_rows.astype(BF), 'tp', scatter_dimension=0, tile...]
    all_gather x4 -> x0, waiting for transfers between devices: 156 us -> none  [the longest x1 52.6 us: local(): tok_all = lax.all_gather(tokens, 'tp', axis=0, tiled=True)]
    reduce_scatter x3, waiting for transfers between devices: 187 us -> 78.7 us  [to_block_owners(): return lax.psum_scatter(stacked, FS, scatter_dimension=0, tiled=False)]
    dot_general x17 -> x13, matrix products: 145 us -> 109 us  [dot(): return jnp.einsum(spec, a, b, preferred_element_type=F32, **kw)]
    all_to_all x1, waiting for transfers between devices: 31.3 us -> 0.01 us  [local(): lax.all_to_all(mom_send.reshape(world, rows, width), ALL, split_axis=0, c...]
  transfers between devices with their start and end apart: 16 -> 8, of which waited for: 14 -> 2; matrix products, arithmetic and copies ran while one was open for 23% -> 25% of each run, Pallas kernels for 0% -> 34%
where the time goes in v2:
time: 1110 us; the launch traced here: 1100 us
  Pallas kernels  378 us (34%)
  local copies, waits for them, and re-layouts  163 us (15%)
  matrix products  162 us (15%)
  blocking collectives  154 us (14%)
  waiting for transfers between devices  145 us (13%)
  other arithmetic  63.4 us (6%)
  starting transfers between devices  19.7 us (2%)
  between operations  15.1 us (1%)
    pallas_call x4, Pallas kernels, call(): pl.pallas_call(body, out_shape=[s for s, _ in outs], in_specs=[spec[stays...  378 us
    dot_general x13, matrix products, dot(): return jnp.einsum(spec, a, b, preferred_element_type=F32, **kw)  109 us
    reduce_scatter x3, waiting for transfers between devices, to_block_owners(): return lax.psum_scatter(stacked, FS, scatter_dimension=0, tiled=False)  78.7 us
    all_to_all x1, blocking collectives, to_row_owners(): lax.all_to_all(mine.astype(BF).reshape(world, rows, width), ALL, split_ax...  74.6 us
    all_to_all x1, waiting for transfers between devices, to_row_owners(): lax.all_to_all(mine.astype(BF).reshape(world, rows, width), ALL, split_ax...  66 us
    all_to_all x2, blocking collectives, spread(): lax.all_to_all(array, 'tp', split_axis=0, concat_axis=0, tiled=True)  49.7 us
    dot_general x15, matrix products, ein(): jnp.einsum(spec, a, b, precision=lax.Precision.HIGH, preferred_element_ty...  47.7 us
  transfers between devices with their start and end apart: 8, of which 2 were waited for; matrix products, arithmetic and copies ran while one was open for 25% of the time, Pallas kernels for 34%

profile of v2, /device:TPU:27, one launch (start us, length us, event | category | flops | bytes accessed | tf_op | source)
XLA Modules:
  0.0 1099.1 jit_solution(10835159484148216912)
XLA Ops:
  15.0 18.7 %all_to_all.35 = bf16[8,64,1024]{2,1,0:T(8,128)(2,1)} all-to-all(bf16[8,64,1024]{2,1,0:T(8,128)(2,1)} %reshape.276), channel_id=1, replica_groups=mesh['dp'=8,'shard'=4] {'dp'}, dimensions={0} | all-to-all | bytes 2097152 | tf_op jit(solution)/shard_map/all_to_all | solution.py:377
  36.7 30.9 %all_to_all.36 = bf16[8,64,2048]{2,1,0:T(8,128)(2,1)} all-to-all(bf16[8,64,2048]{2,1,0:T(8,128)(2,1)} %reshape.283), channel_id=1, replica_groups=mesh['dp'=8,'shard'=4] {'dp'}, dimensions={0} | all-to-all | bytes 4194304 | tf_op jit(solution)/shard_map/all_to_all | solution.py:377
  67.7 9.1 all-gather.5
  76.8 8.1 all-gather.4
  84.9 12.1 %all-gather.1 = bf16[32,64,12]{1,0,2:T(8,128)(2,1)S(1)} all-gather(bf16[8,64,12]{1,0,2:T(8,128)(2,1)S(1)} %copy.231), channel_id=3, replica_groups=mesh['dp'=8,'shard'=4] {'shard'}, dimensions={0}, use_global_device_ids=true | all-gather | bytes 61440 | tf_op jit(solution)/shard_map/all_gather | solution.py:383
  97.3 75.6 %gather_rows.1 = (bf16[8,256,2048]{2,1,0:T(8,128)(2,1)}, bf16[8,256,2048]{2,1,0:T(8,128)(2,1)}) custom-call(bf16[256,2048]{1,0:T(8,128)(2,1)} %tok.3, bf16[256,2048]{1,0:T(8,128)(2,1)} %cot.1), custom_call_target="tpu_custom_call" | custom-call | bytes 225000000 | tf_op jit(solution)/shard_map/gather_rows/pallas_call | solution.py:304
  172.9 4.8 convert_reduce_fusion
  183.7 8.6 fusion.4
  198.9 7.0 fusion.42
  216.0 5.0 fusion.57
  228.5 88.1 %attention_output.1 = (f32[256,2048]{1,0:T(8,128)}, bf16[8,256,2048]{2,1,0:T(8,128)(2,1)}) custom-call(bf16[2048,256]{1,0:T(8,128)(2,1)} %bitcast.261, bf16[2048,256]{1,0:T(8,128)(2,1)} %slice.139.w_out, bf16[256,2048]{1,0:T(8,128)(2,1)} %tok.3, f32[16,2048]{1,0:T(8,128)} %pad.4.vec), custom_call_target="tpu_custom_call" | custom-call | bytes 285000000 | tf_op jit(solution)/shard_map/attention_output/pallas_call | solution.py:304
  316.6 8.3 copy.239
  324.9 16.0 %multiply_convert_fusion = (bf16[2048,1024]{1,0:T(8,128)(2,1)S(1)}, f32[2048,1024]{1,0:T(8,128)}) fusion(f32[1024]{0:T(1024)S(1)} %dynamic_slice.11, bf16[2048,2048]{1,0:T(8,128)(2,1)} %bitcast.300, bf16[2048,2048]{1,0:T(8,128)(2,1)} %bitcast.230), kind=kOutput, calls=%fused_computation.18 | convolution fusion | flops 8610906112 | bytes 25169920 | tf_op jit(solution)/shard_map/td,dn->tn/dot_general | solution.py:319
  340.9 14.2 %convolution_convert_fusion = bf16[2048,1024]{0,1:T(8,128)(2,1)} fusion(bf16[2048,2048]{1,0:T(8,128)(2,1)} %bitcast.296, bf16[2048,1024]{1,0:T(8,128)(2,1)S(1)} %get-tuple-element.64.activated), kind=kOutput, calls=%fused_computation.35 | convolution fusion | flops 8592031744 | bytes 16777216 | tf_op jit(solution)/shard_map/td,tn->dn/dot_general | solution.py:319
  355.1 6.2 copy.256
  361.3 20.2 %convert_reduce_fusion.1 = (f32[1024]{0:T(1024)S(1)}, bf16[2048,1024]{1,0:T(8,128)(2,1)S(1)}) fusion(f32[2048,1024]{1,0:T(8,128)} %get-tuple-element.65, f32[1024]{0:T(1024)S(1)} %dynamic_slice.11, bf16[2048,2048]{1,0:T(8,128)(2,1)} %bitcast.297, bf16[2048,2048]{1,0:T(8,128)(2,1)} %bitcast.231), kind=kOutput, calls=%fused_computation.17 | convolution fusion | flops 8638168064 | bytes 25174016 | tf_op jit(solution)/shard_map/td,dn->tn/dot_general | solution.py:319
  381.5 14.3 %convolution_convert_fusion.1 = bf16[2048,1024]{0,1:T(8,128)(2,1)} fusion(bf16[2048,2048]{1,0:T(8,128)(2,1)} %bitcast.301, bf16[2048,1024]{1,0:T(8,128)(2,1)S(1)} %get-tuple-element.67.grad_before), kind=kOutput, calls=%fused_computation.36 | convolution fusion | flops 8592031744 | bytes 16777216 | tf_op jit(solution)/shard_map/td,tn->dn/dot_general | solution.py:319
  395.9 6.2 copy.255
  402.1 6.3 fusion.52
  408.5 95.6 %second_norm_backward.1 = (f32[256,2048]{1,0:T(8,128)}, f32[4,8,2048]{2,1,0:T(8,128)}, bf16[8,256,2048]{2,1,0:T(8,128)(2,1)}) custom-call(bf16[2048,1024]{1,0:T(8,128)(2,1)} %copy-done.12, bf16[2048,1024]{1,0:T(8,128)(2,1)} %get-tuple-element.37.w_up, f32[256,2048]{1,0:T(8,128)} %get-tuple-element.21.middle, bf16[256,2048]{1,0:T(8,128)(2,1)} %cot.1, ...), custom_call_target="tpu_custom_call" | custom-call | bytes 285000000 | tf_op jit(solution)/shard_map/second_norm_backward/pallas_call | solution.py:304
  504.1 7.1 convolution_convert_fusion.4
  528.5 4.3 convert_reduce_fusion.2
  532.8 4.1 copy.253
  538.9 6.9 convolution_convert_fusion.3
  545.9 7.5 convolution_convert_fusion.2
  555.7 6.2 copy.254
  562.0 78.7 %reduce-scatter.4.cloned.1.call-done = bf16[1,2048,256]{2,1,0:T(8,128)(2,1)} async-done(((bf16[4,2048,256]{2,1,0:T(8,128)(2,1)}), bf16[1,2048,256]{2,1,0:T(8,128)(2,1)}) %reduce-scatter.4.cloned.1.call-update) | async-done | bytes 1048592 | tf_op jit(solution)/shard_map/reduce_scatter | solution.py:493
  642.7 74.6 %all_to_all.37 = bf16[32,64,768]{2,1,0:T(8,128)(2,1)S(1)} all-to-all(bf16[32,64,768]{2,1,0:T(8,128)(2,1)S(1)} %pad_maximum_fusion.1), channel_id=1, replica_groups=mesh['dp'=8,'shard'=4] {'dp','shard'}, dimensions={0} | all-to-all | bytes 6291456 | tf_op jit(solution)/shard_map/all_to_all | solution.py:501
  725.5 10.5 multiply_add_fusion
  748.9 6.3 all-to-all-start.3
  759.4 118.7 %first_norm_backward.1 = (f32[256,2048]{1,0:T(8,128)}, f32[2,8,2048]{2,1,0:T(8,128)}, bf16[256,2048]{1,0:T(8,128)(2,1)}) custom-call(bf16[2048,768]{1,0:T(8,128)(2,1)} %copy-done.4, bf16[2048,768]{1,0:T(8,128)(2,1)} %slice.131.w_qkv, bf16[2048,1024]{1,0:T(8,128)(2,1)} %copy-done.6, bf16[2048,1024]{1,0:T(8,128)(2,1)} %get-tuple-element.36.w_down, ...), custom_call_target="tpu_custom_call" | custom-call | bytes 255000000 | tf_op jit(solution)/shard_map/first_norm_backward/pallas_call | solution.py:304
  887.6 5.0 maximum_convert_fusion.1
  892.6 8.4 copy.268
  901.0 9.3 reshape.317
  910.4 7.4 all-to-all-start.5
  917.8 6.7 multiply_reduce_fusion.1
  924.5 8.5 mul.252
  933.0 8.2 copy.267
  941.4 10.4 fusion.33
  952.2 6.6 bitcast_add_fusion.4
  962.4 3.9 bitcast_add_fusion.3
  969.9 4.1 bitcast_add_fusion.2
  985.1 4.1 fusion.12
  989.2 4.7 copy.284
  993.9 7.7 convert_element_type.174
  1001.6 5.8 all-to-all-start.4
  1009.2 66.0 %all-to-all-done.4 = bf16[32,64,768]{2,1,0:T(8,128)(2,1)S(1)} async-done(((bf16[32,64,768]{2,1,0:T(8,128)(2,1)}), bf16[32,64,768]{2,1,0:T(8,128)(2,1)S(1)}, u32[]{:S(2)}, u32[]{:S(2)}) %all-to-all-start.4) | async-done | bytes 3145760 | tf_op jit(solution)/shard_map/all_to_all | solution.py:501
  1084.4 5.5 multiply_subtract_fusion
  (181 shorter events, 131.1 us)
Async XLA Ops:
  7.2 185.2 %all-gather.9.cloned.1.call-start = ((), (), s32[]{:S(2)}) async-start(), calls=%async_computation.12 | async-start | bytes 5242880 | tf_op jit(solution)/shard_map/all_gather | solution.py:378
  33.8 282.9 %all-gather.11.cloned.1.call-start = ((), (), s32[]{:S(2)}) async-start(), calls=%async_computation.13 | async-start | bytes 10485760 | tf_op jit(solution)/shard_map/all_gather | solution.py:378
  34.3 33.3 %copy-start.22 = (s32[1,4]{1,0:T(1,128)S(1)}, s32[1,4]{1,0:T(1,128)}, u32[]{:S(2)}) copy-start(s32[1,4]{1,0:T(1,128)} %param.9) | copy-start | bytes 52
  34.4 42.4 %copy-start.18 = (f32[64,12]{0,1:T(8,128)S(1)}, f32[64,12]{0,1:T(8,128)}, u32[]{:S(2)}) copy-start(f32[64,12]{0,1:T(8,128)} %param.12) | copy-start | bytes 9220
  67.6 494.4 %reduce-scatter.8.cloned.1.call-start = ((), (), s32[]{:S(2)}) async-start(), calls=%async_computation.11 | async-start | bytes 5242880 | tf_op jit(solution)/shard_map/reduce_scatter | solution.py:493
  172.9 5.9 copy-start
  192.3 6.5 copy-start.2
  195.2 10.7 copy-start.1
  205.9 2.7 copy-start.5
  214.3 10.5 copy-start.10
  216.0 5.0 copy-start.15
  227.2 97.7 %copy-start.8 = (bf16[8,256,2,128]{3,2,1,0:T(2,128)(2,1)}, bf16[8,256,2,128]{3,2,1,0:T(2,128)(2,1)S(1)}, u32[]{:S(2)}) copy-start(bf16[8,256,2,128]{3,2,1,0:T(2,128)(2,1)S(1)} %copy.242) | copy-start | bytes 3145732
  340.9 14.2 %copy-start.6 = (bf16[2048,1024]{1,0:T(8,128)(2,1)}, bf16[2048,1024]{1,0:T(8,128)(2,1)S(1)}, u32[]{:S(2)}) copy-start(bf16[2048,1024]{1,0:T(8,128)(2,1)S(1)} %get-tuple-element.64.activated) | copy-start | bytes 12582916
  361.3 200.7 %reduce-scatter.6.cloned.1.call-start = ((), (), s32[]{:S(2)}) async-start(), calls=%async_computation.10 | async-start | bytes 5242880 | tf_op jit(solution)/shard_map/reduce_scatter | solution.py:493
  381.5 14.3 %copy-start.12 = (bf16[2048,1024]{1,0:T(8,128)(2,1)}, bf16[2048,1024]{1,0:T(8,128)(2,1)S(1)}, u32[]{:S(2)}) copy-start(bf16[2048,1024]{1,0:T(8,128)(2,1)S(1)} %get-tuple-element.67.grad_before) | copy-start | bytes 12582916
  402.1 238.6 %reduce-scatter.4.cloned.1.call-start = ((), (), s32[]{:S(2)}) async-start(), calls=%async_computation.9 | async-start | bytes 5242880 | tf_op jit(solution)/shard_map/reduce_scatter | solution.py:493
  504.1 10.4 copy-start.16
  514.5 3.7 copy-start.7
  532.8 6.1 copy-start.9
  537.0 8.9 slice-start
  538.9 7.0 copy-start.4
  538.9 7.0 slice-start.1
  748.9 10.4 copy-start.17
  748.9 161.4 %all-to-all-start.3 = ((bf16[32,64,768]{2,1,0:T(8,128)(2,1)}), bf16[32,64,768]{2,1,0:T(8,128)(2,1)S(1)}, u32[]{:S(2)}, u32[]{:S(2)}) async-start(bf16[32,64,768]{2,1,0:T(8,128)(2,1)} %bitcast.53), calls=%async_computation.6 | async-start | bytes 6291456 | tf_op jit(solution)/shard_map/all_to_all | solution.py:410
  910.4 91.3 %all-to-all-start.5 = ((f32[32,1,768]{2,1,0:T(1,128)}), f32[32,1,768]{2,1,0:T(1,128)}, u32[]{:S(2)}, u32[]{:S(2)}) async-start(f32[32,1,768]{2,1,0:T(1,128)} %all_to_all.28), calls=%async_computation.8 | async-start | bytes 196608 | tf_op jit(solution)/shard_map/all_to_all | solution.py:542
  941.4 10.8 copy-start.3
  993.9 14.6 %copy-start.19 = (f32[64,12]{0,1:T(8,128)S(1)}, f32[64,12]{0,1:T(8,128)}, u32[]{:S(2)}) copy-start(f32[64,12]{0,1:T(8,128)} %param.12) | copy-start | bytes 9220
  993.9 14.6 %copy-start.20 = (f32[64,12]{0,1:T(8,128)S(1)}, f32[64,12]{0,1:T(8,128)}, u32[]{:S(2)}) copy-start(f32[64,12]{0,1:T(8,128)} %param.14) | copy-start | bytes 9220
  993.9 14.6 %copy-start.21 = (f32[64,12]{0,1:T(8,128)S(1)}, f32[64,12]{0,1:T(8,128)}, u32[]{:S(2)}) copy-start(f32[64,12]{0,1:T(8,128)} %param.13) | copy-start | bytes 9220
  1001.6 73.5 %all-to-all-start.4 = ((bf16[32,64,768]{2,1,0:T(8,128)(2,1)}), bf16[32,64,768]{2,1,0:T(8,128)(2,1)S(1)}, u32[]{:S(2)}, u32[]{:S(2)}) async-start(bf16[32,64,768]{2,1,0:T(8,128)(2,1)} %convert_element_type.174), calls=%async_computation.7 | async-start | bytes 6291456 | tf_op jit(solution)/shard_map/all_to_all | solution.py:501
  1076.9 6.1 copy-start.11
  1084.4 5.5 copy-start.14
  1084.4 6.5 copy-start.13
Sparse Core Ops, SparseCore 0:
  33.9 79.9 all-gather.8
  115.4 147.8 all-gather.10
  361.4 77.2 reduce-scatter.7
  441.0 77.2 reduce-scatter.5
  562.1 78.5 reduce-scatter.3

commit v3 on v2

v3 whole, which is shorter than its diff:
```python
from functools import partial
import math

import jax
import jax.numpy as jnp
from jax import lax
from jax.experimental import pallas as pl
from jax.experimental.pallas import tpu as pltpu
from jax.sharding import Mesh, PartitionSpec as P

HEADS = 16
HEAD = 128
NS_ITERS = 5
STEP = 10

COEF_A = 3.4445
COEF_B = -4.775
COEF_C = 2.0315
BF = jnp.bfloat16
F32 = jnp.float32
ALL = ("hi", "tp", "shard")
FS = ("hi", "shard")


MESH = pl.DeviceIdType.MESH
WIDE = 256


def rem(a, b):
    return lax.rem(a, jnp.int32(b))


def div(a, b):
    return lax.div(a, jnp.int32(b))


def spots():
    me = lax.axis_index("tp")
    c, x, y = rem(me, 2), rem(div(me, 2), 2), div(me, 4)
    return me, c, x, y, me + 1 - 2 * c, me + 2 - 4 * x, me + 4 - 8 * y


def meet(peers):
    barrier = pltpu.get_barrier_semaphore()
    for peer in peers:
        pl.semaphore_signal(barrier, inc=1, device_id={"tp": peer}, device_id_type=MESH)
    pl.semaphore_wait(barrier, len(peers))


def remote(src, dst, send, recv, peer):
    return pltpu.make_async_remote_copy(
        src_ref=src, dst_ref=dst, send_sem=send, recv_sem=recv, device_id={"tp": peer}, device_id_type=MESH
    )


def sum_scratch(rows, width):
    count = width // WIDE
    return [
        pltpu.VMEM((count, 2, 2, 2, rows, WIDE), BF),
        pltpu.VMEM((count, 2, 2, rows, WIDE), BF),
        pltpu.VMEM((count, 2, rows, WIDE), BF),
        pltpu.VMEM((count, rows, WIDE), BF),
        pltpu.SemaphoreType.DMA((3, count)),
        pltpu.SemaphoreType.DMA((3, count)),
    ]


class Summing:
    def __init__(self, left, right, total, scratch):
        self.left, self.right, self.total = left, right, total
        self.part, self.from_c, self.from_1, self.from_2, self.send, self.recv = scratch
        self.count = self.part.shape[0]
        self.rows = self.part.shape[4]
        self.copies = {}

    def fill(self, k):
        right = self.right[k * WIDE : (k + 1) * WIDE, :]

        def one(dest, carry):
            rows = self.left[pl.ds(pl.multiple_of(dest * self.rows, self.rows), self.rows), :]
            made = lax.dot_general(rows, right, (((1,), (1,)), ((), ())), preferred_element_type=F32)
            self.part[k, div(dest, 4), rem(div(dest, 2), 2), rem(dest, 2)] = made.astype(BF)
            return carry

        lax.fori_loop(0, 8, one, 0)

    def begin(self, stage, k, src, dst, peer):
        copy = remote(src, dst, self.send.at[stage, k], self.recv.at[stage, k], peer)
        copy.start()
        self.copies[stage, k] = copy

    def run(self):
        me, c, x, y, pc, px, py = spots()
        oc, ox, oy = 1 - c, 1 - x, 1 - y
        part = self.part

        def core_stage(k):
            self.copies[0, k].wait_recv()
            for i in range(4):
                a, b = i // 2, i % 2
                part[k, a, b, c] = (part[k, a, b, c].astype(F32) + self.from_c[k, a, b].astype(F32)).astype(BF)
            if k % 2 == 0:
                self.begin(1, k, part.at[k, :, ox, c], self.from_1.at[k], px)
            else:
                self.begin(1, k, part.at[k, oy, :, c], self.from_1.at[k], py)

        for k in range(self.count):
            self.fill(k)
            self.begin(0, k, part.at[k, :, :, oc], self.from_c.at[k], pc)
            if k:
                core_stage(k - 1)
        core_stage(self.count - 1)
        for k in range(self.count):
            self.copies[1, k].wait_recv()
            for i in range(2):
                if k % 2 == 0:
                    part[k, i, x, c] = (part[k, i, x, c].astype(F32) + self.from_1[k, i].astype(F32)).astype(BF)
                else:
                    part[k, y, i, c] = (part[k, y, i, c].astype(F32) + self.from_1[k, i].astype(F32)).astype(BF)
            if k % 2 == 0:
                self.begin(2, k, part.at[k, oy, x, c], self.from_2.at[k], py)
            else:
                self.begin(2, k, part.at[k, y, ox, c], self.from_2.at[k], px)
        for k in range(self.count):
            self.copies[2, k].wait_recv()
            self.total[:, k * WIDE : (k + 1) * WIDE] = part[k, y, x, c].astype(F32) + self.from_2[k].astype(F32)

    def end(self):
        for copy in self.copies.values():
            copy.wait_send()


class Gathering:
    def __init__(self, own, out, send, recv, local):
        self.own, self.out, self.send, self.recv, self.local = own, out, send, recv, local
        self.copies = []

    def begin(self, src, dst, peer):
        n = len(self.copies)
        copy = remote(src, dst, self.send.at[n], self.recv.at[n], peer)
        copy.start()
        self.copies.append(copy)
        return copy

    def start(self):
        me, c, x, y, pc, px, py = spots()
        self.spots = me, px, py, pc
        own, out = self.own, self.out
        half = own.shape[-1] // 2
        self.low, self.high = pl.ds(0, half), pl.ds(half, half)
        low, high = self.low, self.high
        self.px_high = self.begin(own.at[:, high], out.at[me, :, high], px)
        self.py_low = self.begin(own.at[:, low], out.at[me, :, low], py)
        self.begin(own, out.at[me], pc)
        self.px_low = self.begin(own.at[:, low], out.at[me, :, low], px)
        self.py_high = self.begin(own.at[:, high], out.at[me, :, high], py)
        self.kept = pltpu.make_async_copy(own, out.at[me], self.local)
        self.kept.start()

    def forward(self):
        me, px, py, pc = self.spots
        out, low, high = self.out, self.low, self.high
        across = px + py - me
        self.px_high.wait_recv()
        a = self.begin(out.at[px, :, high], out.at[px, :, high], py)
        self.begin(out.at[px, :, high], out.at[px, :, high], pc)
        self.py_low.wait_recv()
        b = self.begin(out.at[py, :, low], out.at[py, :, low], px)
        self.begin(out.at[py, :, low], out.at[py, :, low], pc)
        self.px_low.wait_recv()
        self.begin(out.at[px, :, low], out.at[px, :, low], pc)
        self.py_high.wait_recv()
        self.begin(out.at[py, :, high], out.at[py, :, high], pc)
        a.wait_recv()
        self.begin(out.at[across, :, high], out.at[across, :, high], pc)
        b.wait_recv()
        self.begin(out.at[across, :, low], out.at[across, :, low], pc)
        self.seen = (0, 1, 3, 4, 5, 7)

    def end(self):
        for n, copy in enumerate(self.copies):
            if n not in self.seen:
                copy.wait_recv()
            copy.wait_send()
        self.kept.wait()


def gather_scratch():
    return [pltpu.SemaphoreType.DMA((13,)), pltpu.SemaphoreType.DMA((13,)), pltpu.SemaphoreType.DMA]


def row_loop(rows, body):
    def one(i, carry):
        body(pl.ds(pl.multiple_of(i * 16, 16), 16))
        return carry

    lax.fori_loop(0, rows // 16, one, 0)


def normalized(values):
    average = jnp.mean(values, axis=-1, keepdims=True)
    centered = values - average
    variance = jnp.mean(centered * centered, axis=-1, keepdims=True)
    scale = lax.rsqrt(variance + 1e-05)
    return centered * scale, scale


def norm_back(values, grad, gain):
    unit, scale = normalized(values)
    weighted = grad * gain
    mean_one = jnp.mean(weighted, axis=-1, keepdims=True)
    mean_two = jnp.mean(weighted * unit, axis=-1, keepdims=True)
    return scale * (weighted - mean_one - unit * mean_two), grad * unit


def fetch_rows(w, first, held, sem, hi, sh):
    rows, width = w.shape[2], held.shape[1]

    def one(f, carry):
        s, t, h = rem(f, sh), rem(div(f, sh), 8), div(f, 8 * sh)
        pltpu.make_async_copy(
            w.at[h * sh + s, t, :, pl.ds(first, width)], held.at[pl.ds(pl.multiple_of(f * rows, rows), rows)], sem
        ).start()
        return carry

    lax.fori_loop(0, 8 * hi * sh, one, 0)


def fetched(held, sem):
    pltpu.make_async_copy(held, held, sem).wait()


def first_kernel(hi, sh, tok, piece, cot, normed_all, vec, lengths, own, pieces, send_p, recv_p, send_q, recv_q, *sems):
    me, c, x, y, pc, px, py = spots()
    groups = hi * sh
    mine = lax.axis_index("hi") * sh + lax.axis_index("shard")
    barrier = pltpu.get_barrier_semaphore()
    across, around = [], []
    for i in range(1, groups):
        there = rem(mine + i, groups)
        across.append({"hi": div(there, sh), "shard": rem(there, sh)})
    for i in range(1, 8):
        around.append({"tp": rem(me + i, 8)})
    for peer in across + around:
        pl.semaphore_signal(barrier, inc=1, device_id=peer, device_id_type=MESH)
    pl.semaphore_wait(barrier, groups + 6)

    pieces[mine, me] = piece[...]
    spot = pieces.at[mine, me]
    first = [
        pltpu.make_async_remote_copy(
            src_ref=spot, dst_ref=spot, send_sem=send_p.at[i], recv_sem=recv_p.at[i], device_id=peer, device_id_type=MESH
        )
        for i, peer in enumerate(across)
    ]
    for copy in first:
        copy.start()
    for copy in first:
        copy.wait_recv()
    column = pieces.at[:, me]
    second = [
        pltpu.make_async_remote_copy(
            src_ref=column, dst_ref=column, send_sem=send_q.at[i], recv_sem=recv_q.at[i], device_id=peer, device_id_type=MESH
        )
        for i, peer in enumerate(around)
    ]
    for copy in second:
        copy.start()
    for copy in second:
        copy.wait_recv()
    width = tok.shape[1]
    parts = 8 * groups * 128 // width
    for q in range(width // 128):
        found = None
        for f in range(q * parts, (q + 1) * parts):
            value = pieces[f // (8 * sh) * sh + f % sh, f // sh % 8].astype(F32)
            found = value if found is None else found + value
        vec[:, q * 128 : (q + 1) * 128] = found
    for t in range(8):
        lengths[t : t + 1, :] = pieces[mine, t].astype(F32)[12:13, :]

    def body(at):
        unit, _ = normalized(tok[at, :].astype(F32))
        own[at, :] = (unit * vec[0:1, :] + vec[1:2, :]).astype(BF)

    row_loop(own.shape[0], body)
    spread = Gathering(own, normed_all, *sems)
    spread.start()
    spread.forward()
    spread.end()
    for copy in first + second:
        copy.wait_send()


def allowed_of(lengths, row, size):
    line = lengths[pl.ds(row, 1), :]
    ends = [line[:, 0:1]]
    for n in range(1, 3):
        ends.append(ends[-1] + line[:, n : n + 1])
    down = lax.broadcasted_iota(jnp.int32, (size, 1), 0)
    along = lax.broadcasted_iota(jnp.int32, (1, size), 1)

    def span(places):
        places = places.astype(F32)
        return sum(jnp.where(places >= end, 1.0, 0.0) for end in ends)

    span_down, span_along = span(down), span(along)
    tail = jnp.where(span_down == 3.0, down, 0)
    return (span_down == span_along) & (along <= down) & (along >= tail)


def probabilities(query, key, allowed):
    scores = lax.dot_general(query, key, (((1,), (1,)), ((), ())), preferred_element_type=F32) * HEAD ** (-0.5)
    scores = jnp.where(allowed, scores, -1e30)
    exponent = jnp.exp(scores - jnp.max(scores, axis=-1, keepdims=True))
    return exponent / jnp.sum(exponent, axis=-1, keepdims=True)


def attention_kernel(
    hi, sh, normed, w_any, lengths, vec, tok, cot, middle, normed_all, cot_all, qkv, att, total, own, w, w_sem, *scratch
):
    me, c, x, y, pc, px, py = spots()
    fetch_rows(w_any, 0, w, w_sem, hi, sh)
    meet((pc, px, py))
    spread_cot = Gathering(cot, cot_all, *scratch[9:])
    spread_cot.start()
    size = own.shape[0]
    hc = att.shape[1]
    fetched(w, w_sem)

    def one_row(r, carry):
        joined = jnp.dot(normed[r], w[:, : 3 * hc], preferred_element_type=F32)
        here = pl.ds(pl.multiple_of(me * hc, 128), hc)
        queries = (joined[:, :hc] + vec[4:5, here]).astype(BF)
        keys = joined[:, hc : 2 * hc].astype(BF)
        values = (joined[:, 2 * hc :] + vec[5:6, here]).astype(BF)
        qkv[r, :, :hc] = queries
        qkv[r, :, hc : 2 * hc] = keys
        qkv[r, :, 2 * hc :] = values
        allowed = allowed_of(lengths, r, size)
        rows = pl.ds(pl.multiple_of(r * size, size), size)
        for h in range(hc // HEAD):
            at = slice(h * HEAD, (h + 1) * HEAD)
            low = probabilities(queries[:, at], keys[:, at], allowed).astype(BF)
            att[rows, at] = jnp.dot(low, values[:, at], preferred_element_type=F32).astype(BF)
        return carry

    lax.fori_loop(0, 8, one_row, 0)
    sums = Summing(att, w.at[:, 3 * hc :], total, scratch[:6])
    spread_cot.forward()
    sums.run()

    def body(at):
        values = tok[at, :].astype(F32) + total[at, :] + vec[6:7, :]
        middle[at, :] = values
        unit, _ = normalized(values)
        own[at, :] = (unit * vec[2:3, :] + vec[3:4, :]).astype(BF)

    row_loop(own.shape[0], body)
    spread = Gathering(own, normed_all, *scratch[6:9])
    spread.start()
    spread.forward()
    sums.end()
    spread_cot.end()
    spread.end()


GELU_A = math.sqrt(2.0 / math.pi)


def mlp_kernel(hi, sh, normed, cot, w_any, vec, activated, grad_before, w_up, w_down, sems):
    width = w_up.shape[1]

    @pl.when(pl.program_id(0) == 0)
    def _():
        fetch_rows(w_any, 0, w_up, sems.at[0], hi, sh)
        fetch_rows(w_any, width, w_down, sems.at[1], hi, sh)
        fetched(w_up, sems.at[0])
        fetched(w_down, sems.at[1])

    me = lax.axis_index("tp")
    each = vec.shape[1] // width
    for j in range(width // 256):
        at = slice(j * 256, (j + 1) * 256)
        bias = vec[pl.ds(8 + div(me, each), 1), pl.ds(pl.multiple_of(rem(me, each) * width + j * 256, 256), 256)]
        before = jnp.dot(normed[0], w_up[:, at], preferred_element_type=F32) + bias
        grad = jnp.dot(cot[0], w_down[:, at], preferred_element_type=F32)
        square = before * before
        slope = jnp.tanh(before * (GELU_A + GELU_A * 0.044715 * square))
        half = 0.5 * (1.0 + slope)
        activated[:, at] = (before * half).astype(BF)
        inner = GELU_A + 3.0 * GELU_A * 0.044715 * square
        grad_before[:, at] = (grad * (half + 0.5 * before * (1.0 - slope * slope) * inner)).astype(BF)


def attention_back_kernel(hi, sh, branch, w_any, qkv, lengths, grad_joined, w, sem):
    hc = w.shape[1]
    size = branch.shape[1]
    r = pl.program_id(0)

    @pl.when(r == 0)
    def _():
        fetch_rows(w_any, 3 * hc, w, sem, hi, sh)
        fetched(w, sem)

    grad_att = jnp.dot(branch[0], w[...], preferred_element_type=F32).astype(BF)
    allowed = allowed_of(lengths, r, size)
    scale = HEAD ** (-0.5)
    for h in range(hc // HEAD):
        at = slice(h * HEAD, (h + 1) * HEAD)
        query, key, value = (qkv[0, :, n * hc + h * HEAD : n * hc + (h + 1) * HEAD] for n in range(3))
        probability = probabilities(query, key, allowed)
        low = probability.astype(BF)
        grad = grad_att[:, at]
        grad_prob = lax.dot_general(grad, value, (((1,), (1,)), ((), ())), preferred_element_type=F32)
        row_total = jnp.sum(probability * grad_prob, axis=-1, keepdims=True)
        grad_scores = (probability * (grad_prob - row_total)).astype(BF)
        made = (
            jnp.dot(grad_scores, key, preferred_element_type=F32) * scale,
            lax.dot_general(grad_scores, query, (((0,), (0,)), ((), ())), preferred_element_type=F32) * scale,
            lax.dot_general(low, grad, (((0,), (0,)), ((), ())), preferred_element_type=F32),
        )
        for n in range(3):
            grad_joined[:, n * hc + h * HEAD : n * hc + (h + 1) * HEAD] = made[n].astype(BF)


def branch_kernel(
    hi, sh, grad_before, w_any, middle, cot, vec, grad_middle, sums_out, branch_all, total, own, w_up, w_sem, *scratch
):
    me, c, x, y, pc, px, py = spots()
    fetch_rows(w_any, 0, w_up, w_sem, hi, sh)
    meet((pc, px, py))
    fetched(w_up, w_sem)
    sums = Summing(grad_before, w_up, total, scratch[:6])
    sums.run()
    sums_out[...] = jnp.zeros_like(sums_out)

    def body(at):
        grad = total[at, :]
        part, for_gain = norm_back(middle[at, :], grad, vec[2:3, :])
        back = cot[at, :].astype(F32)
        whole = back + part
        grad_middle[at, :] = whole
        low = whole.astype(BF)
        own[at, :] = low
        low = low.astype(F32)
        for n, values in enumerate((for_gain, grad, low, back)):
            sums_out[n] += values[:8] + values[8:]

    row_loop(own.shape[0], body)
    spread = Gathering(own, branch_all, *scratch[6:])
    spread.start()
    spread.forward()
    sums.end()
    spread.end()


def last_kernel(
    hi, sh, grad_joined, w_attn, activated, w_mlp, tok, middle, grad_middle, vec, grad_tokens, sums_out, output, total,
    w_qkv, w_down, w_sems, *scratch
):
    me, c, x, y, pc, px, py = spots()
    fetch_rows(w_attn, 0, w_qkv, w_sems.at[0], hi, sh)
    fetch_rows(w_mlp, w_down.shape[1], w_down, w_sems.at[1], hi, sh)
    meet((pc, px, py))
    fetched(w_qkv, w_sems.at[0])
    fetched(w_down, w_sems.at[1])
    sums = Summing(grad_joined, w_qkv, total, scratch[:6])
    sums.run()
    sums_out[...] = jnp.zeros_like(sums_out)

    def body(at):
        grad = total[at, :]
        part, for_gain = norm_back(tok[at, :].astype(F32), grad, vec[0:1, :])
        grad_tokens[at, :] = grad_middle[at, :] + part
        for n, values in enumerate((for_gain, grad)):
            sums_out[n] += values[:8] + values[8:]

    row_loop(total.shape[0], body)
    more = Summing(activated, w_down, total, scratch[6:])
    more.run()

    def body_two(at):
        output[at, :] = (middle[at, :] + total[at, :] + vec[7:8, :]).astype(BF)

    row_loop(total.shape[0], body_two)
    sums.end()
    more.end()


def call(body, ins, outs, scratch, number, microseconds, name, grid=None):
    def spec(how):
        if how is True:
            return pl.BlockSpec(memory_space=pl.ANY)
        return pl.BlockSpec(memory_space=pltpu.VMEM) if how is False else pl.BlockSpec(*how)

    remote_params = {} if number is None else {"collective_id": number, "has_side_effects": True}
    return pl.pallas_call(
        body,
        out_shape=[s for s, _ in outs],
        in_specs=[spec(how) for _, how in ins],
        out_specs=[spec(how) for _, how in outs],
        scratch_shapes=scratch,
        compiler_params=pltpu.CompilerParams(vmem_limit_bytes=60 * 2**20, **remote_params),
        cost_estimate=pl.CostEstimate(flops=0, transcendentals=0, bytes_accessed=int(microseconds * 3.0e6)),
        name=name,
        **({} if grid is None else {"grid": grid}),
    )(*[a for a, _ in ins])


PAIR = 2 * HEAD


def ortho_kernel(hi, sh, mom, grad, out, gram, arrived, power, send_a, recv_a, send_b, recv_b):
    groups = hi * sh
    mine = lax.axis_index("hi") * sh + lax.axis_index("shard")
    count = out.shape[1] // PAIR
    per = gram.shape[0] // groups

    def peer(i):
        there = rem(mine + i, groups)
        return there, {"hi": div(there, sh), "shard": rem(there, sh)}

    barrier = pltpu.get_barrier_semaphore()
    for i in range(1, groups):
        pl.semaphore_signal(barrier, inc=1, device_id=peer(i)[1], device_id_type=MESH)
    pl.semaphore_wait(barrier, groups - 1)

    rows = lax.broadcasted_iota(jnp.int32, (PAIR, PAIR), 0)
    columns = lax.broadcasted_iota(jnp.int32, (PAIR, PAIR), 1)
    unit = jnp.where(rows == columns, 1.0, 0.0)
    one, two = slice(0, HEAD), slice(HEAD, PAIR)

    def block(k):
        at = pl.ds(pl.multiple_of(k * PAIR, PAIR), PAIR)
        return (0.95 * mom[:, at].astype(F32) + grad[:, at].astype(F32)).astype(BF), at

    def one_gram(k, carry):
        values, _ = block(k)
        made = lax.dot_general(values, values, (((0,), (0,)), ((), ())), preferred_element_type=F32)
        gram[k, 0] = made[one, one].astype(BF)
        gram[k, 1] = made[two, two].astype(BF)
        return carry

    lax.fori_loop(0, count, one_gram, 0)
    for k in range(count, gram.shape[0]):
        gram[k] = jnp.zeros((2, HEAD, HEAD), BF)

    def copies(i, src, dst, send, recv):
        return pltpu.make_async_remote_copy(
            src_ref=src, dst_ref=dst, send_sem=send.at[i - 1], recv_sem=recv.at[i - 1],
            device_id=peer(i)[1], device_id_type=MESH,
        )

    first = [copies(i, gram.at[pl.ds(peer(i)[0] * per, per)], arrived.at[i - 1], send_a, recv_a) for i in range(1, groups)]
    for copy in first:
        copy.start()
    for copy in first:
        copy.wait_recv()

    def product(a, b):
        a_high, b_high = a.astype(BF), b.astype(BF)
        a_low, b_low = (a - a_high.astype(F32)).astype(BF), (b - b_high.astype(F32)).astype(BF)
        made = jnp.dot(a_high, b_low, preferred_element_type=F32) + jnp.dot(a_low, b_high, preferred_element_type=F32)
        return made + jnp.dot(a_high, b_high, preferred_element_type=F32)

    upper = (rows < HEAD) & (rows == columns)
    lower = (rows >= HEAD) & (rows == columns)
    grams, wholes = [], []
    for j in range(per):
        halves = []
        for n in range(2):
            half = gram[mine * per + j, n].astype(F32)
            for i in range(groups - 1):
                half = half + arrived[i, j, n].astype(F32)
            halves.append(half)
        empty = jnp.zeros((HEAD, HEAD), F32)
        total = jnp.concatenate(
            [jnp.concatenate([halves[0], empty], axis=1), jnp.concatenate([empty, halves[1]], axis=1)], axis=0
        )

        def scaling_of(chosen):
            trace = jnp.sum(jnp.sum(jnp.where(chosen, total, 0.0), axis=1, keepdims=True), axis=0, keepdims=True)
            return 1.0 / (jnp.sqrt(trace) + 1e-07)

        scaling = jnp.where(rows < HEAD, scaling_of(upper), scaling_of(lower))
        grams.append(total * (scaling * scaling))
        wholes.append(scaling)
    for number in range(NS_ITERS):
        squares = [product(a, a) for a in grams]
        steps = [COEF_A * unit + COEF_B * a + COEF_C * s for a, s in zip(grams, squares)]
        wholes = [product(w, p) for w, p in zip(wholes, steps)] if number else [w * p for w, p in zip(wholes, steps)]
        if number < NS_ITERS - 1:
            grams = [product(product(a, p), p) for a, p in zip(grams, steps)]
    for j in range(per):
        power[mine * per + j, 0] = wholes[j][one, one].astype(BF)
        power[mine * per + j, 1] = wholes[j][two, two].astype(BF)
    own = power.at[pl.ds(mine * per, per)]
    second = [copies(i, own, own, send_b, recv_b) for i in range(1, groups)]
    for copy in second:
        copy.start()
    for copy in second:
        copy.wait_recv()

    def finish(k, carry):
        values, at = block(k)
        made = [jnp.dot(values[:, side], power[k, n], preferred_element_type=F32) for n, side in enumerate((one, two))]
        out[:, at] = jnp.concatenate(made, axis=1).astype(BF)
        return carry

    lax.fori_loop(0, count, finish, 0)
    for copy in first + second:
        copy.wait_send()


def orthogonalize(mom, grad, hi, sh, number, name):
    groups = hi * sh
    count = mom.shape[1] // PAIR
    per = -(-count // groups)
    return call(
        partial(ortho_kernel, hi, sh),
        [(mom, False), (grad, False)],
        [(jax.ShapeDtypeStruct(mom.shape, BF), False)],
        [
            pltpu.VMEM((groups * per, 2, HEAD, HEAD), BF),
            pltpu.VMEM((groups - 1, per, 2, HEAD, HEAD), BF),
            pltpu.VMEM((groups * per, 2, HEAD, HEAD), BF),
        ]
        + [pltpu.SemaphoreType.DMA((groups - 1,))] * 4,
        number,
        25,
        name,
    )[0]


def dot(spec, a, b, **kw):
    return jnp.einsum(spec, a, b, preferred_element_type=F32, **kw)


def local(tokens, doc_lengths, weights, momentum, vectors, vector_moment, vector_second, cotangent):
    hi, tp, sh = (lax.axis_size(a) for a in ALL)
    groups, world = hi * sh, hi * tp * sh
    rows, blocks, head = weights.shape
    row_tokens, d = tokens.shape
    heads = HEADS // tp
    inner_all = (blocks - 4 * HEADS) // 2
    inner = inner_all // tp
    attn_blocks = 4 * heads
    me = lax.axis_index("tp")
    t_all = tp * row_tokens

    def arrange(array):
        attn = array[:, : 4 * HEADS].reshape(rows, 4, tp, heads, head).transpose(2, 0, 1, 3, 4).reshape(tp, rows, attn_blocks * head)
        mlp = array[:, 4 * HEADS :].reshape(rows, 2, tp, inner, head).transpose(2, 0, 1, 3, 4).reshape(tp, rows, 2 * inner * head)
        return attn, mlp

    def restore(attn, mlp):
        attn = attn.reshape(tp, rows, 4, heads, head).transpose(1, 2, 0, 3, 4).reshape(rows, 4 * HEADS, head)
        mlp = mlp.reshape(tp, rows, 2, inner, head).transpose(1, 2, 0, 3, 4).reshape(rows, 2 * inner_all, head)
        return jnp.concatenate([attn, mlp], axis=1)

    def swap(array):
        return lax.all_to_all(array, "tp", split_axis=0, concat_axis=0, tiled=True)

    attn_send, mlp_send = arrange(weights.astype(BF))

    def spread(array):
        return lax.all_gather(array, FS, axis=0, tiled=False)

    w_attn = spread(swap(attn_send))
    mlp_swapped, tokens = lax.optimization_barrier((swap(mlp_send), tokens))
    w_mlp = spread(mlp_swapped)

    flat = (lax.axis_index("hi") * tp + me) * sh + lax.axis_index("shard")
    lanes = 128 // rows
    spot = lax.broadcasted_iota(jnp.int32, (1, 128), 1) // rows == flat % lanes
    piece = jnp.where(spot, jnp.tile(vectors.T, (1, lanes)), 0.0)
    count = vectors.shape[1]
    spans = jnp.pad(doc_lengths.astype(F32), ((0, 15 - count), (0, 128 - doc_lengths.shape[1])))
    piece = jnp.concatenate([piece, spans], axis=0).astype(BF)

    gathered = jax.ShapeDtypeStruct((tp, row_tokens, d), BF)
    own_f32 = jax.ShapeDtypeStruct((row_tokens, d), F32)
    own_bf = jax.ShapeDtypeStruct((row_tokens, d), BF)
    own_scratch = [pltpu.VMEM(own_f32.shape, F32), pltpu.VMEM(own_f32.shape, BF)]
    small = [pltpu.SemaphoreType.DMA((groups,))] * 2 + [pltpu.SemaphoreType.DMA((8,))] * 2
    normed_one, vec_rows, lengths = call(
        partial(first_kernel, hi, sh),
        [(tokens, False), (piece, False), (cotangent, True)],
        [
            (gathered, True),
            (jax.ShapeDtypeStruct((16, d), F32), False),
            (jax.ShapeDtypeStruct((8, 128), F32), False),
        ],
        [own_scratch[1], pltpu.VMEM((groups, 8, 16, 128), BF)] + small + gather_scratch(),
        1,
        50,
        "first_norm",
    )

    hc = heads * head
    units = inner * head
    middle, normed_two, cot_all, qkv, attended = call(
        partial(attention_kernel, hi, sh),
        [(normed_one, False), (w_attn, True), (lengths, False), (vec_rows, False), (tokens, False), (cotangent, True)],
        [
            (own_f32, False),
            (gathered, True),
            (gathered, True),
            (jax.ShapeDtypeStruct((tp, row_tokens, 3 * hc), BF), False),
            (jax.ShapeDtypeStruct((t_all, hc), BF), False),
        ],
        own_scratch
        + [pltpu.VMEM((d, 4 * hc), BF), pltpu.SemaphoreType.DMA]
        + sum_scratch(row_tokens, d)
        + gather_scratch() * 2,
        2,
        110,
        "attention",
    )

    mom_attn, mom_mlp = [swap(part).reshape(tp * rows, -1) for part in arrange(momentum.astype(BF))]
    normed_two, mom_attn, mom_mlp = lax.optimization_barrier((normed_two, mom_attn, mom_mlp))

    def rows_of(width):
        return (row_tokens, width), lambda r: (r, 0)

    def row_of(width):
        return (1, row_tokens, width), lambda r: (r, 0, 0)

    def fixed(array):
        return array.shape, lambda r: (0,) * array.ndim

    activated, grad_before = call(
        partial(mlp_kernel, hi, sh),
        [(normed_two, row_of(d)), (cot_all, row_of(d)), (w_mlp, True), (vec_rows, fixed(vec_rows))],
        [(jax.ShapeDtypeStruct((t_all, units), BF), rows_of(units))] * 2,
        [pltpu.VMEM((d, units), BF)] * 2 + [pltpu.SemaphoreType.DMA((2,))],
        None,
        30,
        "hidden_units",
        grid=(tp,),
    )
    flat_one, flat_two, flat_cot = (a.reshape(t_all, d) for a in (normed_one, normed_two, cot_all))

    def summed(left_right):
        parts = [dot("td,tn->dn", a, b).astype(BF) for a, b in left_right]
        part = parts[0] if len(parts) == 1 else jnp.concatenate(parts, axis=1)
        stacked = part.reshape(hi, tp, sh, rows, -1).transpose(0, 2, 1, 3, 4).reshape(groups, tp * rows, -1)
        return stacked

    def sent(stacked):
        return lax.psum_scatter(stacked, FS, scatter_dimension=0, tiled=False)

    s_down = summed([(flat_cot, activated)])
    s_up = summed([(flat_two, grad_before)])
    grad_before, s_down, s_up = lax.optimization_barrier((grad_before, s_down, s_up))
    g_down, g_up = sent(s_down), sent(s_up)

    grad_middle, sums_two, grad_branch = call(
        partial(branch_kernel, hi, sh),
        [(grad_before, False), (w_mlp, True), (middle, False), (cotangent, False), (vec_rows, False)],
        [(own_f32, False), (jax.ShapeDtypeStruct((4, 8, d), F32), False), (gathered, True)],
        own_scratch
        + [pltpu.VMEM((d, units), BF), pltpu.SemaphoreType.DMA]
        + sum_scratch(row_tokens, d)
        + gather_scratch(),
        3,
        95,
        "second_norm_backward",
    )
    grad_branch, g_down = lax.optimization_barrier((grad_branch, g_down))
    (grad_joined,) = call(
        partial(attention_back_kernel, hi, sh),
        [(grad_branch, row_of(d)), (w_attn, True), (qkv, row_of(3 * hc)), (lengths, fixed(lengths))],
        [(jax.ShapeDtypeStruct((t_all, 3 * hc), BF), rows_of(3 * hc))],
        [pltpu.VMEM((d, hc), BF), pltpu.SemaphoreType.DMA],
        None,
        25,
        "attention_backward",
        grid=(tp,),
    )
    grad_branch = grad_branch.reshape(t_all, d)
    s_attn = summed([(flat_one, grad_joined), (grad_branch, attended)])
    grad_joined, s_attn = lax.optimization_barrier((grad_joined, s_attn))
    g_attn = sent(s_attn)
    g_mlp = jnp.concatenate([g_up, g_down], axis=1)
    ortho_mlp = orthogonalize(mom_mlp, g_mlp, hi, sh, 5, "orthogonalize_mlp")
    grad_joined, ortho_mlp = lax.optimization_barrier((grad_joined, ortho_mlp))
    grad_tokens, sums_one, output = call(
        partial(last_kernel, hi, sh),
        [(grad_joined, False), (w_attn, True), (activated, False), (w_mlp, True)]
        + [(tokens, False), (middle, False), (grad_middle, False), (vec_rows, False)],
        [(own_f32, False), (jax.ShapeDtypeStruct((2, 8, d), F32), False), (own_bf, False)],
        own_scratch[:1]
        + [pltpu.VMEM((d, 3 * hc), BF), pltpu.VMEM((d, units), BF), pltpu.SemaphoreType.DMA((2,))]
        + sum_scratch(row_tokens, d) * 2,
        4,
        85,
        "first_norm_backward",
    )
    grad_tokens, output, g_attn = lax.optimization_barrier((grad_tokens, output, g_attn))

    def back(part):
        return swap(part.reshape(tp, rows, -1))

    weight_grad = restore(back(g_attn), back(g_mlp)).astype(F32)
    moment_new = 0.95 * momentum + weight_grad
    ortho_attn = orthogonalize(mom_attn, g_attn, hi, sh, 6, "orthogonalize_attention")
    orthogonal_rows = restore(back(ortho_attn), back(ortho_mlp)).astype(F32)
    new_weights = weights * (1.0 - 0.15 * 0.1) - 0.15 * 0.2 * math.sqrt(d) * orthogonal_rows

    sums_one, sums_two = jnp.sum(sums_one, axis=1), jnp.sum(sums_two, axis=1)
    plain = jnp.stack(
        [
            sums_one[0],
            sums_one[1],
            sums_two[0],
            sums_two[1],
            jnp.zeros((d,), F32),
            jnp.zeros((d,), F32),
            sums_two[2],
            sums_two[3],
        ],
        axis=0,
    )
    plain = lax.dynamic_update_slice(plain, jnp.sum(grad_joined[:, :hc], axis=0, dtype=F32)[None], (4, me * hc))
    plain = lax.dynamic_update_slice(plain, jnp.sum(grad_joined[:, 2 * hc :], axis=0, dtype=F32)[None], (5, me * hc))
    hidden = jnp.zeros((inner_all * head,), F32)
    hidden = lax.dynamic_update_slice(hidden, jnp.sum(grad_before, axis=0, dtype=F32), (me * inner * head,))
    terms = jnp.concatenate([plain, hidden.reshape(-1, d)], axis=0)
    terms = terms.reshape(-1, world, rows).transpose(1, 0, 2).reshape(world, -1)
    vector_grad = jnp.sum(lax.all_to_all(terms, ALL, split_axis=0, concat_axis=0, tiled=True), axis=0)
    vector_grad = vector_grad.reshape(-1, rows).T
    first_moment = 0.9 * vector_moment + 0.1 * vector_grad
    second = 0.95 * vector_second + 0.05 * vector_grad * vector_grad
    corrected = first_moment / (1.0 - 0.9**STEP)
    normal_second = second / (1.0 - 0.95**STEP)
    next_vectors = vectors - 0.5 * corrected / (jnp.sqrt(normal_second) + 1e-08)
    return (
        output,
        grad_tokens,
        weight_grad,
        new_weights,
        moment_new,
        first_moment,
        second,
        next_vectors,
    )


def solution(mesh):
    dp, sh = mesh.shape["dp"], mesh.shape["shard"]
    tp = math.gcd(dp, 8)
    fine = Mesh(mesh.devices.reshape(dp // tp, tp, sh), ALL)
    two, three = P(ALL, None), P(ALL, None, None)
    return jax.shard_map(
        local,
        mesh=fine,
        in_specs=(two, two, three, three, two, two, two, two),
        out_specs=(two, two, three, three, three, two, two, two),
        check_vma=False,
    )
```

time: 1110 us -> 844 us (0.76)
  Pallas kernels: 378 us -> 534 us
  matrix products: 162 us -> 37.8 us
  local copies, waits for them, and re-layouts: 163 us -> 51.7 us
  waiting for transfers between devices: 145 us -> 50.5 us
  blocking collectives: 154 us -> 79.4 us
  other arithmetic: 63.4 us -> 30.5 us
  starting transfers between devices: 19.7 us -> 35.6 us
    pallas_call x4 -> x8, Pallas kernels: 378 us -> 534 us  [call(): pl.pallas_call(body, out_shape=[s for s, _ in outs], in_specs=[spec(how)...]
    dot_general x13 -> x4, matrix products: 109 us -> 37.8 us  [dot(): return jnp.einsum(spec, a, b, preferred_element_type=F32, **kw)]
    reduce_scatter x3, waiting for transfers between devices: 78.7 us -> 8.43 us  [sent(): return lax.psum_scatter(stacked, FS, scatter_dimension=0, tiled=False)]
    dot_general x15 -> x0, matrix products: 47.7 us -> none  [ein(): jnp.einsum(spec, a, b, precision=lax.Precision.HIGH, preferred_element_ty...]
    all_to_all x3, blocking collectives: 124 us -> 79.4 us  [swap(): return lax.all_to_all(array, 'tp', split_axis=0, concat_axis=0, tiled=True)]
    convert_element_type x10 -> x0, local copies, waits for them, and re-layouts: 41.9 us -> none  [the longest x2 17.8 us: local(): moment_mine = 0.95 * mom_mine.astype(F32) + g_mine.astype(F32)]
    all_gather x3 -> x0, blocking collectives: 29.3 us -> none  [the longest x1 12.1 us: local(): vec = lax.all_gather(vec, FS, axis=0, tiled=False)]
    all_to_all x2 -> x5, waiting for transfers between devices: 66 us -> 39 us  [swap(): return lax.all_to_all(array, 'tp', split_axis=0, concat_axis=0, tiled=True)]
  transfers between devices with their start and end apart: 8 -> 11, of which waited for: 2 -> 5; matrix products, arithmetic and copies ran while one was open for 25% -> 8% of each run, Pallas kernels for 34% -> 60%
where the time goes in v3:
time: 844 us; the launch traced here: 834 us
  Pallas kernels  534 us (63%)
  blocking collectives  79.4 us (9%)
  local copies, waits for them, and re-layouts  51.7 us (6%)
  waiting for transfers between devices  50.5 us (6%)
  matrix products  37.8 us (4%)
  starting transfers between devices  35.6 us (4%)
  other arithmetic  30.5 us (4%)
  between operations  14.6 us (2%)
    pallas_call x8, Pallas kernels, call(): pl.pallas_call(body, out_shape=[s for s, _ in outs], in_specs=[spec(how)...  534 us
    all_to_all x3, blocking collectives, swap(): return lax.all_to_all(array, 'tp', split_axis=0, concat_axis=0, tiled=True)  79.4 us
    all_to_all x5, waiting for transfers between devices, swap(): return lax.all_to_all(array, 'tp', split_axis=0, concat_axis=0, tiled=True)  39 us
    dot_general x4, matrix products, dot(): return jnp.einsum(spec, a, b, preferred_element_type=F32, **kw)  37.8 us
    all_to_all x5, starting transfers between devices, swap(): return lax.all_to_all(array, 'tp', split_axis=0, concat_axis=0, tiled=True)  29.3 us
  transfers between devices with their start and end apart: 11, of which 5 were waited for; matrix products, arithmetic and copies ran while one was open for 8% of the time, Pallas kernels for 60%

profile of v3, /device:TPU:27, one launch (start us, length us, event | category | flops | bytes accessed | tf_op | source)
XLA Modules:
  0.0 833.9 jit_solution(1263005528668405213)
XLA Ops:
  7.2 3.4 convert_element_type.39
  10.7 1.8 copy.71
  12.4 2.6 reshape.171
  15.0 18.7 %all_to_all.50 = bf16[8,64,1024]{2,1,0:T(8,128)(2,1)} all-to-all(bf16[8,64,1024]{2,1,0:T(8,128)(2,1)} %reshape.171), channel_id=1, replica_groups=mesh['dp'=8,'shard'=4] {'dp'}, dimensions={0} | all-to-all | bytes 2097152 | tf_op jit(solution)/shard_map/all_to_all | solution.py:663
  34.4 2.3 reshape.169
  36.6 30.9 %all_to_all.51 = bf16[8,64,2048]{2,1,0:T(8,128)(2,1)} all-to-all(bf16[8,64,2048]{2,1,0:T(8,128)(2,1)} %reshape.169), channel_id=1, replica_groups=mesh['dp'=8,'shard'=4] {'dp'}, dimensions={0} | all-to-all | bytes 4194304 | tf_op jit(solution)/shard_map/all_to_all | solution.py:663
  67.6 3.4 convert_element_type.41
  71.1 1.8 copy.54
  72.8 2.6 reshape.173
  75.4 5.8 all-to-all-start.2
  81.8 2.3 reshape.176
  84.0 11.1 %all-to-all-done.2 = bf16[8,64,1024]{2,1,0:T(8,128)(2,1)} async-done(((bf16[8,64,1024]{2,1,0:T(8,128)(2,1)}), bf16[8,64,1024]{2,1,0:T(8,128)(2,1)}, u32[]{:S(2)}, u32[]{:S(2)}) %all-to-all-start.2) | async-done | bytes 1048608 | tf_op jit(solution)/shard_map/all_to_all | solution.py:663
  95.1 5.1 all-to-all-start.3
  101.2 68.1 %first_norm.1 = (bf16[8,256,2048]{2,1,0:T(8,128)(2,1)}, f32[16,2048]{1,0:T(8,128)}, f32[8,128]{1,0:T(8,128)}) custom-call(bf16[256,2048]{1,0:T(8,128)(2,1)} %tok.2, bf16[16,128]{1,0:T(8,128)(2,1)} %fusion.3.piece, bf16[256,2048]{1,0:T(8,128)(2,1)} %cot.5), custom_call_target="tpu_custom_call" | custom-call | bytes 150000000 | tf_op jit(solution)/shard_map/first_norm/pallas_call | solution.py:498
  169.3 128.0 %attention.1 = (f32[256,2048]{1,0:T(8,128)}, bf16[8,256,2048]{2,1,0:T(8,128)(2,1)}, bf16[8,256,2048]{2,1,0:T(8,128)(2,1)}, bf16[8,256,768]{2,1,0:T(8,128)(2,1)}, bf16[2048,256]{1,0:T(8,128)(2,1)}) custom-call(bf16[8,256,2048]{2,1,0:T(8,128)(2,1)} %get-tuple-element.42.normed, bf16[4,8,64,1024]{3,2,1,0:T(8,128)(2,1)} %bitcast.89, ...), custom_call_target="tpu_custom_call" | custom-call | bytes 330000000 | tf_op jit(solution)/shard_map/attention/pallas_call | solution.py:498
  297.4 29.7 %hidden_units.1 = (bf16[2048,1024]{1,0:T(8,128)(2,1)}, bf16[2048,1024]{1,0:T(8,128)(2,1)}) custom-call(bf16[8,256,2048]{2,1,0:T(8,128)(2,1)} %get-tuple-element.46.normed, bf16[8,256,2048]{2,1,0:T(8,128)(2,1)} %get-tuple-element.47.cot, bf16[4,8,64,2048]{3,2,1,0:T(8,128)(2,1)} %bitcast.86, f32[16,2048]{1,0:T(8,128)} %get-tuple-element.44.vec), custom_call_target="tpu_custom_call" | custom-call | bytes 90000000 | tf_op jit(solution)/shard_map/hidden_units/pallas_call | solution.py:498
  327.1 13.0 %convolution_convert_fusion.1 = bf16[2048,1024]{1,0:T(8,128)(2,1)S(1)} fusion(bf16[2048,2048]{1,0:T(8,128)(2,1)} %bitcast.97, bf16[2048,1024]{1,0:T(8,128)(2,1)} %get-tuple-element.50.activated), kind=kOutput, calls=%fused_computation.5 | convolution fusion | flops 8592031744 | bytes 16777216 | tf_op jit(solution)/shard_map/td,tn->dn/dot_general | solution.py:637
  340.2 2.6 copy.56
  343.9 9.6 %convolution_convert_fusion = bf16[2048,1024]{1,0:T(8,128)(2,1)S(1)} fusion(bf16[2048,2048]{1,0:T(8,128)(2,1)S(1)} %bitcast.96, bf16[2048,1024]{1,0:T(8,128)(2,1)S(1)} %copy-done.2), kind=kOutput, calls=%fused_computation.4 | convolution fusion | flops 8592031744 | bytes 16777216 | tf_op jit(solution)/shard_map/td,tn->dn/dot_general | solution.py:637
  353.5 2.4 copy.57
  356.5 96.2 %second_norm_backward.1 = (f32[256,2048]{1,0:T(8,128)}, f32[4,8,2048]{2,1,0:T(8,128)}, bf16[8,256,2048]{2,1,0:T(8,128)(2,1)}) custom-call(bf16[2048,1024]{1,0:T(8,128)(2,1)} %get-tuple-element.51.grad_before, bf16[4,8,64,2048]{3,2,1,0:T(8,128)(2,1)} %bitcast.87, f32[256,2048]{1,0:T(8,128)} %get-tuple-element.52.middle, bf16[256,2048]{1,0:T(8,128)(2,1)} %cot.5, ...), custom_call_target="tpu_custom_call" | custom-call | bytes 285000000 | tf_op jit(solution)/shard_map/second_norm_backward/pallas_call | solution.py:498
  452.8 18.0 %attention_backward.1.grad_joined = bf16[2048,768]{1,0:T(8,128)(2,1)} custom-call(bf16[8,256,2048]{2,1,0:T(8,128)(2,1)} %get-tuple-element.55.branch, bf16[4,8,64,1024]{3,2,1,0:T(8,128)(2,1)} %bitcast.90, bf16[8,256,768]{2,1,0:T(8,128)(2,1)} %get-tuple-element.56.qkv, f32[8,128]{1,0:T(8,128)} %get-tuple-element.43.lengths), custom_call_target="tpu_custom_call" | custom-call | bytes 75000000 | tf_op jit(solution)/shard_map/attention_backward/pallas_call | solution.py:498
  470.8 5.9 convolution_convert_fusion.3
  476.7 9.3 %convolution_convert_fusion.2 = bf16[2048,768]{0,1:T(8,128)(2,1)S(1)} fusion(bf16[2048,2048]{1,0:T(8,128)(2,1)} %bitcast.102, bf16[2048,768]{1,0:T(8,128)(2,1)S(1)} %copy-done), kind=kOutput, calls=%fused_computation.6 | convolution fusion | flops 6444023808 | bytes 14680064 | tf_op jit(solution)/shard_map/td,tn->dn/dot_general | solution.py:637
  486.1 2.3 pad_maximum_fusion
  488.4 6.5 copy.58
  494.9 4.9 copy.59
  500.0 3.0 convert_reduce_fusion
  503.5 8.4 %reduce-scatter.6.cloned.1.call-done = bf16[1,512,1024]{2,1,0:T(8,128)(2,1)} async-done(((bf16[4,512,1024]{2,1,0:T(8,128)(2,1)}), bf16[1,512,1024]{2,1,0:T(8,128)(2,1)}) %reduce-scatter.6.cloned.1.call-update) | async-done | bytes 1048592 | tf_op jit(solution)/shard_map/reduce_scatter | solution.py:753
  511.9 2.7 pad_maximum_fusion.1.grad
  514.6 63.2 %orthogonalize_mlp.1 = bf16[512,2048]{1,0:T(8,128)(2,1)} custom-call(bf16[512,2048]{1,0:T(8,128)(2,1)} %bitcast.99, bf16[512,2048]{1,0:T(8,128)(2,1)} %pad_maximum_fusion.1.grad), custom_call_target="tpu_custom_call" | custom-call | bytes 75000000 | tf_op jit(solution)/shard_map/orthogonalize_mlp/pallas_call | solution.py:498
  577.8 108.9 %first_norm_backward.1 = (f32[256,2048]{1,0:T(8,128)}, f32[2,8,2048]{2,1,0:T(8,128)}, bf16[256,2048]{1,0:T(8,128)(2,1)}) custom-call(bf16[2048,768]{1,0:T(8,128)(2,1)} %attention_backward.1.grad_joined, bf16[4,8,64,1024]{3,2,1,0:T(8,128)(2,1)} %bitcast.91, bf16[2048,1024]{1,0:T(8,128)(2,1)} %get-tuple-element.50.activated, ...), custom_call_target="tpu_custom_call" | custom-call | bytes 255000000 | tf_op jit(solution)/shard_map/first_norm_backward/pallas_call | solution.py:498
  689.6 5.9 all-to-all-start.8
  695.6 1.7 pad_maximum_fusion.2
  697.3 2.5 all-to-all-done.8
  699.8 29.7 %all_to_all.52 = bf16[8,64,2048]{2,1,0:T(8,128)(2,1)} all-to-all(bf16[8,64,2048]{2,1,0:T(8,128)(2,1)S(1)} %pad_maximum_fusion.2), channel_id=1, replica_groups=mesh['dp'=8,'shard'=4] {'dp'}, dimensions={0} | all-to-all | bytes 4194304 | tf_op jit(solution)/shard_map/all_to_all | solution.py:663
  729.5 5.2 all-to-all-start.7
  734.8 25.0 %all-to-all-done.7 = bf16[8,64,2048]{2,1,0:T(8,128)(2,1)S(1)} async-done(((bf16[8,64,2048]{2,1,0:T(8,128)(2,1)}), bf16[8,64,2048]{2,1,0:T(8,128)(2,1)S(1)}, u32[]{:S(2)}, u32[]{:S(2)}) %all-to-all-start.7) | async-done | bytes 2097184 | tf_op jit(solution)/shard_map/all_to_all | solution.py:663
  759.8 5.1 all-to-all-start.4
  764.9 21.7 %orthogonalize_attention.1 = bf16[512,1024]{1,0:T(8,128)(2,1)} custom-call(bf16[512,1024]{1,0:T(8,128)(2,1)} %bitcast.8.mom, bf16[512,1024]{1,0:T(8,128)(2,1)} %bitcast.111), custom_call_target="tpu_custom_call" | custom-call | bytes 75000000 | tf_op jit(solution)/shard_map/orthogonalize_attention/pallas_call | solution.py:498
  786.6 8.1 all-to-all-start.6
  795.5 2.2 copy.66
  800.0 1.9 copy.63
  803.4 2.4 copy.60
  805.8 2.8 all-to-all-done.6
  808.6 2.6 reshape.194
  811.2 2.4 copy.62
  813.6 11.2 %multiply_add_fusion = (f32[64,192,128]{2,1,0:T(8,128)}, f32[64,192,128]{2,1,0:T(8,128)}, f32[64,192,128]{2,1,0:T(8,128)}) fusion(f32[64,192,128]{2,1,0:T(8,128)} %param.11, bf16[64,128,128]{2,1,0:T(8,128)(2,1)S(1)} %bitcast.100, bf16[64,64,128]{2,1,0:T(8,128)(2,1)S(1)} %bitcast.113, bf16[64,128,128]{2,1,0:T(8,128)(2,1)} %bitcast.101, ...), kind=kLoop, calls=%fused_computation.1 | loop fusion | flops 20447232 | bytes 37748736 | tf_op jit(solution)/shard_map/add | solution.py:808
  (84 shorter events, 14.3 us)
Async XLA Ops:
  7.2 162.2 %all-gather.5.cloned.1.call-start = ((), (), s32[]{:S(2)}) async-start(), calls=%async_computation.15 | async-start | bytes 5242880 | tf_op jit(solution)/shard_map/all_gather | solution.py:668
  33.8 263.7 %all-gather.7.cloned.1.call-start = ((), (), s32[]{:S(2)}) async-start(), calls=%async_computation.16 | async-start | bytes 10485760 | tf_op jit(solution)/shard_map/all_gather | solution.py:668
  75.4 19.7 %all-to-all-start.2 = ((bf16[8,64,1024]{2,1,0:T(8,128)(2,1)}), bf16[8,64,1024]{2,1,0:T(8,128)(2,1)}, u32[]{:S(2)}, u32[]{:S(2)}) async-start(bf16[8,64,1024]{2,1,0:T(8,128)(2,1)} %reshape.173), calls=%async_computation.2 | async-start | bytes 2097152 | tf_op jit(solution)/shard_map/all_to_all | solution.py:663
  81.7 18.7 %copy-start.11 = (f32[64,12]{0,1:T(8,128)S(1)}, f32[64,12]{0,1:T(8,128)}, u32[]{:S(2)}) copy-start(f32[64,12]{0,1:T(8,128)} %param.12) | copy-start | bytes 9220
  81.7 18.8 %copy-start.15 = (s32[1,4]{1,0:T(1,128)S(1)}, s32[1,4]{1,0:T(1,128)}, u32[]{:S(2)}) copy-start(s32[1,4]{1,0:T(1,128)} %param.9) | copy-start | bytes 52
  95.1 202.2 %all-to-all-start.3 = ((bf16[8,64,2048]{2,1,0:T(8,128)(2,1)}), bf16[8,64,2048]{2,1,0:T(8,128)(2,1)S(1)}, u32[]{:S(2)}, u32[]{:S(2)}) async-start(bf16[8,64,2048]{2,1,0:T(8,128)(2,1)} %reshape.176), calls=%async_computation.3 | async-start | bytes 4194304 | tf_op jit(solution)/shard_map/all_to_all | solution.py:663
  100.3 352.5 %reduce-scatter.4.cloned.1.call-start = ((), (), s32[]{:S(2)}) async-start(), calls=%async_computation.12 | async-start | bytes 5242880 | tf_op jit(solution)/shard_map/reduce_scatter | solution.py:753
  297.4 29.7 %copy-start.4 = (bf16[8,64,2048]{2,1,0:T(8,128)(2,1)}, bf16[8,64,2048]{2,1,0:T(8,128)(2,1)S(1)}, u32[]{:S(2)}) copy-start(bf16[8,64,2048]{2,1,0:T(8,128)(2,1)S(1)} %all-to-all-done.3) | copy-start | bytes 6291460
  327.1 15.6 %copy-start.3 = (bf16[8,256,2048]{2,1,0:T(8,128)(2,1)S(1)}, bf16[8,256,2048]{2,1,0:T(8,128)(2,1)}, u32[]{:S(2)}) copy-start(bf16[8,256,2048]{2,1,0:T(8,128)(2,1)} %get-tuple-element.46.normed) | copy-start | bytes 25165828
  340.2 3.7 copy-start.2
  355.9 155.9 %reduce-scatter.6.cloned.1.call-start = ((), (), s32[]{:S(2)}) async-start(), calls=%async_computation.13 | async-start | bytes 5242880 | tf_op jit(solution)/shard_map/reduce_scatter | solution.py:753
  356.5 378.3 %reduce-scatter.8.cloned.1.call-start = ((), (), s32[]{:S(2)}) async-start(), calls=%async_computation.14 | async-start | bytes 5242880 | tf_op jit(solution)/shard_map/reduce_scatter | solution.py:753
  452.8 18.0 %copy-start.14 = (bf16[2048,256]{1,0:T(8,128)(2,1)S(1)}, bf16[2048,256]{1,0:T(8,128)(2,1)}, u32[]{:S(2)}) copy-start(bf16[2048,256]{1,0:T(8,128)(2,1)} %get-tuple-element.57) | copy-start | bytes 3145732
  470.8 5.9 copy-start
  499.9 3.5 copy-start.10
  499.9 12.0 %copy-start.7 = (bf16[1,512,1024]{2,1,0:T(8,128)(2,1)S(1)}, bf16[1,512,1024]{2,1,0:T(8,128)(2,1)}, u32[]{:S(2)}) copy-start(bf16[1,512,1024]{2,1,0:T(8,128)(2,1)} %reduce-scatter.4.cloned.1.call-done) | copy-start | bytes 3145732
  577.8 109.9 %copy-start.1 = (bf16[2048,768]{1,0:T(8,128)(2,1)S(1)}, bf16[2048,768]{1,0:T(8,128)(2,1)}, u32[]{:S(2)}) copy-start(bf16[2048,768]{1,0:T(8,128)(2,1)} %attention_backward.1.grad_joined) | copy-start | bytes 9437188
  689.6 10.2 %all-to-all-start.8 = ((f32[32,1,768]{2,1,0:T(1,128)}), f32[32,1,768]{2,1,0:T(1,128)S(1)}, u32[]{:S(2)}, u32[]{:S(2)}) async-start(f32[32,1,768]{2,1,0:T(1,128)} %all_to_all.40), calls=%async_computation.11 | async-start | bytes 196608 | tf_op jit(solution)/shard_map/all_to_all | solution.py:833
  729.5 30.3 %all-to-all-start.7 = ((bf16[8,64,2048]{2,1,0:T(8,128)(2,1)}), bf16[8,64,2048]{2,1,0:T(8,128)(2,1)S(1)}, u32[]{:S(2)}, u32[]{:S(2)}) async-start(bf16[8,64,2048]{2,1,0:T(8,128)(2,1)} %bitcast.39), calls=%async_computation.10 | async-start | bytes 4194304 | tf_op jit(solution)/shard_map/all_to_all | solution.py:663
  734.7 60.1 %copy-start.12 = (f32[64,12]{0,1:T(8,128)S(1)}, f32[64,12]{0,1:T(8,128)}, u32[]{:S(2)}) copy-start(f32[64,12]{0,1:T(8,128)} %param.14) | copy-start | bytes 9220
  734.7 60.1 %copy-start.13 = (f32[64,12]{0,1:T(8,128)S(1)}, f32[64,12]{0,1:T(8,128)}, u32[]{:S(2)}) copy-start(f32[64,12]{0,1:T(8,128)} %param.13) | copy-start | bytes 9220
  759.8 37.9 %copy-start.5 = (bf16[8,64,2048]{2,1,0:T(8,128)(2,1)}, bf16[8,64,2048]{2,1,0:T(8,128)(2,1)S(1)}, u32[]{:S(2)}) copy-start(bf16[8,64,2048]{2,1,0:T(8,128)(2,1)S(1)} %all-to-all-done.7) | copy-start | bytes 6291460
  759.8 26.8 %all-to-all-start.4 = ((bf16[8,64,1024]{2,1,0:T(8,128)(2,1)}), bf16[8,64,1024]{2,1,0:T(8,128)(2,1)S(1)}, u32[]{:S(2)}, u32[]{:S(2)}) async-start(bf16[8,64,1024]{2,1,0:T(8,128)(2,1)} %bitcast.110), calls=%async_computation.7 | async-start | bytes 2097152 | tf_op jit(solution)/shard_map/all_to_all | solution.py:663
  786.6 22.0 %all-to-all-start.6 = ((bf16[8,64,1024]{2,1,0:T(8,128)(2,1)}), bf16[8,64,1024]{2,1,0:T(8,128)(2,1)}, u32[]{:S(2)}, u32[]{:S(2)}) async-start(bf16[8,64,1024]{2,1,0:T(8,128)(2,1)} %bitcast.112), calls=%async_computation.9 | async-start | bytes 2097152 | tf_op jit(solution)/shard_map/all_to_all | solution.py:663
  797.7 1.6 copy-start.6
  813.6 11.2 %copy-start.9 = (bf16[256,2048]{1,0:T(8,128)(2,1)S(1)}, bf16[256,2048]{1,0:T(8,128)(2,1)}, u32[]{:S(2)}) copy-start(bf16[256,2048]{1,0:T(8,128)(2,1)} %get-tuple-element.92) | copy-start | bytes 3145732
  813.6 12.2 %copy-start.8 = (f32[256,2048]{1,0:T(8,128)S(1)}, f32[256,2048]{1,0:T(8,128)}, u32[]{:S(2)}) copy-start(f32[256,2048]{1,0:T(8,128)} %get-tuple-element.93) | copy-start | bytes 6291460
Sparse Core Ops, SparseCore 0:
  33.9 78.7 all-gather.4
  114.3 147.7 all-gather.6
  356.0 76.2 reduce-scatter.3
  434.6 77.2 reduce-scatter.5
  514.6 93.9 reduce-scatter.7

commit v4 on v3

--- a/solution.py
+++ b/solution.py
@@ -10,6 +10,7 @@
 
 HEADS = 16
 HEAD = 128
+PAIR = 2 * HEAD
 NS_ITERS = 5
 STEP = 10
 
@@ -90,6 +91,11 @@
         self.copies[stage, k] = copy
 
     def run(self):
+        self.first()
+        self.second()
+        self.third()
+
+    def first(self):
         me, c, x, y, pc, px, py = spots()
         oc, ox, oy = 1 - c, 1 - x, 1 - y
         part = self.part
@@ -110,6 +116,11 @@
             if k:
                 core_stage(k - 1)
         core_stage(self.count - 1)
+
+    def second(self):
+        me, c, x, y, pc, px, py = spots()
+        ox, oy = 1 - x, 1 - y
+        part = self.part
         for k in range(self.count):
             self.copies[1, k].wait_recv()
             for i in range(2):
@@ -121,9 +132,12 @@
                 self.begin(2, k, part.at[k, oy, x, c], self.from_2.at[k], py)
             else:
                 self.begin(2, k, part.at[k, y, ox, c], self.from_2.at[k], px)
+
+    def third(self):
+        me, c, x, y, pc, px, py = spots()
         for k in range(self.count):
             self.copies[2, k].wait_recv()
-            self.total[:, k * WIDE : (k + 1) * WIDE] = part[k, y, x, c].astype(F32) + self.from_2[k].astype(F32)
+            self.total[:, k * WIDE : (k + 1) * WIDE] = self.part[k, y, x, c].astype(F32) + self.from_2[k].astype(F32)
 
     def end(self):
         for copy in self.copies.values():
@@ -230,7 +244,7 @@
     pltpu.make_async_copy(held, held, sem).wait()
 
 
-def first_kernel(hi, sh, tok, piece, cot, normed_all, vec, lengths, own, pieces, send_p, recv_p, send_q, recv_q, *sems):
+def first_kernel(hi, sh, tok, piece, normed_all, vec, lengths, own, pieces, send_p, recv_p, send_q, recv_q, *sems):
     me, c, x, y, pc, px, py = spots()
     groups = hi * sh
     mine = lax.axis_index("hi") * sh + lax.axis_index("shard")
@@ -347,8 +361,10 @@
 
     lax.fori_loop(0, 8, one_row, 0)
     sums = Summing(att, w.at[:, 3 * hc :], total, scratch[:6])
+    sums.first()
     spread_cot.forward()
-    sums.run()
+    sums.second()
+    sums.third()
 
     def body(at):
         values = tok[at, :].astype(F32) + total[at, :] + vec[6:7, :]
@@ -368,13 +384,16 @@
 GELU_A = math.sqrt(2.0 / math.pi)
 
 
-def mlp_kernel(hi, sh, normed, cot, w_any, vec, activated, grad_before, w_up, w_down, sems):
+def mlp_kernel(hi, sh, normed, cot, w_any, vec, mom, activated, grad_before, mom_out, w_up, w_down, sems, *scratch):
     width = w_up.shape[1]
+    swapped = Swapping(mom, mom_out, *scratch)
 
     @pl.when(pl.program_id(0) == 0)
     def _():
         fetch_rows(w_any, 0, w_up, sems.at[0], hi, sh)
         fetch_rows(w_any, width, w_down, sems.at[1], hi, sh)
+        meet_all(group_peers())
+        swapped.start()
         fetched(w_up, sems.at[0])
         fetched(w_down, sems.at[1])
 
@@ -392,8 +411,13 @@
         inner = GELU_A + 3.0 * GELU_A * 0.044715 * square
         grad_before[:, at] = (grad * (half + 0.5 * before * (1.0 - slope * slope) * inner)).astype(BF)
 
-
-def attention_back_kernel(hi, sh, branch, w_any, qkv, lengths, grad_joined, w, sem):
+    @pl.when(pl.program_id(0) == pl.num_programs(0) - 1)
+    def _():
+        swapped.end()
+
+
+def attention_back_kernel(hi, sh, branch, w_any, qkv, lengths, mom, grad_joined, mom_out, w, sem, *scratch):
+    swapped = Swapping(mom, mom_out, *scratch)
     hc = w.shape[1]
     size = branch.shape[1]
     r = pl.program_id(0)
@@ -401,6 +425,8 @@
     @pl.when(r == 0)
     def _():
         fetch_rows(w_any, 3 * hc, w, sem, hi, sh)
+        meet_all(group_peers())
+        swapped.start()
         fetched(w, sem)
 
     grad_att = jnp.dot(branch[0], w[...], preferred_element_type=F32).astype(BF)
@@ -423,14 +449,20 @@
         for n in range(3):
             grad_joined[:, n * hc + h * HEAD : n * hc + (h + 1) * HEAD] = made[n].astype(BF)
 
+    @pl.when(r == pl.num_programs(0) - 1)
+    def _():
+        swapped.end()
+
 
 def branch_kernel(
-    hi, sh, grad_before, w_any, middle, cot, vec, grad_middle, sums_out, branch_all, total, own, w_up, w_sem, *scratch
+    hi, sh, grad_before, activated, w_any, middle, cot, vec, grad_middle, sums_out, branch_all, output, total, own,
+    w_up, w_down, w_sem, *scratch
 ):
     me, c, x, y, pc, px, py = spots()
-    fetch_rows(w_any, 0, w_up, w_sem, hi, sh)
+    fetch_rows(w_any, 0, w_up, w_sem.at[0], hi, sh)
+    fetch_rows(w_any, w_up.shape[1], w_down, w_sem.at[1], hi, sh)
     meet((pc, px, py))
-    fetched(w_up, w_sem)
+    fetched(w_up, w_sem.at[0])
     sums = Summing(grad_before, w_up, total, scratch[:6])
     sums.run()
     sums_out[...] = jnp.zeros_like(sums_out)
@@ -448,44 +480,57 @@
             sums_out[n] += values[:8] + values[8:]
 
     row_loop(own.shape[0], body)
-    spread = Gathering(own, branch_all, *scratch[6:])
+    spread = Gathering(own, branch_all, *scratch[6:9])
     spread.start()
+    fetched(w_down, w_sem.at[1])
+    more = Summing(activated, w_down, total, scratch[9:])
+    more.first()
     spread.forward()
-    sums.end()
-    spread.end()
-
-
-def last_kernel(
-    hi, sh, grad_joined, w_attn, activated, w_mlp, tok, middle, grad_middle, vec, grad_tokens, sums_out, output, total,
-    w_qkv, w_down, w_sems, *scratch
-):
-    me, c, x, y, pc, px, py = spots()
-    fetch_rows(w_attn, 0, w_qkv, w_sems.at[0], hi, sh)
-    fetch_rows(w_mlp, w_down.shape[1], w_down, w_sems.at[1], hi, sh)
-    meet((pc, px, py))
-    fetched(w_qkv, w_sems.at[0])
-    fetched(w_down, w_sems.at[1])
-    sums = Summing(grad_joined, w_qkv, total, scratch[:6])
-    sums.run()
-    sums_out[...] = jnp.zeros_like(sums_out)
-
-    def body(at):
-        grad = total[at, :]
-        part, for_gain = norm_back(tok[at, :].astype(F32), grad, vec[0:1, :])
-        grad_tokens[at, :] = grad_middle[at, :] + part
-        for n, values in enumerate((for_gain, grad)):
-            sums_out[n] += values[:8] + values[8:]
-
-    row_loop(total.shape[0], body)
-    more = Summing(activated, w_down, total, scratch[6:])
-    more.run()
+    more.second()
+    more.third()
 
     def body_two(at):
         output[at, :] = (middle[at, :] + total[at, :] + vec[7:8, :]).astype(BF)
 
-    row_loop(total.shape[0], body_two)
+    row_loop(own.shape[0], body_two)
     sums.end()
     more.end()
+    spread.end()
+
+
+def last_kernel(
+    hi, sh, grad_joined, w_attn, tok, grad_middle, vec, mom, grad, grad_tokens, sums_out, grad_back, ortho_back, total,
+    w_qkv, w_sem, ortho, *scratch
+):
+    fetch_rows(w_attn, 0, w_qkv, w_sem, hi, sh)
+    meet_all(group_peers() + [peer for _, peer in row_peers(hi, sh)])
+    work = Orthogonal(hi, sh, mom, grad, ortho, scratch[6:13])
+    grads = Swapping(grad, grad_back, *scratch[13:16])
+    orthos = Swapping(ortho, ortho_back, *scratch[16:19])
+    sums = Summing(grad_joined, w_qkv, total, scratch[:6])
+    work.grams()
+    fetched(w_qkv, w_sem)
+    sums.first()
+    grads.start()
+    work.iterate()
+    sums.second()
+    work.finish()
+    orthos.start()
+    sums.third()
+    sums_out[...] = jnp.zeros_like(sums_out)
+
+    def body(at):
+        there = total[at, :]
+        part, for_gain = norm_back(tok[at, :].astype(F32), there, vec[0:1, :])
+        grad_tokens[at, :] = grad_middle[at, :] + part
+        for n, values in enumerate((for_gain, there)):
+            sums_out[n] += values[:8] + values[8:]
+
+    row_loop(total.shape[0], body)
+    sums.end()
+    grads.end()
+    work.end()
+    orthos.end()
 
 
 def call(body, ins, outs, scratch, number, microseconds, name, grid=None):
@@ -497,7 +542,7 @@
     remote_params = {} if number is None else {"collective_id": number, "has_side_effects": True}
     return pl.pallas_call(
         body,
-        out_shape=[s for s, _ in outs],
+        out_shape=[jax.ShapeDtypeStruct(s.shape, s.dtype) for s, _ in outs],
         in_specs=[spec(how) for _, how in ins],
         out_specs=[spec(how) for _, how in outs],
         scratch_shapes=scratch,
@@ -508,129 +553,184 @@
     )(*[a for a, _ in ins])
 
 
-PAIR = 2 * HEAD
-
-
-def ortho_kernel(hi, sh, mom, grad, out, gram, arrived, power, send_a, recv_a, send_b, recv_b):
-    groups = hi * sh
+class Swapping:
+    def __init__(self, own, out, send, recv, local):
+        me = lax.axis_index("tp")
+        self.copies = []
+        for i in range(1, 8):
+            peer = rem(me + i, 8)
+            self.copies.append(remote(own.at[peer], out.at[me], send.at[i - 1], recv.at[i - 1], peer))
+        self.kept = pltpu.make_async_copy(own.at[me], out.at[me], local)
+
+    def start(self):
+        for copy in self.copies:
+            copy.start()
+        self.kept.start()
+
+    def end(self):
+        for copy in self.copies:
+            copy.wait_recv()
+        for copy in self.copies:
+            copy.wait_send()
+        self.kept.wait()
+
+
+def swap_scratch():
+    return [pltpu.SemaphoreType.DMA((7,)), pltpu.SemaphoreType.DMA((7,)), pltpu.SemaphoreType.DMA]
+
+
+def group_peers():
+    me = lax.axis_index("tp")
+    return [{"tp": rem(me + i, 8)} for i in range(1, 8)]
+
+
+def row_peers(hi, sh):
     mine = lax.axis_index("hi") * sh + lax.axis_index("shard")
-    count = out.shape[1] // PAIR
-    per = gram.shape[0] // groups
-
-    def peer(i):
-        there = rem(mine + i, groups)
-        return there, {"hi": div(there, sh), "shard": rem(there, sh)}
-
+    theres = [rem(mine + i, hi * sh) for i in range(1, hi * sh)]
+    return [(there, {"hi": div(there, sh), "shard": rem(there, sh)}) for there in theres]
+
+
+def meet_all(peers):
     barrier = pltpu.get_barrier_semaphore()
-    for i in range(1, groups):
-        pl.semaphore_signal(barrier, inc=1, device_id=peer(i)[1], device_id_type=MESH)
-    pl.semaphore_wait(barrier, groups - 1)
-
-    rows = lax.broadcasted_iota(jnp.int32, (PAIR, PAIR), 0)
-    columns = lax.broadcasted_iota(jnp.int32, (PAIR, PAIR), 1)
-    unit = jnp.where(rows == columns, 1.0, 0.0)
-    one, two = slice(0, HEAD), slice(HEAD, PAIR)
-
-    def block(k):
+    for peer in peers:
+        pl.semaphore_signal(barrier, inc=1, device_id=peer, device_id_type=MESH)
+    pl.semaphore_wait(barrier, len(peers))
+
+
+class Orthogonal:
+    def __init__(self, hi, sh, mom, grad, out, scratch):
+        self.mom, self.grad, self.out = mom, grad, out
+        self.gram, self.arrived, self.power, self.send_a, self.recv_a, self.send_b, self.recv_b = scratch
+        self.mine = lax.axis_index("hi") * sh + lax.axis_index("shard")
+        self.peers = row_peers(hi, sh)
+        self.count = out.shape[2] // PAIR
+        self.per = self.gram.shape[0] // (hi * sh)
+
+    def block(self, k):
         at = pl.ds(pl.multiple_of(k * PAIR, PAIR), PAIR)
-        return (0.95 * mom[:, at].astype(F32) + grad[:, at].astype(F32)).astype(BF), at
-
-    def one_gram(k, carry):
-        values, _ = block(k)
-        made = lax.dot_general(values, values, (((0,), (0,)), ((), ())), preferred_element_type=F32)
-        gram[k, 0] = made[one, one].astype(BF)
-        gram[k, 1] = made[two, two].astype(BF)
-        return carry
-
-    lax.fori_loop(0, count, one_gram, 0)
-    for k in range(count, gram.shape[0]):
-        gram[k] = jnp.zeros((2, HEAD, HEAD), BF)
-
-    def copies(i, src, dst, send, recv):
+        values = 0.95 * self.mom[:, :, at].astype(F32) + self.grad[:, :, at].astype(F32)
+        return values.reshape(-1, PAIR).astype(BF), at
+
+    def copy(self, i, src, dst, send, recv):
         return pltpu.make_async_remote_copy(
-            src_ref=src, dst_ref=dst, send_sem=send.at[i - 1], recv_sem=recv.at[i - 1],
-            device_id=peer(i)[1], device_id_type=MESH,
+            src_ref=src, dst_ref=dst, send_sem=send.at[i], recv_sem=recv.at[i],
+            device_id=self.peers[i][1], device_id_type=MESH,
         )
 
-    first = [copies(i, gram.at[pl.ds(peer(i)[0] * per, per)], arrived.at[i - 1], send_a, recv_a) for i in range(1, groups)]
-    for copy in first:
-        copy.start()
-    for copy in first:
-        copy.wait_recv()
-
-    def product(a, b):
-        a_high, b_high = a.astype(BF), b.astype(BF)
-        a_low, b_low = (a - a_high.astype(F32)).astype(BF), (b - b_high.astype(F32)).astype(BF)
-        made = jnp.dot(a_high, b_low, preferred_element_type=F32) + jnp.dot(a_low, b_high, preferred_element_type=F32)
-        return made + jnp.dot(a_high, b_high, preferred_element_type=F32)
-
-    upper = (rows < HEAD) & (rows == columns)
-    lower = (rows >= HEAD) & (rows == columns)
-    grams, wholes = [], []
-    for j in range(per):
-        halves = []
-        for n in range(2):
-            half = gram[mine * per + j, n].astype(F32)
-            for i in range(groups - 1):
-                half = half + arrived[i, j, n].astype(F32)
-            halves.append(half)
-        empty = jnp.zeros((HEAD, HEAD), F32)
-        total = jnp.concatenate(
-            [jnp.concatenate([halves[0], empty], axis=1), jnp.concatenate([empty, halves[1]], axis=1)], axis=0
-        )
-
-        def scaling_of(chosen):
-            trace = jnp.sum(jnp.sum(jnp.where(chosen, total, 0.0), axis=1, keepdims=True), axis=0, keepdims=True)
-            return 1.0 / (jnp.sqrt(trace) + 1e-07)
-
-        scaling = jnp.where(rows < HEAD, scaling_of(upper), scaling_of(lower))
-        grams.append(total * (scaling * scaling))
-        wholes.append(scaling)
-    for number in range(NS_ITERS):
-        squares = [product(a, a) for a in grams]
-        steps = [COEF_A * unit + COEF_B * a + COEF_C * s for a, s in zip(grams, squares)]
-        wholes = [product(w, p) for w, p in zip(wholes, steps)] if number else [w * p for w, p in zip(wholes, steps)]
-        if number < NS_ITERS - 1:
-            grams = [product(product(a, p), p) for a, p in zip(grams, steps)]
-    for j in range(per):
-        power[mine * per + j, 0] = wholes[j][one, one].astype(BF)
-        power[mine * per + j, 1] = wholes[j][two, two].astype(BF)
-    own = power.at[pl.ds(mine * per, per)]
-    second = [copies(i, own, own, send_b, recv_b) for i in range(1, groups)]
-    for copy in second:
-        copy.start()
-    for copy in second:
-        copy.wait_recv()
-
-    def finish(k, carry):
-        values, at = block(k)
-        made = [jnp.dot(values[:, side], power[k, n], preferred_element_type=F32) for n, side in enumerate((one, two))]
-        out[:, at] = jnp.concatenate(made, axis=1).astype(BF)
-        return carry
-
-    lax.fori_loop(0, count, finish, 0)
-    for copy in first + second:
-        copy.wait_send()
-
-
-def orthogonalize(mom, grad, hi, sh, number, name):
-    groups = hi * sh
-    count = mom.shape[1] // PAIR
-    per = -(-count // groups)
-    return call(
-        partial(ortho_kernel, hi, sh),
-        [(mom, False), (grad, False)],
-        [(jax.ShapeDtypeStruct(mom.shape, BF), False)],
-        [
-            pltpu.VMEM((groups * per, 2, HEAD, HEAD), BF),
-            pltpu.VMEM((groups - 1, per, 2, HEAD, HEAD), BF),
-            pltpu.VMEM((groups * per, 2, HEAD, HEAD), BF),
+    def grams(self):
+        one, two = slice(0, HEAD), slice(HEAD, PAIR)
+
+        def one_gram(k, carry):
+            values, _ = self.block(k)
+            made = lax.dot_general(values, values, (((0,), (0,)), ((), ())), preferred_element_type=F32)
+            self.gram[k, 0] = made[one, one].astype(BF)
+            self.gram[k, 1] = made[two, two].astype(BF)
+            return carry
+
+        lax.fori_loop(0, self.count, one_gram, 0)
+        for k in range(self.count, self.gram.shape[0]):
+            self.gram[k] = jnp.zeros((2, HEAD, HEAD), BF)
+        self.first = [
+            self.copy(i, self.gram.at[pl.ds(there * self.per, self.per)], self.arrived.at[i], self.send_a, self.recv_a)
+            for i, (there, _) in enumerate(self.peers)
         ]
-        + [pltpu.SemaphoreType.DMA((groups - 1,))] * 4,
-        number,
-        25,
-        name,
-    )[0]
+        for copy in self.first:
+            copy.start()
+
+    def iterate(self):
+        gram, arrived, per, mine = self.gram, self.arrived, self.per, self.mine
+        one, two = slice(0, HEAD), slice(HEAD, PAIR)
+        rows = lax.broadcasted_iota(jnp.int32, (PAIR, PAIR), 0)
+        columns = lax.broadcasted_iota(jnp.int32, (PAIR, PAIR), 1)
+        unit = jnp.where(rows == columns, 1.0, 0.0)
+        upper = (rows < HEAD) & (rows == columns)
+        lower = (rows >= HEAD) & (rows == columns)
+
+        def product(a, b):
+            a_high, b_high = a.astype(BF), b.astype(BF)
+            a_low, b_low = (a - a_high.astype(F32)).astype(BF), (b - b_high.astype(F32)).astype(BF)
+            made = jnp.dot(a_high, b_low, preferred_element_type=F32) + jnp.dot(a_low, b_high, preferred_element_type=F32)
+            return made + jnp.dot(a_high, b_high, preferred_element_type=F32)
+
+        for copy in self.first:
+            copy.wait_recv()
+        grams, wholes = [], []
+        for j in range(per):
+            halves = []
+            for n in range(2):
+                half = gram[mine * per + j, n].astype(F32)
+                for i in range(len(self.peers)):
+                    half = half + arrived[i, j, n].astype(F32)
+                halves.append(half)
+            empty = jnp.zeros((HEAD, HEAD), F32)
+            total = jnp.concatenate(
+                [jnp.concatenate([halves[0], empty], axis=1), jnp.concatenate([empty, halves[1]], axis=1)], axis=0
+            )
+
+            def scaling_of(chosen):
+                trace = jnp.sum(jnp.sum(jnp.where(chosen, total, 0.0), axis=1, keepdims=True), axis=0, keepdims=True)
+                return 1.0 / (jnp.sqrt(trace) + 1e-07)
+
+            scaling = jnp.where(rows < HEAD, scaling_of(upper), scaling_of(lower))
+            grams.append(total * (scaling * scaling))
+            wholes.append(scaling)
+        for number in range(NS_ITERS):
+            squares = [product(a, a) for a in grams]
+            steps = [COEF_A * unit + COEF_B * a + COEF_C * s for a, s in zip(grams, squares)]
+            wholes = [product(w, p) for w, p in zip(wholes, steps)] if number else [w * p for w, p in zip(wholes, steps)]
+            if number < NS_ITERS - 1:
+                grams = [product(product(a, p), p) for a, p in zip(grams, steps)]
+        for j in range(per):
+            self.power[mine * per + j, 0] = wholes[j][one, one].astype(BF)
+            self.power[mine * per + j, 1] = wholes[j][two, two].astype(BF)
+        own = self.power.at[pl.ds(mine * per, per)]
+        self.second = [self.copy(i, own, own, self.send_b, self.recv_b) for i in range(len(self.peers))]
+        for copy in self.second:
+            copy.start()
+
+    def finish(self):
+        one, two = slice(0, HEAD), slice(HEAD, PAIR)
+        for copy in self.second:
+            copy.wait_recv()
+
+        def last(k, carry):
+            values, at = self.block(k)
+            made = [
+                jnp.dot(values[:, side], self.power[k, n], preferred_element_type=F32) for n, side in enumerate((one, two))
+            ]
+            made = jnp.concatenate(made, axis=1).astype(BF)
+            self.out[:, :, at] = made.reshape(self.out.shape[0], self.out.shape[1], PAIR)
+            return carry
+
+        lax.fori_loop(0, self.count, last, 0)
+
+    def end(self):
+        for copy in self.first + self.second:
+            copy.wait_send()
+
+
+def ortho_scratch(groups, columns):
+    per = -(-(columns // PAIR) // groups)
+    return [
+        pltpu.VMEM((groups * per, 2, HEAD, HEAD), BF),
+        pltpu.VMEM((groups - 1, per, 2, HEAD, HEAD), BF),
+        pltpu.VMEM((groups * per, 2, HEAD, HEAD), BF),
+    ] + [pltpu.SemaphoreType.DMA((groups - 1,))] * 4
+
+
+def ortho_kernel(hi, sh, mom, grad, grad_back, ortho_back, ortho, *scratch):
+    meet_all(group_peers() + [peer for _, peer in row_peers(hi, sh)])
+    work = Orthogonal(hi, sh, mom, grad, ortho, scratch[:7])
+    grads = Swapping(grad, grad_back, *scratch[7:10])
+    orthos = Swapping(ortho, ortho_back, *scratch[10:13])
+    work.grams()
+    grads.start()
+    work.iterate()
+    work.finish()
+    orthos.start()
+    grads.end()
+    work.end()
+    orthos.end()
 
 
 def dot(spec, a, b, **kw):
@@ -686,7 +786,7 @@
     small = [pltpu.SemaphoreType.DMA((groups,))] * 2 + [pltpu.SemaphoreType.DMA((8,))] * 2
     normed_one, vec_rows, lengths = call(
         partial(first_kernel, hi, sh),
-        [(tokens, False), (piece, False), (cotangent, True)],
+        [(tokens, False), (piece, False)],
         [
             (gathered, True),
             (jax.ShapeDtypeStruct((16, d), F32), False),
@@ -719,8 +819,8 @@
         "attention",
     )
 
-    mom_attn, mom_mlp = [swap(part).reshape(tp * rows, -1) for part in arrange(momentum.astype(BF))]
-    normed_two, mom_attn, mom_mlp = lax.optimization_barrier((normed_two, mom_attn, mom_mlp))
+    normed_two, momentum_now = lax.optimization_barrier((normed_two, momentum))
+    send_attn, send_mlp = lax.optimization_barrier(arrange(momentum_now.astype(BF)))
 
     def rows_of(width):
         return (row_tokens, width), lambda r: (r, 0)
@@ -731,12 +831,12 @@
     def fixed(array):
         return array.shape, lambda r: (0,) * array.ndim
 
-    activated, grad_before = call(
+    activated, grad_before, mom_mlp = call(
         partial(mlp_kernel, hi, sh),
-        [(normed_two, row_of(d)), (cot_all, row_of(d)), (w_mlp, True), (vec_rows, fixed(vec_rows))],
-        [(jax.ShapeDtypeStruct((t_all, units), BF), rows_of(units))] * 2,
-        [pltpu.VMEM((d, units), BF)] * 2 + [pltpu.SemaphoreType.DMA((2,))],
-        None,
+        [(normed_two, row_of(d)), (cot_all, row_of(d)), (w_mlp, True), (vec_rows, fixed(vec_rows)), (send_mlp, True)],
+        [(jax.ShapeDtypeStruct((t_all, units), BF), rows_of(units))] * 2 + [(send_mlp, True)],
+        [pltpu.VMEM((d, units), BF)] * 2 + [pltpu.SemaphoreType.DMA((2,))] + swap_scratch(),
+        7,
         30,
         "hidden_units",
         grid=(tp,),
@@ -757,25 +857,27 @@
     grad_before, s_down, s_up = lax.optimization_barrier((grad_before, s_down, s_up))
     g_down, g_up = sent(s_down), sent(s_up)
 
-    grad_middle, sums_two, grad_branch = call(
+    grad_middle, sums_two, grad_branch, output = call(
         partial(branch_kernel, hi, sh),
-        [(grad_before, False), (w_mlp, True), (middle, False), (cotangent, False), (vec_rows, False)],
-        [(own_f32, False), (jax.ShapeDtypeStruct((4, 8, d), F32), False), (gathered, True)],
+        [(grad_before, False), (activated, False), (w_mlp, True), (middle, False), (cotangent, False), (vec_rows, False)],
+        [(own_f32, False), (jax.ShapeDtypeStruct((4, 8, d), F32), False), (gathered, True), (own_bf, False)],
         own_scratch
-        + [pltpu.VMEM((d, units), BF), pltpu.SemaphoreType.DMA]
+        + [pltpu.VMEM((d, units), BF)] * 2
+        + [pltpu.SemaphoreType.DMA((2,))]
         + sum_scratch(row_tokens, d)
-        + gather_scratch(),
+        + gather_scratch()
+        + sum_scratch(row_tokens, d),
         3,
-        95,
+        115,
         "second_norm_backward",
     )
     grad_branch, g_down = lax.optimization_barrier((grad_branch, g_down))
-    (grad_joined,) = call(
+    grad_joined, mom_attn = call(
         partial(attention_back_kernel, hi, sh),
-        [(grad_branch, row_of(d)), (w_attn, True), (qkv, row_of(3 * hc)), (lengths, fixed(lengths))],
-        [(jax.ShapeDtypeStruct((t_all, 3 * hc), BF), rows_of(3 * hc))],
-        [pltpu.VMEM((d, hc), BF), pltpu.SemaphoreType.DMA],
-        None,
+        [(grad_branch, row_of(d)), (w_attn, True), (qkv, row_of(3 * hc)), (lengths, fixed(lengths)), (send_attn, True)],
+        [(jax.ShapeDtypeStruct((t_all, 3 * hc), BF), rows_of(3 * hc)), (send_attn, True)],
+        [pltpu.VMEM((d, hc), BF), pltpu.SemaphoreType.DMA] + swap_scratch(),
+        8,
         25,
         "attention_backward",
         grid=(tp,),
@@ -783,31 +885,36 @@
     grad_branch = grad_branch.reshape(t_all, d)
     s_attn = summed([(flat_one, grad_joined), (grad_branch, attended)])
     grad_joined, s_attn = lax.optimization_barrier((grad_joined, s_attn))
-    g_attn = sent(s_attn)
-    g_mlp = jnp.concatenate([g_up, g_down], axis=1)
-    ortho_mlp = orthogonalize(mom_mlp, g_mlp, hi, sh, 5, "orthogonalize_mlp")
-    grad_joined, ortho_mlp = lax.optimization_barrier((grad_joined, ortho_mlp))
-    grad_tokens, sums_one, output = call(
+    g_attn = sent(s_attn).reshape(send_attn.shape)
+    g_mlp = jnp.concatenate([g_up, g_down], axis=1).reshape(send_mlp.shape)
+    grad_tokens, sums_one, back_mlp, ortho_mlp = call(
         partial(last_kernel, hi, sh),
-        [(grad_joined, False), (w_attn, True), (activated, False), (w_mlp, True)]
-        + [(tokens, False), (middle, False), (grad_middle, False), (vec_rows, False)],
-        [(own_f32, False), (jax.ShapeDtypeStruct((2, 8, d), F32), False), (own_bf, False)],
+        [(grad_joined, False), (w_attn, True), (tokens, False), (grad_middle, False), (vec_rows, False)]
+        + [(mom_mlp, False), (g_mlp, False)],
+        [(own_f32, False), (jax.ShapeDtypeStruct((2, 8, d), F32), False), (send_mlp, True), (send_mlp, True)],
         own_scratch[:1]
-        + [pltpu.VMEM((d, 3 * hc), BF), pltpu.VMEM((d, units), BF), pltpu.SemaphoreType.DMA((2,))]
-        + sum_scratch(row_tokens, d) * 2,
+        + [pltpu.VMEM((d, 3 * hc), BF), pltpu.SemaphoreType.DMA, pltpu.VMEM(send_mlp.shape, BF)]
+        + sum_scratch(row_tokens, d)
+        + ortho_scratch(groups, send_mlp.shape[2])
+        + swap_scratch() * 2,
         4,
-        85,
+        75,
         "first_norm_backward",
     )
-    grad_tokens, output, g_attn = lax.optimization_barrier((grad_tokens, output, g_attn))
-
-    def back(part):
-        return swap(part.reshape(tp, rows, -1))
-
-    weight_grad = restore(back(g_attn), back(g_mlp)).astype(F32)
+    grad_tokens, g_attn = lax.optimization_barrier((grad_tokens, g_attn))
+
+    back_attn, ortho_attn = call(
+        partial(ortho_kernel, hi, sh),
+        [(mom_attn, False), (g_attn, False)],
+        [(send_attn, True), (send_attn, True)],
+        [pltpu.VMEM(send_attn.shape, BF)] + ortho_scratch(groups, send_attn.shape[2]) + swap_scratch() * 2,
+        6,
+        30,
+        "orthogonalize_attention",
+    )
+    weight_grad = restore(back_attn, back_mlp).astype(F32)
     moment_new = 0.95 * momentum + weight_grad
-    ortho_attn = orthogonalize(mom_attn, g_attn, hi, sh, 6, "orthogonalize_attention")
-    orthogonal_rows = restore(back(ortho_attn), back(ortho_mlp)).astype(F32)
+    orthogonal_rows = restore(ortho_attn, ortho_mlp).astype(F32)
     new_weights = weights * (1.0 - 0.15 * 0.1) - 0.15 * 0.2 * math.sqrt(d) * orthogonal_rows
 
     sums_one, sums_two = jnp.sum(sums_one, axis=1), jnp.sum(sums_two, axis=1)

time: 844 us -> 698 us (0.83)
  waiting for transfers between devices: 50.5 us -> 5.42 us
  Pallas kernels: 534 us -> 496 us
  starting transfers between devices: 35.6 us -> 5.92 us
  blocking collectives: 79.4 us -> 49.8 us
    all_to_all x5 -> x0, waiting for transfers between devices: 39 us -> none  [swap(): return lax.all_to_all(array, 'tp', split_axis=0, concat_axis=0, tiled=True)]
    pallas_call x8 -> x7, Pallas kernels: 534 us -> 496 us  [call(): pl.pallas_call(body, out_shape=[jax.ShapeDtypeStruct(s.shape, s.dtype) fo...]
    all_to_all x3 -> x2, blocking collectives: 79.4 us -> 49.8 us  [swap(): return lax.all_to_all(array, 'tp', split_axis=0, concat_axis=0, tiled=True)]
    all_to_all x5 -> x0, starting transfers between devices: 29.3 us -> none  [swap(): return lax.all_to_all(array, 'tp', split_axis=0, concat_axis=0, tiled=True)]
  transfers between devices with their start and end apart: 11 -> 6, of which waited for: 5 -> 1; matrix products, arithmetic and copies ran while one was open for 8% -> 9% of each run, Pallas kernels for 60% -> 62%
where the time goes in v4:
time: 698 us; the launch traced here: 695 us
  Pallas kernels  496 us (71%)
  local copies, waits for them, and re-layouts  54.2 us (8%)
  blocking collectives  49.8 us (7%)
  matrix products  39.9 us (6%)
  other arithmetic  28.6 us (4%)
  between operations  14.5 us (2%)
    pallas_call x7, Pallas kernels, call(): pl.pallas_call(body, out_shape=[jax.ShapeDtypeStruct(s.shape, s.dtype) fo...  496 us
    all_to_all x2, blocking collectives, swap(): return lax.all_to_all(array, 'tp', split_axis=0, concat_axis=0, tiled=True)  49.8 us
    dot_general x4, matrix products, dot(): return jnp.einsum(spec, a, b, preferred_element_type=F32, **kw)  39.9 us
  transfers between devices with their start and end apart: 6, of which 1 were waited for; matrix products, arithmetic and copies ran while one was open for 9% of the time, Pallas kernels for 62%

profile of v4, /device:TPU:27, one launch (start us, length us, event | category | flops | bytes accessed | tf_op | source)
XLA Modules:
  0.0 694.6 jit_solution(8307858729005298065)
XLA Ops:
  7.2 3.4 convert_element_type.39
  10.7 1.8 copy.74
  12.4 2.6 reshape.156
  15.0 18.7 %all_to_all.20 = bf16[8,64,1024]{2,1,0:T(8,128)(2,1)} all-to-all(bf16[8,64,1024]{2,1,0:T(8,128)(2,1)} %reshape.156), channel_id=1, replica_groups=mesh['dp'=8,'shard'=4] {'dp'}, dimensions={0} | all-to-all | bytes 2097152 | tf_op jit(solution)/shard_map/all_to_all | solution.py:763
  34.4 2.3 reshape.154
  36.6 31.1 %all_to_all.21 = bf16[8,64,2048]{2,1,0:T(8,128)(2,1)} all-to-all(bf16[8,64,2048]{2,1,0:T(8,128)(2,1)} %reshape.154), channel_id=1, replica_groups=mesh['dp'=8,'shard'=4] {'dp'}, dimensions={0} | all-to-all | bytes 4194304 | tf_op jit(solution)/shard_map/all_to_all | solution.py:763
  68.1 0.6 fusion.3.piece
  68.7 54.7 %first_norm.1 = (bf16[8,256,2048]{2,1,0:T(8,128)(2,1)}, f32[16,2048]{1,0:T(8,128)}, f32[8,128]{1,0:T(8,128)}) custom-call(bf16[256,2048]{1,0:T(8,128)(2,1)} %tok.2, bf16[16,128]{1,0:T(8,128)(2,1)} %fusion.3.piece), custom_call_target="tpu_custom_call" | custom-call | bytes 150000000 | tf_op jit(solution)/shard_map/first_norm/pallas_call | solution.py:543
  123.5 121.5 %attention.1 = (f32[256,2048]{1,0:T(8,128)}, bf16[8,256,2048]{2,1,0:T(8,128)(2,1)}, bf16[8,256,2048]{2,1,0:T(8,128)(2,1)}, bf16[8,256,768]{2,1,0:T(8,128)(2,1)}, bf16[2048,256]{1,0:T(8,128)(2,1)}) custom-call(bf16[8,256,2048]{2,1,0:T(8,128)(2,1)} %get-tuple-element.47.normed, bf16[4,8,64,1024]{3,2,1,0:T(8,128)(2,1)} %bitcast.80, ...), custom_call_target="tpu_custom_call" | custom-call | bytes 330000000 | tf_op jit(solution)/shard_map/attention/pallas_call | solution.py:543
  245.0 3.3 convert_element_type.41
  248.5 2.1 copy.71
  250.7 4.2 reshape.160.mom
  255.0 0.7 copy.73
  255.7 1.5 reshape.158.mom
  257.3 4.8 all-gather.7.cloned.1.call-done
  262.0 29.9 %hidden_units.1 = (bf16[2048,1024]{1,0:T(8,128)(2,1)}, bf16[2048,1024]{1,0:T(8,128)(2,1)}, bf16[8,64,2048]{2,1,0:T(8,128)(2,1)}) custom-call(bf16[8,256,2048]{2,1,0:T(8,128)(2,1)} %get-tuple-element.51.normed, bf16[8,256,2048]{2,1,0:T(8,128)(2,1)} %get-tuple-element.52.cot, bf16[4,8,64,2048]{3,2,1,0:T(8,128)(2,1)} %bitcast.83, ...), custom_call_target="tpu_custom_call" | custom-call | bytes 90000000 | tf_op jit(solution)/shard_map/hidden_units/pallas_call | solution.py:543
  291.9 12.9 %convolution_convert_fusion = bf16[2048,1024]{1,0:T(8,128)(2,1)S(1)} fusion(bf16[2048,2048]{1,0:T(8,128)(2,1)} %bitcast.95, bf16[2048,1024]{1,0:T(8,128)(2,1)} %get-tuple-element.58.grad_before), kind=kOutput, calls=%fused_computation.4 | convolution fusion | flops 8592031744 | bytes 16777216 | tf_op jit(solution)/shard_map/td,tn->dn/dot_general | solution.py:737
  304.9 2.6 copy.56
  307.4 1.1 copy-done.3
  308.5 11.5 %convolution_convert_fusion.1 = bf16[2048,1024]{1,0:T(8,128)(2,1)S(1)} fusion(bf16[2048,2048]{1,0:T(8,128)(2,1)} %bitcast.94, bf16[2048,1024]{1,0:T(8,128)(2,1)S(1)} %copy-done.3), kind=kOutput, calls=%fused_computation.5 | convolution fusion | flops 8592031744 | bytes 16777216 | tf_op jit(solution)/shard_map/td,tn->dn/dot_general | solution.py:737
  320.1 2.5 copy.55
  323.2 131.6 %second_norm_backward.1 = (f32[256,2048]{1,0:T(8,128)}, f32[4,8,2048]{2,1,0:T(8,128)}, bf16[8,256,2048]{2,1,0:T(8,128)(2,1)}, bf16[256,2048]{1,0:T(8,128)(2,1)}) custom-call(bf16[2048,1024]{1,0:T(8,128)(2,1)} %get-tuple-element.58.grad_before, bf16[2048,1024]{1,0:T(8,128)(2,1)} %get-tuple-element.57.activated, bf16[4,8,64,2048]{3,2,1,0:T(8,128)(2,1)} %bitcast.84, ...), custom_call_target="tpu_custom_call" | custom-call | bytes 345000000 | tf_op jit(solution)/shard_map/second_norm_backward/pallas_call | solution.py:543
  454.8 19.9 %attention_backward.1 = (bf16[2048,768]{1,0:T(8,128)(2,1)}, bf16[8,64,1024]{2,1,0:T(8,128)(2,1)}) custom-call(bf16[8,256,2048]{2,1,0:T(8,128)(2,1)} %get-tuple-element.63.branch, bf16[4,8,64,1024]{3,2,1,0:T(8,128)(2,1)} %bitcast.81, bf16[8,256,768]{2,1,0:T(8,128)(2,1)} %get-tuple-element.64.qkv, f32[8,128]{1,0:T(8,128)} %get-tuple-element.48.lengths, ...), custom_call_target="tpu_custom_call" | custom-call | bytes 75000000 | tf_op jit(solution)/shard_map/attention_backward/pallas_call | solution.py:543
  474.7 6.1 convolution_convert_fusion.3
  480.9 9.3 %convolution_convert_fusion.2 = bf16[2048,768]{0,1:T(8,128)(2,1)S(1)} fusion(bf16[2048,2048]{1,0:T(8,128)(2,1)} %bitcast.93, bf16[2048,768]{1,0:T(8,128)(2,1)S(1)} %copy-done.1), kind=kOutput, calls=%fused_computation.6 | convolution fusion | flops 6444023808 | bytes 14680064 | tf_op jit(solution)/shard_map/td,tn->dn/dot_general | solution.py:737
  490.2 2.3 pad_maximum_fusion
  492.6 6.4 copy.57
  498.9 4.9 copy.58
  504.0 0.8 copy-done.8
  504.9 2.9 convert_reduce_fusion
  508.2 2.7 pad_maximum_fusion.1.grad
  510.9 100.6 %first_norm_backward.1 = (f32[256,2048]{1,0:T(8,128)}, f32[2,8,2048]{2,1,0:T(8,128)}, bf16[8,64,2048]{2,1,0:T(8,128)(2,1)}, bf16[8,64,2048]{2,1,0:T(8,128)(2,1)}) custom-call(bf16[2048,768]{1,0:T(8,128)(2,1)} %get-tuple-element.68.grad_joined, bf16[4,8,64,1024]{3,2,1,0:T(8,128)(2,1)} %bitcast.82, bf16[256,2048]{1,0:T(8,128)(2,1)} %tok.2, ...), custom_call_target="tpu_custom_call" | custom-call | bytes 225000000 | tf_op jit(solution)/shard_map/first_norm_backward/pallas_call | solution.py:543
  611.5 1.0 reduce_sum.54
  613.6 0.8 all_to_all.16
  614.4 5.5 all-to-all-start.2
  620.0 2.4 copy.65
  622.3 0.6 copy.60
  623.0 0.6 copy.66
  623.6 1.9 copy.62
  625.7 0.6 divide_subtract_fusion
  626.3 38.0 %orthogonalize_attention.1 = (bf16[8,64,1024]{2,1,0:T(8,128)(2,1)}, bf16[8,64,1024]{2,1,0:T(8,128)(2,1)}) custom-call(bf16[8,64,1024]{2,1,0:T(8,128)(2,1)} %get-tuple-element.76.mom, bf16[8,64,1024]{2,1,0:T(8,128)(2,1)} %bitcast.113), custom_call_target="tpu_custom_call" | custom-call | bytes 90000000 | tf_op jit(solution)/shard_map/orthogonalize_attention/pallas_call | solution.py:543
  664.3 2.6 reshape.171
  666.9 2.4 copy.59
  669.3 2.6 reshape.175
  671.9 2.4 copy.61
  674.3 11.2 %multiply_add_fusion = (f32[64,192,128]{2,1,0:T(8,128)}, f32[64,192,128]{2,1,0:T(8,128)}, f32[64,192,128]{2,1,0:T(8,128)}) fusion(f32[64,192,128]{2,1,0:T(8,128)} %param.11, bf16[64,128,128]{2,1,0:T(8,128)(2,1)S(1)} %bitcast.91, bf16[64,64,128]{2,1,0:T(8,128)(2,1)S(1)} %bitcast.102, bf16[64,128,128]{2,1,0:T(8,128)(2,1)} %bitcast.92, ...), kind=kLoop, calls=%fused_computation.1 | loop fusion | flops 20447232 | bytes 37748736 | tf_op jit(solution)/shard_map/add | solution.py:916
  685.5 1.0 copy.80
  686.5 1.3 copy.81
  (66 shorter events, 3.8 us)
Async XLA Ops:
  7.2 116.3 %all-gather.5.cloned.1.call-start = ((), (), s32[]{:S(2)}) async-start(), calls=%async_computation.9 | async-start | bytes 5242880 | tf_op jit(solution)/shard_map/all_gather | solution.py:768
  33.8 228.3 %all-gather.7.cloned.1.call-start = ((), (), s32[]{:S(2)}) async-start(), calls=%async_computation.10 | async-start | bytes 10485760 | tf_op jit(solution)/shard_map/all_gather | solution.py:768
  36.6 31.3 %copy-start.9 = (f32[64,12]{0,1:T(8,128)S(1)}, f32[64,12]{0,1:T(8,128)}, u32[]{:S(2)}) copy-start(f32[64,12]{0,1:T(8,128)} %param.12) | copy-start | bytes 9220
  36.6 31.5 %copy-start.12 = (s32[1,4]{1,0:T(1,128)S(1)}, s32[1,4]{1,0:T(1,128)}, u32[]{:S(2)}) copy-start(s32[1,4]{1,0:T(1,128)} %param.9) | copy-start | bytes 52
  67.8 387.1 %reduce-scatter.4.cloned.1.call-start = ((), (), s32[]{:S(2)}) async-start(), calls=%async_computation.6 | async-start | bytes 5242880 | tf_op jit(solution)/shard_map/reduce_scatter | solution.py:853
  248.4 2.4 copy-start
  250.7 4.2 slice-start
  304.8 3.7 copy-start.3
  322.6 185.6 %reduce-scatter.6.cloned.1.call-start = ((), (), s32[]{:S(2)}) async-start(), calls=%async_computation.7 | async-start | bytes 5242880 | tf_op jit(solution)/shard_map/reduce_scatter | solution.py:853
  323.1 303.2 %reduce-scatter.8.cloned.1.call-start = ((), (), s32[]{:S(2)}) async-start(), calls=%async_computation.8 | async-start | bytes 5242880 | tf_op jit(solution)/shard_map/reduce_scatter | solution.py:853
  474.7 6.1 copy-start.1
  503.9 0.9 copy-start.8
  503.9 4.3 copy-start.7
  510.9 101.6 %copy-start.2 = (bf16[2048,768]{1,0:T(8,128)(2,1)S(1)}, bf16[2048,768]{1,0:T(8,128)(2,1)}, u32[]{:S(2)}) copy-start(bf16[2048,768]{1,0:T(8,128)(2,1)} %get-tuple-element.68.grad_joined) | copy-start | bytes 9437188
  614.4 11.1 %all-to-all-start.2 = ((f32[32,1,768]{2,1,0:T(1,128)}), f32[32,1,768]{2,1,0:T(1,128)S(1)}, u32[]{:S(2)}, u32[]{:S(2)}) async-start(f32[32,1,768]{2,1,0:T(1,128)} %all_to_all.16), calls=%async_computation.5 | async-start | bytes 196608 | tf_op jit(solution)/shard_map/all_to_all | solution.py:940
  620.0 3.0 copy-start.5
  623.0 2.7 copy-start.10
  623.0 2.7 copy-start.11
  674.2 11.2 %copy-start.6 = (bf16[256,2048]{1,0:T(8,128)(2,1)S(1)}, bf16[256,2048]{1,0:T(8,128)(2,1)}, u32[]{:S(2)}) copy-start(bf16[256,2048]{1,0:T(8,128)(2,1)} %get-tuple-element.102) | copy-start | bytes 3145732
  674.2 12.2 %copy-start.4 = (f32[256,2048]{1,0:T(8,128)S(1)}, f32[256,2048]{1,0:T(8,128)}, u32[]{:S(2)}) copy-start(f32[256,2048]{1,0:T(8,128)} %get-tuple-element.103) | copy-start | bytes 6291460
Sparse Core Ops, SparseCore 0:
  33.9 78.7 all-gather.4
  114.2 147.7 all-gather.6
  322.7 76.7 reduce-scatter.3
  402.3 77.2 reduce-scatter.5
  504.0 93.0 reduce-scatter.7

commit v5 on v4

--- a/solution.py
+++ b/solution.py
@@ -72,7 +72,6 @@
         self.part, self.from_c, self.from_1, self.from_2, self.send, self.recv = scratch
         self.count = self.part.shape[0]
         self.rows = self.part.shape[4]
-        self.copies = {}
 
     def fill(self, k):
         right = self.right[k * WIDE : (k + 1) * WIDE, :]
@@ -85,10 +84,18 @@
 
         lax.fori_loop(0, 8, one, 0)
 
-    def begin(self, stage, k, src, dst, peer):
-        copy = remote(src, dst, self.send.at[stage, k], self.recv.at[stage, k], peer)
-        copy.start()
-        self.copies[stage, k] = copy
+    def copy(self, stage, k, at):
+        me, c, x, y, pc, px, py = at
+        even = k % 2 == 0
+        if stage == 0:
+            src, dst, peer = self.part.at[k, :, :, 1 - c], self.from_c.at[k], pc
+        elif stage == 1:
+            src = self.part.at[k, :, 1 - x, c] if even else self.part.at[k, 1 - y, :, c]
+            dst, peer = self.from_1.at[k], px if even else py
+        else:
+            src = self.part.at[k, 1 - y, x, c] if even else self.part.at[k, y, 1 - x, c]
+            dst, peer = self.from_2.at[k], py if even else px
+        return remote(src, dst, self.send.at[stage, k], self.recv.at[stage, k], peer)
 
     def run(self):
         self.first()
@@ -96,52 +103,49 @@
         self.third()
 
     def first(self):
-        me, c, x, y, pc, px, py = spots()
-        oc, ox, oy = 1 - c, 1 - x, 1 - y
+        at = spots()
+        c = at[1]
         part = self.part
 
         def core_stage(k):
-            self.copies[0, k].wait_recv()
+            self.copy(0, k, at).wait_recv()
             for i in range(4):
                 a, b = i // 2, i % 2
                 part[k, a, b, c] = (part[k, a, b, c].astype(F32) + self.from_c[k, a, b].astype(F32)).astype(BF)
-            if k % 2 == 0:
-                self.begin(1, k, part.at[k, :, ox, c], self.from_1.at[k], px)
-            else:
-                self.begin(1, k, part.at[k, oy, :, c], self.from_1.at[k], py)
+            self.copy(1, k, at).start()
 
         for k in range(self.count):
             self.fill(k)
-            self.begin(0, k, part.at[k, :, :, oc], self.from_c.at[k], pc)
+            self.copy(0, k, at).start()
             if k:
                 core_stage(k - 1)
         core_stage(self.count - 1)
 
     def second(self):
-        me, c, x, y, pc, px, py = spots()
-        ox, oy = 1 - x, 1 - y
+        at = spots()
+        _, c, x, y = at[:4]
         part = self.part
         for k in range(self.count):
-            self.copies[1, k].wait_recv()
+            self.copy(1, k, at).wait_recv()
             for i in range(2):
                 if k % 2 == 0:
                     part[k, i, x, c] = (part[k, i, x, c].astype(F32) + self.from_1[k, i].astype(F32)).astype(BF)
                 else:
                     part[k, y, i, c] = (part[k, y, i, c].astype(F32) + self.from_1[k, i].astype(F32)).astype(BF)
-            if k % 2 == 0:
-                self.begin(2, k, part.at[k, oy, x, c], self.from_2.at[k], py)
-            else:
-                self.begin(2, k, part.at[k, y, ox, c], self.from_2.at[k], px)
+            self.copy(2, k, at).start()
 
     def third(self):
-        me, c, x, y, pc, px, py = spots()
+        at = spots()
+        _, c, x, y = at[:4]
         for k in range(self.count):
-            self.copies[2, k].wait_recv()
+            self.copy(2, k, at).wait_recv()
             self.total[:, k * WIDE : (k + 1) * WIDE] = self.part[k, y, x, c].astype(F32) + self.from_2[k].astype(F32)
 
     def end(self):
-        for copy in self.copies.values():
-            copy.wait_send()
+        at = spots()
+        for stage in range(3):
+            for k in range(self.count):
+                self.copy(stage, k, at).wait_send()
 
 
 class Gathering:
@@ -331,13 +335,15 @@
 
 
 def attention_kernel(
-    hi, sh, normed, w_any, lengths, vec, tok, cot, middle, normed_all, cot_all, qkv, att, total, own, w, w_sem, *scratch
+    hi, sh, normed, w_any, lengths, vec, tok, cot, mom, middle, normed_all, cot_all, qkv, att, mom_out, total, own, w,
+    w_sem, *scratch
 ):
     me, c, x, y, pc, px, py = spots()
     fetch_rows(w_any, 0, w, w_sem, hi, sh)
-    meet((pc, px, py))
-    spread_cot = Gathering(cot, cot_all, *scratch[9:])
+    meet_all(group_peers())
+    spread_cot = Gathering(cot, cot_all, *scratch[9:12])
     spread_cot.start()
+    swapped = Swapping(mom, mom_out, *scratch[12:])
     size = own.shape[0]
     hc = att.shape[1]
     fetched(w, w_sem)
@@ -363,6 +369,7 @@
     sums = Summing(att, w.at[:, 3 * hc :], total, scratch[:6])
     sums.first()
     spread_cot.forward()
+    swapped.start()
     sums.second()
     sums.third()
 
@@ -379,6 +386,7 @@
     sums.end()
     spread_cot.end()
     spread.end()
+    swapped.end()
 
 
 GELU_A = math.sqrt(2.0 / math.pi)
@@ -416,8 +424,10 @@
         swapped.end()
 
 
-def attention_back_kernel(hi, sh, branch, w_any, qkv, lengths, mom, grad_joined, mom_out, w, sem, *scratch):
-    swapped = Swapping(mom, mom_out, *scratch)
+def attention_back_kernel(
+    hi, sh, branch, w_any, qkv, lengths, grad_down, grad_joined, back_down, w, sem, *scratch
+):
+    swapped = Swapping(grad_down, back_down, *scratch)
     hc = w.shape[1]
     size = branch.shape[1]
     r = pl.program_id(0)
@@ -499,19 +509,28 @@
 
 
 def last_kernel(
-    hi, sh, grad_joined, w_attn, tok, grad_middle, vec, mom, grad, grad_tokens, sums_out, grad_back, ortho_back, total,
-    w_qkv, w_sem, ortho, *scratch
+    hi, sh, grad_joined, w_attn, tok, grad_middle, vec, mom, grad_up, grad_down, grad_tokens, sums_out, back_up, ortho_back,
+    total, w_qkv, w_sem, grad, grad_sems, ortho, *scratch
 ):
     fetch_rows(w_attn, 0, w_qkv, w_sem, hi, sh)
+    width = grad_up.shape[2]
+    loads = [
+        pltpu.make_async_copy(part, grad.at[:, :, pl.ds(n * width, width)], grad_sems.at[n])
+        for n, part in enumerate((grad_up, grad_down))
+    ]
+    for load in loads:
+        load.start()
     meet_all(group_peers() + [peer for _, peer in row_peers(hi, sh)])
     work = Orthogonal(hi, sh, mom, grad, ortho, scratch[6:13])
-    grads = Swapping(grad, grad_back, *scratch[13:16])
+    ups = Swapping(grad_up, back_up, *scratch[13:16])
     orthos = Swapping(ortho, ortho_back, *scratch[16:19])
     sums = Summing(grad_joined, w_qkv, total, scratch[:6])
+    fetched(w_qkv, w_sem)
+    for load in loads:
+        load.wait()
     work.grams()
-    fetched(w_qkv, w_sem)
     sums.first()
-    grads.start()
+    ups.start()
     work.iterate()
     sums.second()
     work.finish()
@@ -528,9 +547,52 @@
 
     row_loop(total.shape[0], body)
     sums.end()
-    grads.end()
+    ups.end()
     work.end()
     orthos.end()
+
+
+def outer_kernel(*refs):
+    *pairs, out = refs
+    _, sh, some, rows, _ = out.shape
+    first = 0
+    for left, right in zip(pairs[::2], pairs[1::2]):
+        made = lax.dot_general(
+            left[...].reshape(-1, left.shape[-1]), right[...], (((0,), (0,)), ((), ())), preferred_element_type=F32
+        ).astype(BF)
+        n = right.shape[1]
+        for a in range(some):
+            for s in range(sh):
+                at = (a * sh + s) * rows
+                out[0, s, a, :, first : first + n] = made[at : at + rows]
+        first += n
+
+
+def outer(pairs, hi, sh, name):
+    tp, tokens, d = pairs[0][0].shape
+    n = sum(right.shape[1] for _, right in pairs)
+    rows = d // (hi * tp * sh)
+    some = 256 // (sh * rows)
+    turns = tp // some
+    ins = []
+    for left, right in pairs:
+        ins += [(left, ((tp, tokens, 256), lambda i: (0, 0, i))), (right, (right.shape, lambda i: (0, 0)))]
+    (made,) = call(
+        outer_kernel,
+        ins,
+        [
+            (
+                jax.ShapeDtypeStruct((hi, sh, tp, rows, n), BF),
+                ((1, sh, some, rows, n), lambda i: (i // turns, 0, i % turns, 0, 0)),
+            )
+        ],
+        [],
+        None,
+        n / 70,
+        name,
+        grid=(d // 256,),
+    )
+    return made.reshape(hi * sh, tp * rows, n)
 
 
 def call(body, ins, outs, scratch, number, microseconds, name, grid=None):
@@ -718,23 +780,155 @@
     ] + [pltpu.SemaphoreType.DMA((groups - 1,))] * 4
 
 
-def ortho_kernel(hi, sh, mom, grad, grad_back, ortho_back, ortho, *scratch):
+class Terms:
+    def __init__(self, hi, sh, terms, got_a, summed, got_b, send_a, recv_a, send_b, recv_b):
+        self.hi, self.sh, self.terms, self.got_a, self.summed, self.got_b = hi, sh, terms, got_a, summed, got_b
+        self.sems = send_a, recv_a, send_b, recv_b
+        self.rows = terms.shape[1] // (8 * hi * sh)
+        self.wide = summed.shape[2]
+
+    def columns(self, h, t):
+        start = (h * 8 + t) * self.sh * self.rows // 128 * 128
+        return pl.ds(pl.multiple_of(start, 128), self.wide)
+
+    def start(self):
+        me = lax.axis_index("tp")
+        self.first = []
+        for i in range(1, 8):
+            peer = rem(me + i, 8)
+            for h in range(self.hi):
+                n = (i - 1) * self.hi + h
+                self.first.append(
+                    remote(
+                        self.terms.at[:, self.columns(h, peer)], self.got_a.at[i - 1, h],
+                        self.sems[0].at[n], self.sems[1].at[n], peer,
+                    )
+                )
+        for copy in self.first:
+            copy.start()
+
+    def middle(self):
+        me = lax.axis_index("tp")
+        for copy in self.first:
+            copy.wait_recv()
+        for h in range(self.hi):
+            value = self.terms[:, self.columns(h, me)]
+            for i in range(7):
+                value = value + self.got_a[i, h]
+            self.summed[h] = value
+        self.second = []
+        for j, (there, peer) in enumerate(row_peers(self.hi, self.sh)):
+            self.second.append(
+                pltpu.make_async_remote_copy(
+                    src_ref=self.part(there), dst_ref=self.got_b.at[j], send_sem=self.sems[2].at[j],
+                    recv_sem=self.sems[3].at[j], device_id=peer, device_id_type=MESH,
+                )
+            )
+        for copy in self.second:
+            copy.start()
+
+    def part(self, there):
+        at = pl.multiple_of(div(rem(there, self.sh) * self.rows, 128) * 128, 128)
+        return self.summed.at[div(there, self.sh), :, pl.ds(at, 128)]
+
+    def end(self, out):
+        mine = lax.axis_index("hi") * self.sh + lax.axis_index("shard")
+        for copy in self.second:
+            copy.wait_recv()
+        value = self.part(mine)[...]
+        for j in range(len(self.second)):
+            value = value + self.got_b[j]
+        out[...] = value
+        for copy in self.first + self.second:
+            copy.wait_send()
+
+
+def terms_scratch(hi, sh, d):
+    groups = hi * sh
+    wide = max(128, d // 8 // hi)
+    return [
+        pltpu.VMEM((16, d), F32),
+        pltpu.VMEM((7, hi, 16, wide), F32),
+        pltpu.VMEM((hi, 16, wide), F32),
+        pltpu.VMEM((groups - 1, 16, 128), F32),
+    ] + [pltpu.SemaphoreType.DMA((7 * hi,))] * 2 + [pltpu.SemaphoreType.DMA((groups - 1,))] * 2
+
+
+def ortho_kernel(hi, sh, mom, grad, early, sums_one, grad_back, ortho_back, vector_grad, ortho, *scratch):
     meet_all(group_peers() + [peer for _, peer in row_peers(hi, sh)])
     work = Orthogonal(hi, sh, mom, grad, ortho, scratch[:7])
     grads = Swapping(grad, grad_back, *scratch[7:10])
     orthos = Swapping(ortho, ortho_back, *scratch[10:13])
+    terms = Terms(hi, sh, *scratch[13:])
     work.grams()
+    terms.terms[...] = early[...]
+    for n in range(2):
+        terms.terms[n : n + 1, :] = jnp.sum(sums_one[n], axis=0, keepdims=True)
+    terms.start()
     grads.start()
     work.iterate()
+    terms.middle()
     work.finish()
     orthos.start()
+    terms.end(vector_grad)
     grads.end()
     work.end()
     orthos.end()
 
 
-def dot(spec, a, b, **kw):
-    return jnp.einsum(spec, a, b, preferred_element_type=F32, **kw)
+def update_kernel(
+    weights, momentum, back_attn, ortho_attn, back_up, back_down, ortho_up, ortho_down, weight_grad, new_weights, new_momentum
+):
+    rows, each, _ = weights.shape
+    flat = [ref.reshape(rows * each, HEAD) for ref in (weights, momentum, weight_grad, new_weights, new_momentum)]
+    step = 0.15 * 0.2 * math.sqrt(2048)
+    i = pl.program_id(0)
+
+    def blocks(back, ortho):
+        inside = back.shape[2] // HEAD
+        for b in range(each):
+            to = pl.ds(b, rows, each)
+            at = slice(b % inside * HEAD, (b % inside + 1) * HEAD)
+            grad = back[b // inside, :, at].astype(F32)
+            flat[2][to, :] = grad
+            flat[4][to, :] = 0.95 * flat[1][to, :] + grad
+            flat[3][to, :] = flat[0][to, :] * (1.0 - 0.15 * 0.1) - step * ortho[b // inside, :, at].astype(F32)
+
+    @pl.when(i < 4)
+    def _():
+        blocks(back_attn, ortho_attn)
+
+    @pl.when((i >= 4) & (i < 8))
+    def _():
+        blocks(back_up, ortho_up)
+
+    @pl.when(i >= 8)
+    def _():
+        blocks(back_down, ortho_down)
+
+
+def update(weights, momentum, back_attn, ortho_attn, back_up, back_down, ortho_mlp):
+    rows, blocks, head = weights.shape
+    tp = back_attn.shape[0]
+    width = back_attn.shape[2] // 4
+    units = back_up.shape[2]
+    some = HEADS * head // units
+    whole = (weights, ((rows, HEADS, head), lambda i: (0, i, 0)))
+    attn = ((tp, rows, width), lambda i: (0, 0, jnp.minimum(i, 3)))
+    ups = ((some, rows, units), lambda i: (jnp.clip(i - 4, 0, 3), 0, 0))
+    downs = ((some, rows, units), lambda i: (jnp.maximum(i - 8, 0), 0, 0))
+    ortho_downs = ((some, rows, units), lambda i: (jnp.maximum(i - 8, 0), 0, 1))
+    return call(
+        update_kernel,
+        [whole, (momentum, whole[1]), (back_attn, attn), (ortho_attn, attn)]
+        + [(back_up, ups), (back_down, downs), (ortho_mlp, ups), (ortho_mlp, ortho_downs)],
+        [whole] * 3,
+        [],
+        None,
+        15,
+        "update",
+        grid=(blocks // HEADS,),
+    )
 
 
 def local(tokens, doc_lengths, weights, momentum, vectors, vector_moment, vector_second, cotangent):
@@ -750,19 +944,14 @@
     t_all = tp * row_tokens
 
     def arrange(array):
-        attn = array[:, : 4 * HEADS].reshape(rows, 4, tp, heads, head).transpose(2, 0, 1, 3, 4).reshape(tp, rows, attn_blocks * head)
-        mlp = array[:, 4 * HEADS :].reshape(rows, 2, tp, inner, head).transpose(2, 0, 1, 3, 4).reshape(tp, rows, 2 * inner * head)
+        attn = array[:, : 4 * HEADS].astype(BF).reshape(rows, 4, tp, heads, head).transpose(2, 0, 1, 3, 4).reshape(tp, rows, attn_blocks * head)
+        mlp = array[:, 4 * HEADS :].astype(BF).reshape(rows, 2, tp, inner, head).transpose(2, 0, 1, 3, 4).reshape(tp, rows, 2 * inner * head)
         return attn, mlp
-
-    def restore(attn, mlp):
-        attn = attn.reshape(tp, rows, 4, heads, head).transpose(1, 2, 0, 3, 4).reshape(rows, 4 * HEADS, head)
-        mlp = mlp.reshape(tp, rows, 2, inner, head).transpose(1, 2, 0, 3, 4).reshape(rows, 2 * inner_all, head)
-        return jnp.concatenate([attn, mlp], axis=1)
 
     def swap(array):
         return lax.all_to_all(array, "tp", split_axis=0, concat_axis=0, tiled=True)
 
-    attn_send, mlp_send = arrange(weights.astype(BF))
+    attn_send, mlp_send = arrange(weights)
 
     def spread(array):
         return lax.all_gather(array, FS, axis=0, tiled=False)
@@ -800,27 +989,29 @@
 
     hc = heads * head
     units = inner * head
-    middle, normed_two, cot_all, qkv, attended = call(
+    normed_one, momentum_now = lax.optimization_barrier((normed_one, momentum))
+    send_attn, send_mlp = arrange(momentum_now)
+    middle, normed_two, cot_all, qkv, attended, mom_attn = call(
         partial(attention_kernel, hi, sh),
-        [(normed_one, False), (w_attn, True), (lengths, False), (vec_rows, False), (tokens, False), (cotangent, True)],
+        [(normed_one, False), (w_attn, True), (lengths, False), (vec_rows, False), (tokens, False), (cotangent, True)]
+        + [(send_attn, True)],
         [
             (own_f32, False),
             (gathered, True),
             (gathered, True),
             (jax.ShapeDtypeStruct((tp, row_tokens, 3 * hc), BF), False),
             (jax.ShapeDtypeStruct((t_all, hc), BF), False),
+            (send_attn, True),
         ],
         own_scratch
         + [pltpu.VMEM((d, 4 * hc), BF), pltpu.SemaphoreType.DMA]
         + sum_scratch(row_tokens, d)
-        + gather_scratch() * 2,
+        + gather_scratch() * 2
+        + swap_scratch(),
         2,
-        110,
+        120,
         "attention",
     )
-
-    normed_two, momentum_now = lax.optimization_barrier((normed_two, momentum))
-    send_attn, send_mlp = lax.optimization_barrier(arrange(momentum_now.astype(BF)))
 
     def rows_of(width):
         return (row_tokens, width), lambda r: (r, 0)
@@ -841,19 +1032,13 @@
         "hidden_units",
         grid=(tp,),
     )
-    flat_one, flat_two, flat_cot = (a.reshape(t_all, d) for a in (normed_one, normed_two, cot_all))
-
-    def summed(left_right):
-        parts = [dot("td,tn->dn", a, b).astype(BF) for a, b in left_right]
-        part = parts[0] if len(parts) == 1 else jnp.concatenate(parts, axis=1)
-        stacked = part.reshape(hi, tp, sh, rows, -1).transpose(0, 2, 1, 3, 4).reshape(groups, tp * rows, -1)
-        return stacked
 
     def sent(stacked):
         return lax.psum_scatter(stacked, FS, scatter_dimension=0, tiled=False)
 
-    s_down = summed([(flat_cot, activated)])
-    s_up = summed([(flat_two, grad_before)])
+    s_down = outer([(cot_all, activated)], hi, sh, "grad_down")
+    grad_before, s_down = lax.optimization_barrier((grad_before, s_down))
+    s_up = outer([(normed_two, grad_before)], hi, sh, "grad_up")
     grad_before, s_down, s_up = lax.optimization_barrier((grad_before, s_down, s_up))
     g_down, g_up = sent(s_down), sent(s_up)
 
@@ -872,73 +1057,66 @@
         "second_norm_backward",
     )
     grad_branch, g_down = lax.optimization_barrier((grad_branch, g_down))
-    grad_joined, mom_attn = call(
+    g_down = g_down.reshape(tp, rows, -1)
+    grad_joined, back_down = call(
         partial(attention_back_kernel, hi, sh),
-        [(grad_branch, row_of(d)), (w_attn, True), (qkv, row_of(3 * hc)), (lengths, fixed(lengths)), (send_attn, True)],
-        [(jax.ShapeDtypeStruct((t_all, 3 * hc), BF), rows_of(3 * hc)), (send_attn, True)],
+        [(grad_branch, row_of(d)), (w_attn, True), (qkv, row_of(3 * hc)), (lengths, fixed(lengths)), (g_down, True)],
+        [(jax.ShapeDtypeStruct((t_all, 3 * hc), BF), rows_of(3 * hc)), (g_down, True)],
         [pltpu.VMEM((d, hc), BF), pltpu.SemaphoreType.DMA] + swap_scratch(),
         8,
         25,
         "attention_backward",
         grid=(tp,),
     )
-    grad_branch = grad_branch.reshape(t_all, d)
-    s_attn = summed([(flat_one, grad_joined), (grad_branch, attended)])
+    s_attn = outer([(normed_one, grad_joined), (grad_branch, attended)], hi, sh, "grad_attention")
     grad_joined, s_attn = lax.optimization_barrier((grad_joined, s_attn))
     g_attn = sent(s_attn).reshape(send_attn.shape)
-    g_mlp = jnp.concatenate([g_up, g_down], axis=1).reshape(send_mlp.shape)
-    grad_tokens, sums_one, back_mlp, ortho_mlp = call(
+    g_up = g_up.reshape(tp, rows, -1)
+    grad_tokens, sums_one, back_up, ortho_mlp = call(
         partial(last_kernel, hi, sh),
         [(grad_joined, False), (w_attn, True), (tokens, False), (grad_middle, False), (vec_rows, False)]
-        + [(mom_mlp, False), (g_mlp, False)],
-        [(own_f32, False), (jax.ShapeDtypeStruct((2, 8, d), F32), False), (send_mlp, True), (send_mlp, True)],
+        + [(mom_mlp, False), (g_up, True), (g_down, True)],
+        [(own_f32, False), (jax.ShapeDtypeStruct((2, 8, d), F32), False), (g_up, True), (send_mlp, True)],
         own_scratch[:1]
-        + [pltpu.VMEM((d, 3 * hc), BF), pltpu.SemaphoreType.DMA, pltpu.VMEM(send_mlp.shape, BF)]
+        + [pltpu.VMEM((d, 3 * hc), BF), pltpu.SemaphoreType.DMA]
+        + [pltpu.VMEM(send_mlp.shape, BF), pltpu.SemaphoreType.DMA((2,)), pltpu.VMEM(send_mlp.shape, BF)]
         + sum_scratch(row_tokens, d)
         + ortho_scratch(groups, send_mlp.shape[2])
         + swap_scratch() * 2,
         4,
-        75,
+        85,
         "first_norm_backward",
     )
     grad_tokens, g_attn = lax.optimization_barrier((grad_tokens, g_attn))
 
-    back_attn, ortho_attn = call(
+    sums_two = jnp.sum(sums_two, axis=1)
+    early = jnp.zeros((16, d), F32)
+    for row, value in ((2, sums_two[:2]), (6, sums_two[2:])):
+        early = lax.dynamic_update_slice(early, value, (row, 0))
+    biases = jnp.sum(grad_joined, axis=0, dtype=F32)[None]
+    early = lax.dynamic_update_slice(early, biases[:, :hc], (4, me * hc))
+    early = lax.dynamic_update_slice(early, biases[:, 2 * hc :], (5, me * hc))
+    each = d // units
+    hidden = jnp.sum(grad_before, axis=0, dtype=F32)[None]
+    early = lax.dynamic_update_slice(early, hidden, (8 + me // each, me % each * units))
+    early, sums_one = lax.optimization_barrier((early, sums_one))
+
+    back_attn, ortho_attn, vector_sums = call(
         partial(ortho_kernel, hi, sh),
-        [(mom_attn, False), (g_attn, False)],
-        [(send_attn, True), (send_attn, True)],
-        [pltpu.VMEM(send_attn.shape, BF)] + ortho_scratch(groups, send_attn.shape[2]) + swap_scratch() * 2,
+        [(mom_attn, False), (g_attn, False), (early, False), (sums_one, False)],
+        [(send_attn, True), (send_attn, True), (jax.ShapeDtypeStruct((16, 128), F32), False)],
+        [pltpu.VMEM(send_attn.shape, BF)]
+        + ortho_scratch(groups, send_attn.shape[2])
+        + swap_scratch() * 2
+        + terms_scratch(hi, sh, d),
         6,
-        30,
+        40,
         "orthogonalize_attention",
     )
-    weight_grad = restore(back_attn, back_mlp).astype(F32)
-    moment_new = 0.95 * momentum + weight_grad
-    orthogonal_rows = restore(ortho_attn, ortho_mlp).astype(F32)
-    new_weights = weights * (1.0 - 0.15 * 0.1) - 0.15 * 0.2 * math.sqrt(d) * orthogonal_rows
-
-    sums_one, sums_two = jnp.sum(sums_one, axis=1), jnp.sum(sums_two, axis=1)
-    plain = jnp.stack(
-        [
-            sums_one[0],
-            sums_one[1],
-            sums_two[0],
-            sums_two[1],
-            jnp.zeros((d,), F32),
-            jnp.zeros((d,), F32),
-            sums_two[2],
-            sums_two[3],
-        ],
-        axis=0,
-    )
-    plain = lax.dynamic_update_slice(plain, jnp.sum(grad_joined[:, :hc], axis=0, dtype=F32)[None], (4, me * hc))
-    plain = lax.dynamic_update_slice(plain, jnp.sum(grad_joined[:, 2 * hc :], axis=0, dtype=F32)[None], (5, me * hc))
-    hidden = jnp.zeros((inner_all * head,), F32)
-    hidden = lax.dynamic_update_slice(hidden, jnp.sum(grad_before, axis=0, dtype=F32), (me * inner * head,))
-    terms = jnp.concatenate([plain, hidden.reshape(-1, d)], axis=0)
-    terms = terms.reshape(-1, world, rows).transpose(1, 0, 2).reshape(world, -1)
-    vector_grad = jnp.sum(lax.all_to_all(terms, ALL, split_axis=0, concat_axis=0, tiled=True), axis=0)
-    vector_grad = vector_grad.reshape(-1, rows).T
+    weight_grad, new_weights, moment_new = update(weights, momentum, back_attn, ortho_attn, back_up, back_down, ortho_mlp)
+
+    spot = (flat % lanes) * rows
+    vector_grad = lax.dynamic_slice(vector_sums, (0, spot), (16, rows))[:count].T
     first_moment = 0.9 * vector_moment + 0.1 * vector_grad
     second = 0.95 * vector_second + 0.05 * vector_grad * vector_grad
     corrected = first_moment / (1.0 - 0.9**STEP)

time: 698 us -> 674 us (0.966)
  Pallas kernels: 496 us -> 571 us
  matrix products: 39.9 us -> 0 us
  local copies, waits for them, and re-layouts: 54.2 us -> 20.4 us
  other arithmetic: 28.6 us -> 12.9 us
    pallas_call x7 -> x11, Pallas kernels: 496 us -> 571 us  [call(): pl.pallas_call(body, out_shape=[jax.ShapeDtypeStruct(s.shape, s.dtype) fo...]
    dot_general x4 -> x0, matrix products: 39.9 us -> none  [dot(): return jnp.einsum(spec, a, b, preferred_element_type=F32, **kw)]
    transpose x8 -> x0, local copies, waits for them, and re-layouts: 17.3 us -> none  [the longest x3 9.95 us: summed(): part.reshape(hi, tp, sh, rows, -1).transpose(0, 2, 1, 3, 4)]
    add x1 -> x0, other arithmetic: 11.2 us -> none  [local(): moment_new = 0.95 * momentum + weight_grad]
    another operation x3 -> x4, other arithmetic: 0.09 us -> 7.44 us  [the longest x1 0.08 us: local(): jnp.stack([sums_one[0], sums_one[1], sums_two[0], sums_two[1], jnp.zeros(...]
    reshape x11 -> x8, local copies, waits for them, and re-layouts: 20.8 us -> 15.1 us  [the longest x4 8.53 us: arrange(): array[:, 4 * HEADS:].astype(BF).reshape(rows, 2, tp, inner, head)]
  transfers between devices with their start and end apart: 6 -> 5, of which waited for: 1 -> 0; matrix products, arithmetic and copies ran while one was open for 9% -> 3% of each run, Pallas kernels for 62% -> 68%
where the time goes in v5:
time: 674 us; the launch traced here: 669 us
  Pallas kernels  571 us (85%)
  blocking collectives  49.8 us (7%)
  local copies, waits for them, and re-layouts  20.4 us (3%)
  between operations  14.3 us (2%)
  other arithmetic  12.9 us (2%)
    pallas_call x11, Pallas kernels, call(): pl.pallas_call(body, out_shape=[jax.ShapeDtypeStruct(s.shape, s.dtype) fo...  571 us
    all_to_all x2, blocking collectives, swap(): return lax.all_to_all(array, 'tp', split_axis=0, concat_axis=0, tiled=True)  49.8 us
  transfers between devices with their start and end apart: 5, of which 0 were waited for; matrix products, arithmetic and copies ran while one was open for 3% of the time, Pallas kernels for 68%

profile of v5, /device:TPU:27, one launch (start us, length us, event | category | flops | bytes accessed | tf_op | source)
XLA Modules:
  0.0 669.0 jit_solution(14573119067753909617)
XLA Ops:
  7.2 0.0 all-gather.5.cloned.1.call-start
  7.2 3.4 convert.16
  10.6 0.1 slice.41
  10.7 1.8 copy.31
  12.4 2.6 reshape.98
  15.0 18.7 %all_to_all.10 = bf16[8,64,1024]{2,1,0:T(8,128)(2,1)} all-to-all(bf16[8,64,1024]{2,1,0:T(8,128)(2,1)} %reshape.98), channel_id=1, replica_groups=mesh['dp'=8,'shard'=4] {'dp'}, dimensions={0} | all-to-all | bytes 2097152 | tf_op jit(solution)/shard_map/all_to_all | solution.py:952
  33.8 0.0 all-gather.7.cloned.1.call-start
  33.8 0.1 slice.40
  34.0 0.4 copy.29
  34.4 2.3 reshape.96
  36.6 31.1 %all_to_all.11 = bf16[8,64,2048]{2,1,0:T(8,128)(2,1)} all-to-all(bf16[8,64,2048]{2,1,0:T(8,128)(2,1)} %reshape.96), channel_id=1, replica_groups=mesh['dp'=8,'shard'=4] {'dp'}, dimensions={0} | all-to-all | bytes 4194304 | tf_op jit(solution)/shard_map/all_to_all | solution.py:952
  67.8 0.0 reduce-scatter.4.cloned.1.call-start
  67.8 0.1 tile.10
  68.0 0.6 fusion.2.piece
  68.6 54.9 %first_norm.1 = (bf16[8,256,2048]{2,1,0:T(8,128)(2,1)}, f32[16,2048]{1,0:T(8,128)}, f32[8,128]{1,0:T(8,128)}) custom-call(bf16[256,2048]{1,0:T(8,128)(2,1)} %tok.2, bf16[16,128]{1,0:T(8,128)(2,1)} %fusion.2.piece), custom_call_target="tpu_custom_call" | custom-call | bytes 150000000 | tf_op jit(solution)/shard_map/first_norm/pallas_call | solution.py:605
  123.5 4.1 convert.19
  127.5 0.1 slice.42
  127.6 0.1 slice.43
  127.8 0.7 copy.30
  128.5 1.5 reshape.100.mom
  130.0 1.7 copy.28
  131.7 4.2 reshape.102.mom
  135.9 132.7 %attention.1 = (f32[256,2048]{1,0:T(8,128)}, bf16[8,256,2048]{2,1,0:T(8,128)(2,1)}, bf16[8,256,2048]{2,1,0:T(8,128)(2,1)}, bf16[8,256,768]{2,1,0:T(8,128)(2,1)},...) custom-call(bf16[8,256,2048]{2,1,0:T(8,128)(2,1)} %get-tuple-element.55.normed.refs_0_, ...), custom_call_target="tpu_custom_call" | custom-call | bytes 360000000 | tf_op jit(solution)/shard_map/attention/pallas_call | solution.py:605
  268.7 0.0 all-gather.7.cloned.1.call-done
  268.7 29.8 %hidden_units.1 = (bf16[2048,1024]{1,0:T(8,128)(2,1)}, bf16[2048,1024]{1,0:T(8,128)(2,1)}, bf16[8,64,2048]{2,1,0:T(8,128)(2,1)}) custom-call(bf16[8,256,2048]{2,1,0:T(8,128)(2,1)} %get-tuple-element.59.normed.refs_0_, bf16[8,256,2048]{2,1,0:T(8,128)(2,1)} %get-tuple-element.60.cot.refs_0_, bf16[4,8,64,2048]{3,2,1,0:T(8,128)(2,1)} %bitcast.42, ...), custom_call_target="tpu_custom_call" | custom-call | bytes 90000000 | tf_op jit(solution)/shard_map/hidden_units/pallas_call | solution.py:605
  298.5 14.2 %grad_down.1 = bf16[1,4,8,64,1024]{4,3,2,1,0:T(8,128)(2,1)} custom-call(bf16[8,256,2048]{2,1,0:T(8,128)(2,1)} %get-tuple-element.60.cot.refs_0_, bf16[2048,1024]{1,0:T(8,128)(2,1)} %get-tuple-element.63.refs_1_.activated), custom_call_target="tpu_custom_call" | custom-call | bytes 43885712 | tf_op jit(solution)/shard_map/grad_down/pallas_call | solution.py:605
  312.7 14.3 %grad_up.1 = bf16[1,4,8,64,1024]{4,3,2,1,0:T(8,128)(2,1)} custom-call(bf16[8,256,2048]{2,1,0:T(8,128)(2,1)} %get-tuple-element.59.normed.refs_0_, bf16[2048,1024]{1,0:T(8,128)(2,1)} %get-tuple-element.66.refs_1_.grad_before), custom_call_target="tpu_custom_call" | custom-call | bytes 43885712 | tf_op jit(solution)/shard_map/grad_up/pallas_call | solution.py:605
  327.0 0.0 reduce-scatter.6.cloned.1.call-start
  327.1 0.5 reduce-scatter.6.cloned.1.call-update
  327.6 0.0 reduce-scatter.8.cloned.1.call-start
  327.7 130.4 %second_norm_backward.1 = (f32[256,2048]{1,0:T(8,128)}, f32[4,8,2048]{2,1,0:T(8,128)}, bf16[8,256,2048]{2,1,0:T(8,128)(2,1)}, bf16[256,2048]{1,0:T(8,128)(2,1)}) custom-call(bf16[2048,1024]{1,0:T(8,128)(2,1)} %get-tuple-element.66.refs_1_.grad_before, bf16[2048,1024]{1,0:T(8,128)(2,1)} %get-tuple-element.63.refs_1_.activated, ...), custom_call_target="tpu_custom_call" | custom-call | bytes 345000000 | tf_op jit(solution)/shard_map/second_norm_backward/pallas_call | solution.py:605
  458.0 20.3 %attention_backward.1 = (bf16[2048,768]{1,0:T(8,128)(2,1)}, bf16[8,64,1024]{2,1,0:T(8,128)(2,1)}) custom-call(bf16[8,256,2048]{2,1,0:T(8,128)(2,1)} %get-tuple-element.71.branch.refs_2_, bf16[4,8,64,1024]{3,2,1,0:T(8,128)(2,1)} %bitcast.40, bf16[8,256,768]{2,1,0:T(8,128)(2,1)} %get-tuple-element.72.qkv, f32[8,128]{1,0:T(8,128)} %get-tuple-element.56.lengths, ...), custom_call_target="tpu_custom_call" | custom-call | bytes 75000000 | tf_op jit(solution)/shard_map/attention_backward/pallas_call | solution.py:605
  478.3 16.1 %grad_attention.1 = bf16[1,4,8,64,1024]{4,3,2,1,0:T(8,128)(2,1)} custom-call(bf16[8,256,2048]{2,1,0:T(8,128)(2,1)} %get-tuple-element.55.normed.refs_0_, bf16[2048,768]{1,0:T(8,128)(2,1)} %get-tuple-element.76.refs_1_.grad_joined, bf16[8,256,2048]{2,1,0:T(8,128)(2,1)} %get-tuple-element.71.branch.refs_2_, bf16[2048,256]{1,0:T(8,128)(2,1)} %get-tuple-element.75.refs_3_), custom_call_target="tpu_custom_call" | custom-call | bytes 43885712 | tf_op jit(solution)/shard_map/grad_attention/pallas_call | solution.py:605
  494.5 0.9 copy-done.4
  495.3 0.1 reduce_sum.27
  495.5 2.9 convert_reduce_fusion
  498.4 0.5 convert_reduce_fusion.1
  498.9 0.3 dynamic_update_slice.17
  499.2 0.3 dynamic_update_slice.18
  499.4 0.0 reduce-scatter.6.cloned.1.call-done
  499.5 99.4 %first_norm_backward.1 = (f32[256,2048]{1,0:T(8,128)}, f32[2,8,2048]{2,1,0:T(8,128)}, bf16[8,64,1024]{2,1,0:T(8,128)(2,1)}, bf16[8,64,2048]{2,1,0:T(8,128)(2,1)}) custom-call(bf16[2048,768]{1,0:T(8,128)(2,1)} %get-tuple-element.76.refs_1_.grad_joined, bf16[4,8,64,1024]{3,2,1,0:T(8,128)(2,1)} %bitcast.41, bf16[256,2048]{1,0:T(8,128)(2,1)} %tok.2, ...), custom_call_target="tpu_custom_call" | custom-call | bytes 255000000 | tf_op jit(solution)/shard_map/first_norm_backward/pallas_call | solution.py:605
  598.9 0.3 dynamic_update_slice.19.early
  599.2 0.6 copy-done.3
  599.8 39.1 %orthogonalize_attention.1 = (bf16[8,64,1024]{2,1,0:T(8,128)(2,1)}, bf16[8,64,1024]{2,1,0:T(8,128)(2,1)}, f32[16,128]{1,0:T(8,128)}) custom-call(bf16[8,64,1024]{2,1,0:T(8,128)(2,1)} %get-tuple-element.83.mom, bf16[8,64,1024]{2,1,0:T(8,128)(2,1)} %bitcast.58, f32[16,2048]{1,0:T(8,128)} %copy-done.3, f32[2,8,2048]{2,1,0:T(8,128)} %get-tuple-element.88.sums_one), custom_call_target="tpu_custom_call" | custom-call | bytes 120000000 | tf_op jit(solution)/shard_map/orthogonalize_attention/pallas_call | solution.py:605
  638.9 1.4 divide_subtract_fusion
  640.3 19.7 %update.1 = (f32[64,192,128]{2,1,0:T(8,128)}, f32[64,192,128]{2,1,0:T(8,128)}, f32[64,192,128]{2,1,0:T(8,128)}) custom-call(f32[64,192,128]{2,1,0:T(8,128)} %weights.1, f32[64,192,128]{2,1,0:T(8,128)} %momentum.1, bf16[8,64,1024]{2,1,0:T(8,128)(2,1)} %get-tuple-element.89.back_attn, bf16[8,64,1024]{2,1,0:T(8,128)(2,1)} %get-tuple-element.90.ortho_attn, ...), custom_call_target="tpu_custom_call" | custom-call | bytes 45000000 | tf_op jit(solution)/shard_map/update/pallas_call | solution.py:605
  660.0 1.0 copy.38
  661.0 1.3 copy.39
  (32 shorter events, 0.2 us)
Async XLA Ops:
  7.2 128.7 %all-gather.5.cloned.1.call-start = ((), (), s32[]{:S(2)}) async-start(), calls=%async_computation.8 | async-start | bytes 5242880 | tf_op jit(solution)/shard_map/all_gather | solution.py:957
  33.8 234.9 %all-gather.7.cloned.1.call-start = ((), (), s32[]{:S(2)}) async-start(), calls=%async_computation.9 | async-start | bytes 10485760 | tf_op jit(solution)/shard_map/all_gather | solution.py:957
  36.6 31.2 %copy-start.5 = (f32[64,12]{0,1:T(8,128)S(1)}, f32[64,12]{0,1:T(8,128)}, u32[]{:S(2)}) copy-start(f32[64,12]{0,1:T(8,128)} %param.12) | copy-start | bytes 9220
  36.6 31.3 %copy-start.8 = (s32[1,4]{1,0:T(1,128)S(1)}, s32[1,4]{1,0:T(1,128)}, u32[]{:S(2)}) copy-start(s32[1,4]{1,0:T(1,128)} %param.9) | copy-start | bytes 52
  67.8 390.3 %reduce-scatter.4.cloned.1.call-start = ((), (), s32[]{:S(2)}) async-start(), calls=%async_computation.5 | async-start | bytes 5242880 | tf_op jit(solution)/shard_map/reduce_scatter | solution.py:1037
  327.0 172.4 %reduce-scatter.6.cloned.1.call-start = ((), (), s32[]{:S(2)}) async-start(), calls=%async_computation.6 | async-start | bytes 5242880 | tf_op jit(solution)/shard_map/reduce_scatter | solution.py:1037
  327.6 271.6 %reduce-scatter.8.cloned.1.call-start = ((), (), s32[]{:S(2)}) async-start(), calls=%async_computation.7 | async-start | bytes 5242880 | tf_op jit(solution)/shard_map/reduce_scatter | solution.py:1037
  494.4 1.0 copy-start.4
  494.4 3.9 copy-start
  499.5 139.4 %copy-start.6 = (f32[64,12]{0,1:T(8,128)S(1)}, f32[64,12]{0,1:T(8,128)}, u32[]{:S(2)}) copy-start(f32[64,12]{0,1:T(8,128)} %param.14) | copy-start | bytes 9220
  499.5 139.4 %copy-start.7 = (f32[64,12]{0,1:T(8,128)S(1)}, f32[64,12]{0,1:T(8,128)}, u32[]{:S(2)}) copy-start(f32[64,12]{0,1:T(8,128)} %param.13) | copy-start | bytes 9220
  599.2 0.7 copy-start.3
  640.3 19.7 %copy-start.2 = (bf16[256,2048]{1,0:T(8,128)(2,1)S(1)}, bf16[256,2048]{1,0:T(8,128)(2,1)}, u32[]{:S(2)}) copy-start(bf16[256,2048]{1,0:T(8,128)(2,1)} %get-tuple-element.111) | copy-start | bytes 3145732
  640.3 20.7 %copy-start.1 = (f32[256,2048]{1,0:T(8,128)S(1)}, f32[256,2048]{1,0:T(8,128)}, u32[]{:S(2)}) copy-start(f32[256,2048]{1,0:T(8,128)} %get-tuple-element.112) | copy-start | bytes 6291460
Sparse Core Ops, SparseCore 0:
  33.9 78.7 all-gather.4
  114.2 147.7 all-gather.6
  327.2 76.0 reduce-scatter.3
  406.1 77.2 reduce-scatter.5
  494.6 93.1 reduce-scatter.7

commit v6 on v5

--- a/solution.py
+++ b/solution.py
@@ -474,6 +474,7 @@
     meet((pc, px, py))
     fetched(w_up, w_sem.at[0])
     sums = Summing(grad_before, w_up, total, scratch[:6])
+    more = Summing(activated, w_down, total, scratch[9:])
     sums.run()
     sums_out[...] = jnp.zeros_like(sums_out)
 
@@ -493,7 +494,6 @@
     spread = Gathering(own, branch_all, *scratch[6:9])
     spread.start()
     fetched(w_down, w_sem.at[1])
-    more = Summing(activated, w_down, total, scratch[9:])
     more.first()
     spread.forward()
     more.second()
@@ -951,13 +951,15 @@
     def swap(array):
         return lax.all_to_all(array, "tp", split_axis=0, concat_axis=0, tiled=True)
 
-    attn_send, mlp_send = arrange(weights)
+    attn_send = arrange(weights)[0]
+    attn_send, weights_later = lax.optimization_barrier((attn_send, weights))
+    mlp_send = arrange(weights_later)[1]
 
     def spread(array):
         return lax.all_gather(array, FS, axis=0, tiled=False)
 
     w_attn = spread(swap(attn_send))
-    mlp_swapped, tokens = lax.optimization_barrier((swap(mlp_send), tokens))
+    mlp_swapped, tokens, send_attn, send_mlp = lax.optimization_barrier((swap(mlp_send), tokens, *arrange(momentum)))
     w_mlp = spread(mlp_swapped)
 
     flat = (lax.axis_index("hi") * tp + me) * sh + lax.axis_index("shard")
@@ -989,8 +991,6 @@
 
     hc = heads * head
     units = inner * head
-    normed_one, momentum_now = lax.optimization_barrier((normed_one, momentum))
-    send_attn, send_mlp = arrange(momentum_now)
     middle, normed_two, cot_all, qkv, attended, mom_attn = call(
         partial(attention_kernel, hi, sh),
         [(normed_one, False), (w_attn, True), (lengths, False), (vec_rows, False), (tokens, False), (cotangent, True)]

time: 674 us -> 662 us (0.982)
  blocking collectives: 49.8 us -> 18.1 us
  waiting for transfers between devices: 0.68 us -> 15.1 us
    all_to_all x2 -> x1, blocking collectives: 49.8 us -> 18.1 us  [swap(): return lax.all_to_all(array, 'tp', split_axis=0, concat_axis=0, tiled=True)]
    all_to_all x0 -> x1, waiting for transfers between devices: none -> 12.9 us  [swap(): return lax.all_to_all(array, 'tp', split_axis=0, concat_axis=0, tiled=True)]
  transfers between devices with their start and end apart: 5 -> 6, of which waited for: 0 -> 2; matrix products, arithmetic and copies ran while one was open for 3% -> 3% of each run, Pallas kernels for 68% -> 69%
where the time goes in v6:
time: 662 us; the launch traced here: 657 us
  Pallas kernels  572 us (86%)
  local copies, waits for them, and re-layouts  22.2 us (3%)
  blocking collectives  18.1 us (3%)
  waiting for transfers between devices  15.1 us (2%)
  between operations  14.3 us (2%)
  other arithmetic  8.82 us (1%)
    pallas_call x11, Pallas kernels, call(): pl.pallas_call(body, out_shape=[jax.ShapeDtypeStruct(s.shape, s.dtype) fo...  572 us
    all_to_all x1, blocking collectives, swap(): return lax.all_to_all(array, 'tp', split_axis=0, concat_axis=0, tiled=True)  18.1 us
  transfers between devices with their start and end apart: 6, of which 2 were waited for; matrix products, arithmetic and copies ran while one was open for 3% of the time, Pallas kernels for 69%

profile of v6, /device:TPU:27, one launch (start us, length us, event | category | flops | bytes accessed | tf_op | source)
XLA Modules:
  0.0 656.7 jit_solution(1405990687384005090)
XLA Ops:
  7.2 0.0 all-gather.5.cloned.1.call-start
  7.2 1.8 slice.52
  9.0 0.7 copy.31
  9.7 0.8 reshape.96
  10.5 18.1 %all_to_all.10 = bf16[8,64,1024]{2,1,0:T(8,128)(2,1)} all-to-all(bf16[8,64,1024]{2,1,0:T(8,128)(2,1)S(1)} %reshape.96), channel_id=1, replica_groups=mesh['dp'=8,'shard'=4] {'dp'}, dimensions={0} | all-to-all | bytes 2097152 | tf_op jit(solution)/shard_map/all_to_all | solution.py:952
  28.7 2.6 slice.51
  31.3 0.4 copy.29
  31.7 2.3 reshape.98
  33.9 6.0 all-to-all-start
  39.9 3.3 convert.20
  43.3 0.1 slice.43
  43.4 2.0 copy.28
  45.5 0.1 copy-done.1
  45.6 4.2 reshape.102.mom
  49.9 0.7 copy.30
  50.6 1.5 reshape.100.mom
  52.2 12.9 %all-to-all-done = bf16[8,64,2048]{2,1,0:T(8,128)(2,1)} async-done(((bf16[8,64,2048]{2,1,0:T(8,128)(2,1)}), bf16[8,64,2048]{2,1,0:T(8,128)(2,1)}, u32[]{:S(2)}, u32[]{:S(2)}) %all-to-all-start) | async-done | bytes 2097184 | tf_op jit(solution)/shard_map/all_to_all | solution.py:952
  65.1 0.2 reduce-scatter.4.cloned.1.call-start
  65.4 0.1 tile.10
  65.5 0.6 fusion.2.piece
  66.1 56.6 %first_norm.1 = (bf16[8,256,2048]{2,1,0:T(8,128)(2,1)}, f32[16,2048]{1,0:T(8,128)}, f32[8,128]{1,0:T(8,128)}) custom-call(bf16[256,2048]{1,0:T(8,128)(2,1)} %tok.2, bf16[16,128]{1,0:T(8,128)(2,1)} %fusion.2.piece), custom_call_target="tpu_custom_call" | custom-call | bytes 150000000 | tf_op jit(solution)/shard_map/first_norm/pallas_call | solution.py:605
  122.7 0.0 all-gather.5.cloned.1.call-done
  122.7 132.8 %attention.1 = (f32[256,2048]{1,0:T(8,128)}, bf16[8,256,2048]{2,1,0:T(8,128)(2,1)}, bf16[8,256,2048]{2,1,0:T(8,128)(2,1)}, bf16[8,256,768]{2,1,0:T(8,128)(2,1)},...) custom-call(bf16[8,256,2048]{2,1,0:T(8,128)(2,1)} %get-tuple-element.57.normed.refs_0_, ...), custom_call_target="tpu_custom_call" | custom-call | bytes 360000000 | tf_op jit(solution)/shard_map/attention/pallas_call | solution.py:605
  255.5 1.5 all-gather.7.cloned.1.call-done
  257.0 29.9 %hidden_units.1 = (bf16[2048,1024]{1,0:T(8,128)(2,1)}, bf16[2048,1024]{1,0:T(8,128)(2,1)}, bf16[8,64,2048]{2,1,0:T(8,128)(2,1)}) custom-call(bf16[8,256,2048]{2,1,0:T(8,128)(2,1)} %get-tuple-element.62.normed.refs_0_, bf16[8,256,2048]{2,1,0:T(8,128)(2,1)} %get-tuple-element.63.cot.refs_0_, bf16[4,8,64,2048]{3,2,1,0:T(8,128)(2,1)} %bitcast.42, ...), custom_call_target="tpu_custom_call" | custom-call | bytes 90000000 | tf_op jit(solution)/shard_map/hidden_units/pallas_call | solution.py:605
  286.9 14.2 %grad_down.1 = bf16[1,4,8,64,1024]{4,3,2,1,0:T(8,128)(2,1)} custom-call(bf16[8,256,2048]{2,1,0:T(8,128)(2,1)} %get-tuple-element.63.cot.refs_0_, bf16[2048,1024]{1,0:T(8,128)(2,1)} %get-tuple-element.67.refs_1_.activated), custom_call_target="tpu_custom_call" | custom-call | bytes 43885712 | tf_op jit(solution)/shard_map/grad_down/pallas_call | solution.py:605
  301.1 14.1 %grad_up.1 = bf16[1,4,8,64,1024]{4,3,2,1,0:T(8,128)(2,1)} custom-call(bf16[8,256,2048]{2,1,0:T(8,128)(2,1)} %get-tuple-element.62.normed.refs_0_, bf16[2048,1024]{1,0:T(8,128)(2,1)} %get-tuple-element.70.refs_1_.grad_before), custom_call_target="tpu_custom_call" | custom-call | bytes 43885712 | tf_op jit(solution)/shard_map/grad_up/pallas_call | solution.py:605
  315.2 0.0 reduce-scatter.6.cloned.1.call-start
  315.3 0.5 reduce-scatter.6.cloned.1.call-update
  315.8 0.3 reduce-scatter.8.cloned.1.call-start
  316.1 131.1 %second_norm_backward.1 = (f32[256,2048]{1,0:T(8,128)}, f32[4,8,2048]{2,1,0:T(8,128)}, bf16[8,256,2048]{2,1,0:T(8,128)(2,1)}, bf16[256,2048]{1,0:T(8,128)(2,1)}) custom-call(bf16[2048,1024]{1,0:T(8,128)(2,1)} %get-tuple-element.70.refs_1_.grad_before, bf16[2048,1024]{1,0:T(8,128)(2,1)} %get-tuple-element.67.refs_1_.activated, ...), custom_call_target="tpu_custom_call" | custom-call | bytes 345000000 | tf_op jit(solution)/shard_map/second_norm_backward/pallas_call | solution.py:605
  447.2 19.9 %attention_backward.1 = (bf16[2048,768]{1,0:T(8,128)(2,1)}, bf16[8,64,1024]{2,1,0:T(8,128)(2,1)}) custom-call(bf16[8,256,2048]{2,1,0:T(8,128)(2,1)} %get-tuple-element.75.branch.refs_2_, bf16[4,8,64,1024]{3,2,1,0:T(8,128)(2,1)} %bitcast.40, bf16[8,256,768]{2,1,0:T(8,128)(2,1)} %get-tuple-element.76.qkv, f32[8,128]{1,0:T(8,128)} %get-tuple-element.59.lengths, ...), custom_call_target="tpu_custom_call" | custom-call | bytes 75000000 | tf_op jit(solution)/shard_map/attention_backward/pallas_call | solution.py:605
  467.0 16.1 %grad_attention.1 = bf16[1,4,8,64,1024]{4,3,2,1,0:T(8,128)(2,1)} custom-call(bf16[8,256,2048]{2,1,0:T(8,128)(2,1)} %get-tuple-element.57.normed.refs_0_, bf16[2048,768]{1,0:T(8,128)(2,1)} %get-tuple-element.80.refs_1_.grad_joined, bf16[8,256,2048]{2,1,0:T(8,128)(2,1)} %get-tuple-element.75.branch.refs_2_, bf16[2048,256]{1,0:T(8,128)(2,1)} %get-tuple-element.79.refs_3_), custom_call_target="tpu_custom_call" | custom-call | bytes 43885712 | tf_op jit(solution)/shard_map/grad_attention/pallas_call | solution.py:605
  483.2 0.9 copy-done.5
  484.1 0.1 reduce_sum.27
  484.2 2.9 convert_reduce_fusion
  487.1 0.5 convert_reduce_fusion.1
  487.6 0.3 dynamic_update_slice.17
  487.9 0.3 dynamic_update_slice.18
  488.2 99.3 %first_norm_backward.1 = (f32[256,2048]{1,0:T(8,128)}, f32[2,8,2048]{2,1,0:T(8,128)}, bf16[8,64,1024]{2,1,0:T(8,128)(2,1)}, bf16[8,64,2048]{2,1,0:T(8,128)(2,1)}) custom-call(bf16[2048,768]{1,0:T(8,128)(2,1)} %get-tuple-element.80.refs_1_.grad_joined, bf16[4,8,64,1024]{3,2,1,0:T(8,128)(2,1)} %bitcast.41, bf16[256,2048]{1,0:T(8,128)(2,1)} %tok.2, ...), custom_call_target="tpu_custom_call" | custom-call | bytes 255000000 | tf_op jit(solution)/shard_map/first_norm_backward/pallas_call | solution.py:605
  587.5 0.3 dynamic_update_slice.19.early
  587.9 0.0 reduce-scatter.8.cloned.1.call-done
  587.9 0.6 copy-done.4
  588.5 38.1 %orthogonalize_attention.1 = (bf16[8,64,1024]{2,1,0:T(8,128)(2,1)}, bf16[8,64,1024]{2,1,0:T(8,128)(2,1)}, f32[16,128]{1,0:T(8,128)}) custom-call(bf16[8,64,1024]{2,1,0:T(8,128)(2,1)} %get-tuple-element.87.mom, bf16[8,64,1024]{2,1,0:T(8,128)(2,1)} %bitcast.58, f32[16,2048]{1,0:T(8,128)} %copy-done.4, f32[2,8,2048]{2,1,0:T(8,128)} %get-tuple-element.92.sums_one), custom_call_target="tpu_custom_call" | custom-call | bytes 120000000 | tf_op jit(solution)/shard_map/orthogonalize_attention/pallas_call | solution.py:605
  626.6 1.4 divide_subtract_fusion
  628.0 19.7 %update.1 = (f32[64,192,128]{2,1,0:T(8,128)}, f32[64,192,128]{2,1,0:T(8,128)}, f32[64,192,128]{2,1,0:T(8,128)}) custom-call(f32[64,192,128]{2,1,0:T(8,128)} %weights.1, f32[64,192,128]{2,1,0:T(8,128)} %momentum.1, bf16[8,64,1024]{2,1,0:T(8,128)(2,1)} %get-tuple-element.93.back_attn, bf16[8,64,1024]{2,1,0:T(8,128)(2,1)} %get-tuple-element.94.ortho_attn, ...), custom_call_target="tpu_custom_call" | custom-call | bytes 45000000 | tf_op jit(solution)/shard_map/update/pallas_call | solution.py:605
  647.7 1.0 copy.38
  648.7 1.3 copy.39
  (35 shorter events, 0.2 us)
Async XLA Ops:
  7.2 115.5 %all-gather.5.cloned.1.call-start = ((), (), s32[]{:S(2)}) async-start(), calls=%async_computation.8 | async-start | bytes 5242880 | tf_op jit(solution)/shard_map/all_gather | solution.py:959
  33.9 31.1 %all-to-all-start = ((bf16[8,64,2048]{2,1,0:T(8,128)(2,1)}), bf16[8,64,2048]{2,1,0:T(8,128)(2,1)}, u32[]{:S(2)}, u32[]{:S(2)}) async-start(bf16[8,64,2048]{2,1,0:T(8,128)(2,1)} %reshape.98), calls=%async_computation | async-start | bytes 4194304 | tf_op jit(solution)/shard_map/all_to_all | solution.py:952
  39.9 217.1 %all-gather.7.cloned.1.call-start = ((), (), s32[]{:S(2)}) async-start(), calls=%async_computation.9 | async-start | bytes 10485760 | tf_op jit(solution)/shard_map/all_gather | solution.py:959
  43.3 2.4 copy-start.1
  45.6 4.3 slice-start
  49.9 15.5 %copy-start.6 = (f32[64,12]{0,1:T(8,128)S(1)}, f32[64,12]{0,1:T(8,128)}, u32[]{:S(2)}) copy-start(f32[64,12]{0,1:T(8,128)} %param.12) | copy-start | bytes 9220
  49.9 15.6 %copy-start.9 = (s32[1,4]{1,0:T(1,128)S(1)}, s32[1,4]{1,0:T(1,128)}, u32[]{:S(2)}) copy-start(s32[1,4]{1,0:T(1,128)} %param.9) | copy-start | bytes 52
  65.1 382.1 %reduce-scatter.4.cloned.1.call-start = ((), (), s32[]{:S(2)}) async-start(), calls=%async_computation.5 | async-start | bytes 5242880 | tf_op jit(solution)/shard_map/reduce_scatter | solution.py:1037
  315.2 173.0 %reduce-scatter.6.cloned.1.call-start = ((), (), s32[]{:S(2)}) async-start(), calls=%async_computation.6 | async-start | bytes 5242880 | tf_op jit(solution)/shard_map/reduce_scatter | solution.py:1037
  315.8 272.1 %reduce-scatter.8.cloned.1.call-start = ((), (), s32[]{:S(2)}) async-start(), calls=%async_computation.7 | async-start | bytes 5242880 | tf_op jit(solution)/shard_map/reduce_scatter | solution.py:1037
  483.1 1.0 copy-start.5
  483.1 3.9 copy-start
  488.2 138.4 %copy-start.7 = (f32[64,12]{0,1:T(8,128)S(1)}, f32[64,12]{0,1:T(8,128)}, u32[]{:S(2)}) copy-start(f32[64,12]{0,1:T(8,128)} %param.14) | copy-start | bytes 9220
  488.2 138.4 %copy-start.8 = (f32[64,12]{0,1:T(8,128)S(1)}, f32[64,12]{0,1:T(8,128)}, u32[]{:S(2)}) copy-start(f32[64,12]{0,1:T(8,128)} %param.13) | copy-start | bytes 9220
  587.9 0.7 copy-start.4
  628.0 19.7 %copy-start.3 = (bf16[256,2048]{1,0:T(8,128)(2,1)S(1)}, bf16[256,2048]{1,0:T(8,128)(2,1)}, u32[]{:S(2)}) copy-start(bf16[256,2048]{1,0:T(8,128)(2,1)} %get-tuple-element.115) | copy-start | bytes 3145732
  628.0 20.7 %copy-start.2 = (f32[256,2048]{1,0:T(8,128)S(1)}, f32[256,2048]{1,0:T(8,128)}, u32[]{:S(2)}) copy-start(f32[256,2048]{1,0:T(8,128)} %get-tuple-element.116) | copy-start | bytes 6291460
Sparse Core Ops, SparseCore 0:
  28.8 78.6 all-gather.4
  109.1 147.8 all-gather.6
  315.3 76.7 reduce-scatter.3
  395.0 77.2 reduce-scatter.5
  483.3 93.0 reduce-scatter.7

commit v7 on v6

--- a/solution.py
+++ b/solution.py
@@ -76,13 +76,13 @@
     def fill(self, k):
         right = self.right[k * WIDE : (k + 1) * WIDE, :]
 
-        def one(dest, carry):
-            rows = self.left[pl.ds(pl.multiple_of(dest * self.rows, self.rows), self.rows), :]
+        def one(y, carry):
+            rows = self.left[pl.ds(pl.multiple_of(y * 4 * self.rows, 4 * self.rows), 4 * self.rows), :]
             made = lax.dot_general(rows, right, (((1,), (1,)), ((), ())), preferred_element_type=F32)
-            self.part[k, div(dest, 4), rem(div(dest, 2), 2), rem(dest, 2)] = made.astype(BF)
+            self.part[k, y] = made.astype(BF).reshape(2, 2, self.rows, WIDE)
             return carry
 
-        lax.fori_loop(0, 8, one, 0)
+        lax.fori_loop(0, 2, one, 0)
 
     def copy(self, stage, k, at):
         me, c, x, y, pc, px, py = at

time: 662 us -> 657 us (level)
  no operation moved by 1% of the time
where the time goes in v7:
time: 657 us; the launch traced here: 651 us
  Pallas kernels  566 us (86%)
  local copies, waits for them, and re-layouts  22.2 us (3%)
  blocking collectives  18.1 us (3%)
  waiting for transfers between devices  15 us (2%)
  between operations  14.3 us (2%)
  other arithmetic  8.82 us (1%)
  starting transfers between devices  6.83 us (1%)
    pallas_call x11, Pallas kernels, call(): pl.pallas_call(body, out_shape=[jax.ShapeDtypeStruct(s.shape, s.dtype) fo...  566 us
    all_to_all x1, blocking collectives, swap(): return lax.all_to_all(array, 'tp', split_axis=0, concat_axis=0, tiled=True)  18.1 us
  transfers between devices with their start and end apart: 6, of which 2 were waited for; matrix products, arithmetic and copies ran while one was open for 3% of the time, Pallas kernels for 69%

profile of v7, /device:TPU:27, one launch (start us, length us, event | category | flops | bytes accessed | tf_op | source)
XLA Modules:
  0.0 650.9 jit_solution(352066803871470861)
XLA Ops:
  7.2 0.0 all-gather.5.cloned.1.call-start
  7.2 1.8 slice.52
  9.0 0.7 copy.31
  9.7 0.8 reshape.96
  10.5 18.1 %all_to_all.10 = bf16[8,64,1024]{2,1,0:T(8,128)(2,1)} all-to-all(bf16[8,64,1024]{2,1,0:T(8,128)(2,1)S(1)} %reshape.96), channel_id=1, replica_groups=mesh['dp'=8,'shard'=4] {'dp'}, dimensions={0} | all-to-all | bytes 2097152 | tf_op jit(solution)/shard_map/all_to_all | solution.py:952
  28.7 2.6 slice.51
  31.3 0.4 copy.29
  31.7 2.3 reshape.98
  33.9 6.0 all-to-all-start
  39.9 3.3 convert.20
  43.3 0.1 slice.43
  43.4 2.0 copy.28
  45.5 0.1 copy-done.1
  45.6 4.2 reshape.102.mom
  49.9 0.7 copy.30
  50.6 1.5 reshape.100.mom
  52.2 12.9 %all-to-all-done = bf16[8,64,2048]{2,1,0:T(8,128)(2,1)} async-done(((bf16[8,64,2048]{2,1,0:T(8,128)(2,1)}), bf16[8,64,2048]{2,1,0:T(8,128)(2,1)}, u32[]{:S(2)}, u32[]{:S(2)}) %all-to-all-start) | async-done | bytes 2097184 | tf_op jit(solution)/shard_map/all_to_all | solution.py:952
  65.1 0.6 reduce-scatter.4.cloned.1.call-start
  65.7 0.1 tile.10
  65.8 0.6 fusion.2.piece
  66.4 56.4 %first_norm.1 = (bf16[8,256,2048]{2,1,0:T(8,128)(2,1)}, f32[16,2048]{1,0:T(8,128)}, f32[8,128]{1,0:T(8,128)}) custom-call(bf16[256,2048]{1,0:T(8,128)(2,1)} %tok.2, bf16[16,128]{1,0:T(8,128)(2,1)} %fusion.2.piece), custom_call_target="tpu_custom_call" | custom-call | bytes 150000000 | tf_op jit(solution)/shard_map/first_norm/pallas_call | solution.py:605
  122.8 0.0 all-gather.5.cloned.1.call-done
  122.9 132.7 %attention.1 = (f32[256,2048]{1,0:T(8,128)}, bf16[8,256,2048]{2,1,0:T(8,128)(2,1)}, bf16[8,256,2048]{2,1,0:T(8,128)(2,1)}, bf16[8,256,768]{2,1,0:T(8,128)(2,1)},...) custom-call(bf16[8,256,2048]{2,1,0:T(8,128)(2,1)} %get-tuple-element.57.normed.refs_0_, ...), custom_call_target="tpu_custom_call" | custom-call | bytes 360000000 | tf_op jit(solution)/shard_map/attention/pallas_call | solution.py:605
  255.6 1.4 all-gather.7.cloned.1.call-done
  257.0 29.9 %hidden_units.1 = (bf16[2048,1024]{1,0:T(8,128)(2,1)}, bf16[2048,1024]{1,0:T(8,128)(2,1)}, bf16[8,64,2048]{2,1,0:T(8,128)(2,1)}) custom-call(bf16[8,256,2048]{2,1,0:T(8,128)(2,1)} %get-tuple-element.62.normed.refs_0_, bf16[8,256,2048]{2,1,0:T(8,128)(2,1)} %get-tuple-element.63.cot.refs_0_, bf16[4,8,64,2048]{3,2,1,0:T(8,128)(2,1)} %bitcast.42, ...), custom_call_target="tpu_custom_call" | custom-call | bytes 90000000 | tf_op jit(solution)/shard_map/hidden_units/pallas_call | solution.py:605
  286.9 14.2 %grad_down.1 = bf16[1,4,8,64,1024]{4,3,2,1,0:T(8,128)(2,1)} custom-call(bf16[8,256,2048]{2,1,0:T(8,128)(2,1)} %get-tuple-element.63.cot.refs_0_, bf16[2048,1024]{1,0:T(8,128)(2,1)} %get-tuple-element.67.refs_1_.activated), custom_call_target="tpu_custom_call" | custom-call | bytes 43885712 | tf_op jit(solution)/shard_map/grad_down/pallas_call | solution.py:605
  301.1 14.1 %grad_up.1 = bf16[1,4,8,64,1024]{4,3,2,1,0:T(8,128)(2,1)} custom-call(bf16[8,256,2048]{2,1,0:T(8,128)(2,1)} %get-tuple-element.62.normed.refs_0_, bf16[2048,1024]{1,0:T(8,128)(2,1)} %get-tuple-element.70.refs_1_.grad_before), custom_call_target="tpu_custom_call" | custom-call | bytes 43885712 | tf_op jit(solution)/shard_map/grad_up/pallas_call | solution.py:605
  315.2 0.0 reduce-scatter.6.cloned.1.call-start
  315.2 0.5 reduce-scatter.6.cloned.1.call-update
  315.8 0.2 reduce-scatter.8.cloned.1.call-start
  316.0 125.1 %second_norm_backward.1 = (f32[256,2048]{1,0:T(8,128)}, f32[4,8,2048]{2,1,0:T(8,128)}, bf16[8,256,2048]{2,1,0:T(8,128)(2,1)}, bf16[256,2048]{1,0:T(8,128)(2,1)}) custom-call(bf16[2048,1024]{1,0:T(8,128)(2,1)} %get-tuple-element.70.refs_1_.grad_before, bf16[2048,1024]{1,0:T(8,128)(2,1)} %get-tuple-element.67.refs_1_.activated, ...), custom_call_target="tpu_custom_call" | custom-call | bytes 345000000 | tf_op jit(solution)/shard_map/second_norm_backward/pallas_call | solution.py:605
  441.1 0.0 reduce-scatter.4.cloned.1.call-done
  441.2 20.6 %attention_backward.1 = (bf16[2048,768]{1,0:T(8,128)(2,1)}, bf16[8,64,1024]{2,1,0:T(8,128)(2,1)}) custom-call(bf16[8,256,2048]{2,1,0:T(8,128)(2,1)} %get-tuple-element.75.branch.refs_2_, bf16[4,8,64,1024]{3,2,1,0:T(8,128)(2,1)} %bitcast.40, bf16[8,256,768]{2,1,0:T(8,128)(2,1)} %get-tuple-element.76.qkv, f32[8,128]{1,0:T(8,128)} %get-tuple-element.59.lengths, ...), custom_call_target="tpu_custom_call" | custom-call | bytes 75000000 | tf_op jit(solution)/shard_map/attention_backward/pallas_call | solution.py:605
  461.7 15.7 %grad_attention.1 = bf16[1,4,8,64,1024]{4,3,2,1,0:T(8,128)(2,1)} custom-call(bf16[8,256,2048]{2,1,0:T(8,128)(2,1)} %get-tuple-element.57.normed.refs_0_, bf16[2048,768]{1,0:T(8,128)(2,1)} %get-tuple-element.80.refs_1_.grad_joined, bf16[8,256,2048]{2,1,0:T(8,128)(2,1)} %get-tuple-element.75.branch.refs_2_, bf16[2048,256]{1,0:T(8,128)(2,1)} %get-tuple-element.79.refs_3_), custom_call_target="tpu_custom_call" | custom-call | bytes 43885712 | tf_op jit(solution)/shard_map/grad_attention/pallas_call | solution.py:605
  477.5 0.9 copy-done.5
  478.4 0.1 reduce_sum.27
  478.5 2.9 convert_reduce_fusion
  481.4 0.5 convert_reduce_fusion.1
  481.9 0.3 dynamic_update_slice.17
  482.2 0.3 dynamic_update_slice.18
  482.5 99.2 %first_norm_backward.1 = (f32[256,2048]{1,0:T(8,128)}, f32[2,8,2048]{2,1,0:T(8,128)}, bf16[8,64,1024]{2,1,0:T(8,128)(2,1)}, bf16[8,64,2048]{2,1,0:T(8,128)(2,1)}) custom-call(bf16[2048,768]{1,0:T(8,128)(2,1)} %get-tuple-element.80.refs_1_.grad_joined, bf16[4,8,64,1024]{3,2,1,0:T(8,128)(2,1)} %bitcast.41, bf16[256,2048]{1,0:T(8,128)(2,1)} %tok.2, ...), custom_call_target="tpu_custom_call" | custom-call | bytes 255000000 | tf_op jit(solution)/shard_map/first_norm_backward/pallas_call | solution.py:605
  581.7 0.3 dynamic_update_slice.19.early
  582.0 0.6 copy-done.4
  582.7 37.9 %orthogonalize_attention.1 = (bf16[8,64,1024]{2,1,0:T(8,128)(2,1)}, bf16[8,64,1024]{2,1,0:T(8,128)(2,1)}, f32[16,128]{1,0:T(8,128)}) custom-call(bf16[8,64,1024]{2,1,0:T(8,128)(2,1)} %get-tuple-element.87.mom, bf16[8,64,1024]{2,1,0:T(8,128)(2,1)} %bitcast.58, f32[16,2048]{1,0:T(8,128)} %copy-done.4, f32[2,8,2048]{2,1,0:T(8,128)} %get-tuple-element.92.sums_one), custom_call_target="tpu_custom_call" | custom-call | bytes 120000000 | tf_op jit(solution)/shard_map/orthogonalize_attention/pallas_call | solution.py:605
  620.6 1.4 divide_subtract_fusion
  622.0 19.9 %update.1 = (f32[64,192,128]{2,1,0:T(8,128)}, f32[64,192,128]{2,1,0:T(8,128)}, f32[64,192,128]{2,1,0:T(8,128)}) custom-call(f32[64,192,128]{2,1,0:T(8,128)} %weights.1, f32[64,192,128]{2,1,0:T(8,128)} %momentum.1, bf16[8,64,1024]{2,1,0:T(8,128)(2,1)} %get-tuple-element.93.back_attn, bf16[8,64,1024]{2,1,0:T(8,128)(2,1)} %get-tuple-element.94.ortho_attn, ...), custom_call_target="tpu_custom_call" | custom-call | bytes 45000000 | tf_op jit(solution)/shard_map/update/pallas_call | solution.py:605
  641.9 1.0 copy.38
  642.9 1.3 copy.39
  (35 shorter events, 0.2 us)
Async XLA Ops:
  7.2 115.7 %all-gather.5.cloned.1.call-start = ((), (), s32[]{:S(2)}) async-start(), calls=%async_computation.8 | async-start | bytes 5242880 | tf_op jit(solution)/shard_map/all_gather | solution.py:959
  33.9 31.1 %all-to-all-start = ((bf16[8,64,2048]{2,1,0:T(8,128)(2,1)}), bf16[8,64,2048]{2,1,0:T(8,128)(2,1)}, u32[]{:S(2)}, u32[]{:S(2)}) async-start(bf16[8,64,2048]{2,1,0:T(8,128)(2,1)} %reshape.98), calls=%async_computation | async-start | bytes 4194304 | tf_op jit(solution)/shard_map/all_to_all | solution.py:952
  39.9 217.1 %all-gather.7.cloned.1.call-start = ((), (), s32[]{:S(2)}) async-start(), calls=%async_computation.9 | async-start | bytes 10485760 | tf_op jit(solution)/shard_map/all_gather | solution.py:959
  43.3 2.4 copy-start.1
  45.6 4.3 slice-start
  49.9 15.8 %copy-start.6 = (f32[64,12]{0,1:T(8,128)S(1)}, f32[64,12]{0,1:T(8,128)}, u32[]{:S(2)}) copy-start(f32[64,12]{0,1:T(8,128)} %param.12) | copy-start | bytes 9220
  49.9 15.9 %copy-start.9 = (s32[1,4]{1,0:T(1,128)S(1)}, s32[1,4]{1,0:T(1,128)}, u32[]{:S(2)}) copy-start(s32[1,4]{1,0:T(1,128)} %param.9) | copy-start | bytes 52
  65.1 376.1 %reduce-scatter.4.cloned.1.call-start = ((), (), s32[]{:S(2)}) async-start(), calls=%async_computation.5 | async-start | bytes 5242880 | tf_op jit(solution)/shard_map/reduce_scatter | solution.py:1037
  315.2 167.3 %reduce-scatter.6.cloned.1.call-start = ((), (), s32[]{:S(2)}) async-start(), calls=%async_computation.6 | async-start | bytes 5242880 | tf_op jit(solution)/shard_map/reduce_scatter | solution.py:1037
  315.8 266.3 %reduce-scatter.8.cloned.1.call-start = ((), (), s32[]{:S(2)}) async-start(), calls=%async_computation.7 | async-start | bytes 5242880 | tf_op jit(solution)/shard_map/reduce_scatter | solution.py:1037
  477.4 0.9 copy-start.5
  477.4 4.0 copy-start
  482.5 138.1 %copy-start.7 = (f32[64,12]{0,1:T(8,128)S(1)}, f32[64,12]{0,1:T(8,128)}, u32[]{:S(2)}) copy-start(f32[64,12]{0,1:T(8,128)} %param.14) | copy-start | bytes 9220
  482.5 138.1 %copy-start.8 = (f32[64,12]{0,1:T(8,128)S(1)}, f32[64,12]{0,1:T(8,128)}, u32[]{:S(2)}) copy-start(f32[64,12]{0,1:T(8,128)} %param.13) | copy-start | bytes 9220
  582.0 0.7 copy-start.4
  622.0 19.9 %copy-start.3 = (bf16[256,2048]{1,0:T(8,128)(2,1)S(1)}, bf16[256,2048]{1,0:T(8,128)(2,1)}, u32[]{:S(2)}) copy-start(bf16[256,2048]{1,0:T(8,128)(2,1)} %get-tuple-element.115) | copy-start | bytes 3145732
  622.0 20.8 %copy-start.2 = (f32[256,2048]{1,0:T(8,128)S(1)}, f32[256,2048]{1,0:T(8,128)}, u32[]{:S(2)}) copy-start(f32[256,2048]{1,0:T(8,128)} %get-tuple-element.116) | copy-start | bytes 6291460
Sparse Core Ops, SparseCore 0:
  28.8 78.6 all-gather.4
  109.1 147.8 all-gather.6
  315.3 76.7 reduce-scatter.3
  395.0 77.2 reduce-scatter.5
  477.6 93.4 reduce-scatter.7
